TPU v7x, 32 devices: a whole 2x2x4 slice. The times are simulated.
32 devices in a mesh: node: 8 (over z, x), feat: 4 (over y, core).
Axes of the slice: x: 2, y: 2, z: 4, core: 2. Of those that a mesh axis runs over, the one named last changes fastest.
Arguments:
- features: bfloat16 [256, 4096], P('feat', 'node'), may hold values from -6 to 6
- tile_values: bfloat16 [256, 128, 128], P('node'), may hold values from -0.1875 to 0.1875
- tile_rows: int32 [64, 4], P('node'), may hold values from 0 to 3
- tile_cols: int32 [64, 4], P('node'), may hold values from 0 to 3
- tile_counts: int32 [64], P('node'), may hold values from 0 to 4, as said below
- weight: bfloat16 [256, 256], replicated, may hold values from -0.375 to 0.375
- cotangent: bfloat16 [256, 4096], P(None, ('node', 'feat')), may hold values from -6 to 6
Outputs:
- activated: bfloat16 [256, 4096], P(None, ('node', 'feat'))
- grad_weight: float32 [256, 256], replicated
- grad_features: float32 [256, 4096], P('feat', 'node')
Inputs may be any that keep to these rules, and one draw needn't show every extreme that they name: `tile_counts`: slots at or past a pair's count are ignored; some pair has all 4 slots live, and the live slots of one receiving node index vary strongly between indices.
All inputs are finite; a program needn't handle non-finite values.
Results may differ from a plain program's by a relative error of at most 0.012.
Values may be sent and summed in bfloat16 or wider, within the bound.
No kernel may reach another device: no remote copies, remote signals or barrier semaphores. Data moves between devices by JAX's collectives and lax.ppermute only.
A program may use at most 64 MiB of HBM per device.

v0:
```python
import jax
import jax.numpy as jnp
from jax import lax
from jax.sharding import PartitionSpec as P


def passed_along(x, axis, by):
    count = lax.axis_size(axis)
    return lax.ppermute(x, axis, [(i, (i + by) % count) for i in range(count)])


def select_pair(tile_values, tile_rows, tile_cols, tile_counts, source):
    slots = tile_rows.shape[1]
    values = lax.dynamic_slice_in_dim(tile_values, source * slots, slots, 0)
    row_ids = lax.dynamic_index_in_dim(tile_rows, source, 0, keepdims=False)
    col_ids = lax.dynamic_index_in_dim(tile_cols, source, 0, keepdims=False)
    number = lax.dynamic_index_in_dim(tile_counts, source, 0, keepdims=False)
    live = (jnp.arange(slots) < number).astype(jnp.float32)
    return (values, row_ids, col_ids, live)


def add_forward(totals, piece, parts, keep):
    values, row_ids, col_ids, live = parts
    blocks_in = piece.reshape(piece.shape[0], -1, values.shape[1])
    block_count = blocks_in.shape[1]
    pick = jax.nn.one_hot(col_ids, block_count, dtype=jnp.bfloat16)
    chosen = jnp.einsum("frm,sr->fsm", blocks_in, pick, preferred_element_type=jnp.float32).astype(
        jnp.bfloat16
    )
    product = jnp.einsum("fsm,sjm->fsj", chosen, values, preferred_element_type=jnp.float32)
    place = jax.nn.one_hot(row_ids, block_count, dtype=jnp.float32) * (live * keep)[:, None]
    return totals + jnp.einsum("fsj,sr->frj", product, place)


def add_backward(totals, grad_blocks, parts, keep):
    values, row_ids, col_ids, live = parts
    block_count = grad_blocks.shape[1]
    pick = jax.nn.one_hot(row_ids, block_count, dtype=jnp.bfloat16)
    chosen = jnp.einsum(
        "frj,sr->fsj", grad_blocks, pick, preferred_element_type=jnp.float32
    ).astype(jnp.bfloat16)
    product = jnp.einsum("fsj,sjm->fsm", chosen, values, preferred_element_type=jnp.float32)
    place = jax.nn.one_hot(col_ids, block_count, dtype=jnp.float32) * (live * keep)[:, None]
    return totals + jnp.einsum("fsm,sc->fcm", product, place)


def per_device(features, tile_values, tile_rows, tile_cols, tile_counts, weight, cotangent):
    node_count = lax.axis_size("node")
    own_index = lax.axis_index("node")
    slice_width = features.shape[0]
    local_nodes = features.shape[1]
    tile_side = tile_values.shape[1]
    block_count = local_nodes // tile_side

    def pair_of(source):
        return select_pair(tile_values, tile_rows, tile_cols, tile_counts, source)

    totals = jnp.zeros((slice_width, block_count, tile_side), jnp.float32)
    totals = add_forward(totals, features, pair_of(own_index), 1.0)

    def ahead_step(step, carry):
        running, moving = carry
        moving = passed_along(moving, "node", 1)
        source = (own_index - step) % node_count
        return (add_forward(running, moving, pair_of(source), 1.0), moving)

    totals, _ = lax.fori_loop(1, node_count, ahead_step, (totals, features))
    aggregated = totals.reshape(slice_width, local_nodes).astype(jnp.bfloat16)
    full_rows = lax.all_to_all(aggregated, "feat", split_axis=1, concat_axis=0, tiled=True)
    pre = jnp.dot(weight.T, full_rows, preferred_element_type=jnp.float32)
    activated = jax.nn.silu(pre).astype(jnp.bfloat16)
    sigma = jax.nn.sigmoid(pre)
    dpre = (cotangent.astype(jnp.float32) * sigma * (1.0 + pre * (1.0 - sigma))).astype(
        jnp.bfloat16
    )
    weight_part = lax.dot_general(
        full_rows, dpre, (((1,), (1,)), ((), ())), preferred_element_type=jnp.float32
    )
    grad_weight = lax.psum(weight_part, ("node", "feat"))
    dagg = jnp.dot(weight, dpre, preferred_element_type=jnp.float32).astype(jnp.bfloat16)
    grad_slices = lax.all_to_all(dagg, "feat", split_axis=0, concat_axis=1, tiled=True)
    grad_blocks = grad_slices.reshape(slice_width, block_count, tile_side)
    zeros = jnp.zeros((slice_width, block_count, tile_side), jnp.float32)
    start = add_backward(zeros, grad_blocks, pair_of((own_index - 1) % node_count), 1.0)

    def carry_step(step, running):
        running = passed_along(running, "node", 1)
        owner = (own_index - step - 1) % node_count
        return add_backward(running, grad_blocks, pair_of(owner), 1.0)

    gradient = lax.fori_loop(1, node_count, carry_step, start)
    return (activated, grad_weight, gradient.reshape(slice_width, local_nodes))


def solution(mesh):
    placed = (
        P("feat", "node"),
        P("node", None, None),
        P("node", None),
        P("node", None),
        P("node"),
        P(),
        P(None, ("node", "feat")),
    )
    return jax.shard_map(
        per_device,
        mesh=mesh,
        in_specs=placed,
        out_specs=(P(None, ("node", "feat")), P(), P("feat", "node")),
        check_vma=False,
    )
```

profile of v0, /device:TPU:0, one launch (start us, length us, event | category | flops | bytes accessed | tf_op | source)
XLA Modules:
  0.0 227.0 jit_solution(9543807741233657913)
XLA Ops:
  7.2 0.9 copy.98
  8.1 0.7 copy-done.2
  8.8 0.6 copy-done.3
  10.7 0.6 compare_convert_fusion.3
  11.7 1.1 fusion.47
  12.9 62.7 %while.32 = (s32[]{:T(128)}, f32[64,4,128]{2,1,0:T(4,128)S(1)}, bf16[64,512]{1,0:T(8,128)(2,1)S(1)}, s32[]{:T(128)}, s32[8,4]{1,0:T(8,128)S(1)}, /*index=5*/s32[...) while((s32[]{:T(128)}, f32[64,4,128]{2,1,0:T(4,128)S(1)}, ...), condition=%wide.region_1.2_spmd, body=%wide.region_0.1_spmd.sunk | while | flops 8945741 | bytes 1245694 | solution.py:67
  12.9 3.0 %collective-permute-start = (bf16[64,512]{1,0:T(8,128)(2,1)S(1)}, bf16[64,512]{1,0:T(8,128)(2,1)S(1)}, u32[]{:S(2)}, u32[]{:S(2)}) collective-permute-start(bf16[64,512]{1,0:T(8,128)(2,1)S(1)} %get-tuple-element.610), channel_id=1, source_target_pairs={{0,4},{4,8},{8,12},{12,16},{16,20},{20,24},{24,28},{28,0},{1,5},{5... | collective-permute-start | bytes 196616 | tf_op jit(solution)/shard_map/while/body/eval_jaxpr/ppermute | solution.py:9
  16.5 0.6 compare_convert_fusion.6
  17.2 4.0 %collective-permute-done = bf16[64,512]{1,0:T(8,128)(2,1)S(1)} collective-permute-done((bf16[64,512]{1,0:T(8,128)(2,1)S(1)}, bf16[64,512]{1,0:T(8,128)(2,1)S(1)}, u32[]{:S(2)}, u32[]{:S(2)}) %collective-permute-start) | collective-permute-done | bytes 65568 | tf_op jit(solution)/shard_map/while/body/eval_jaxpr/ppermute | solution.py:9
  21.5 1.1 fusion.115
  23.7 0.6 compare_convert_fusion.6
  24.3 5.7 %collective-permute-done = bf16[64,512]{1,0:T(8,128)(2,1)S(1)} collective-permute-done((bf16[64,512]{1,0:T(8,128)(2,1)S(1)}, bf16[64,512]{1,0:T(8,128)(2,1)S(1)}, u32[]{:S(2)}, u32[]{:S(2)}) %collective-permute-start) | collective-permute-done | bytes 65568 | tf_op jit(solution)/shard_map/while/body/eval_jaxpr/ppermute | solution.py:9
  30.3 1.1 fusion.115
  32.4 0.6 compare_convert_fusion.6
  33.1 5.7 %collective-permute-done = bf16[64,512]{1,0:T(8,128)(2,1)S(1)} collective-permute-done((bf16[64,512]{1,0:T(8,128)(2,1)S(1)}, bf16[64,512]{1,0:T(8,128)(2,1)S(1)}, u32[]{:S(2)}, u32[]{:S(2)}) %collective-permute-start) | collective-permute-done | bytes 65568 | tf_op jit(solution)/shard_map/while/body/eval_jaxpr/ppermute | solution.py:9
  39.0 1.1 fusion.115
  41.2 0.6 compare_convert_fusion.6
  41.9 5.7 %collective-permute-done = bf16[64,512]{1,0:T(8,128)(2,1)S(1)} collective-permute-done((bf16[64,512]{1,0:T(8,128)(2,1)S(1)}, bf16[64,512]{1,0:T(8,128)(2,1)S(1)}, u32[]{:S(2)}, u32[]{:S(2)}) %collective-permute-start) | collective-permute-done | bytes 65568 | tf_op jit(solution)/shard_map/while/body/eval_jaxpr/ppermute | solution.py:9
  47.8 1.1 fusion.115
  50.0 0.6 compare_convert_fusion.6
  50.6 5.7 %collective-permute-done = bf16[64,512]{1,0:T(8,128)(2,1)S(1)} collective-permute-done((bf16[64,512]{1,0:T(8,128)(2,1)S(1)}, bf16[64,512]{1,0:T(8,128)(2,1)S(1)}, u32[]{:S(2)}, u32[]{:S(2)}) %collective-permute-start) | collective-permute-done | bytes 65568 | tf_op jit(solution)/shard_map/while/body/eval_jaxpr/ppermute | solution.py:9
  56.6 1.1 fusion.115
  58.7 0.6 compare_convert_fusion.6
  59.4 5.7 %collective-permute-done = bf16[64,512]{1,0:T(8,128)(2,1)S(1)} collective-permute-done((bf16[64,512]{1,0:T(8,128)(2,1)S(1)}, bf16[64,512]{1,0:T(8,128)(2,1)S(1)}, u32[]{:S(2)}, u32[]{:S(2)}) %collective-permute-start) | collective-permute-done | bytes 65568 | tf_op jit(solution)/shard_map/while/body/eval_jaxpr/ppermute | solution.py:9
  65.3 1.1 fusion.115
  67.5 0.6 compare_convert_fusion.6
  68.2 5.7 %collective-permute-done = bf16[64,512]{1,0:T(8,128)(2,1)S(1)} collective-permute-done((bf16[64,512]{1,0:T(8,128)(2,1)S(1)}, bf16[64,512]{1,0:T(8,128)(2,1)S(1)}, u32[]{:S(2)}, u32[]{:S(2)}) %collective-permute-start) | collective-permute-done | bytes 65568 | tf_op jit(solution)/shard_map/while/body/eval_jaxpr/ppermute | solution.py:9
  74.1 1.1 fusion.115
  75.6 0.6 copy.71
  76.2 3.4 %all-to-all-start = ((bf16[64,4,128]{2,0,1:T(8,128)(2,1)}), bf16[64,4,128]{2,0,1:T(8,128)(2,1)S(1)}, u32[]{:S(2)}, u32[]{:S(2)}) async-start(bf16[64,4,128]{2,0,1:T(8,128)(2,1)} %copy.71), calls=%async_computation | async-start | bytes 131072 | tf_op jit(solution)/shard_map/all_to_all | solution.py:69
  79.7 0.7 compare_convert_fusion.2
  80.5 3.3 %all-to-all-done = bf16[64,4,128]{2,0,1:T(8,128)(2,1)S(1)} async-done(((bf16[64,4,128]{2,0,1:T(8,128)(2,1)}), bf16[64,4,128]{2,0,1:T(8,128)(2,1)S(1)}, u32[]{:S(2)}, u32[]{:S(2)}) %all-to-all-start) | async-done | bytes 65568 | tf_op jit(solution)/shard_map/all_to_all | solution.py:69
  84.2 0.7 copy.21
  84.9 3.3 %all-to-all-start.1 = ((bf16[4,64,128]{2,1,0:T(8,128)(2,1)}), bf16[4,64,128]{2,1,0:T(8,128)(2,1)S(1)}, u32[]{:S(2)}, u32[]{:S(2)}) async-start(bf16[4,64,128]{2,1,0:T(8,128)(2,1)} %bitcast.30), calls=%async_computation.1 | async-start | bytes 131072 | tf_op jit(solution)/shard_map/all_to_all | solution.py:81
  88.3 0.9 fusion.77
  89.2 0.7 copy.25
  89.9 2.4 %all-to-all-done.1 = bf16[4,64,128]{2,1,0:T(8,128)(2,1)S(1)} async-done(((bf16[4,64,128]{2,1,0:T(8,128)(2,1)}), bf16[4,64,128]{2,1,0:T(8,128)(2,1)S(1)}, u32[]{:S(2)}, u32[]{:S(2)}) %all-to-all-start.1) | async-done | bytes 65568 | tf_op jit(solution)/shard_map/all_to_all | solution.py:81
  92.6 1.1 fusion.45
  93.9 58.6 %while.33 = (s32[]{:T(128)}, f32[64,4,128]{2,1,0:T(4,128)S(1)}, s32[]{:T(128)}, s32[8,4]{1,0:T(8,128)S(1)}, s32[8]{0:T(128)S(1)}, /*index=5*/bf16[32,128,128]{2,...) while((s32[]{:T(128)}, f32[64,4,128]{2,1,0:T(4,128)S(1)}, ...), condition=%wide.region_4.5_spmd, body=%wide.region_3.4_spmd.sunk | while | flops 8945742 | bytes 1245714 | solution.py:91
  94.2 1.1 fusion.125
  95.9 0.6 compare_convert_fusion.7
  96.5 5.2 %collective-permute-done.1 = f32[64,4,128]{2,1,0:T(4,128)S(1)} collective-permute-done((f32[64,4,128]{2,1,0:T(4,128)S(1)}, f32[64,4,128]{2,1,0:T(4,128)S(1)}, u32[]{:S(2)}, u32[]{:S(2)}) %collective-permute-start.1) | collective-permute-done | bytes 131104 | tf_op jit(solution)/shard_map/while/body/eval_jaxpr/ppermute | solution.py:9
  102.5 1.1 fusion.125
  104.1 0.6 compare_convert_fusion.7
  104.8 5.2 %collective-permute-done.1 = f32[64,4,128]{2,1,0:T(4,128)S(1)} collective-permute-done((f32[64,4,128]{2,1,0:T(4,128)S(1)}, f32[64,4,128]{2,1,0:T(4,128)S(1)}, u32[]{:S(2)}, u32[]{:S(2)}) %collective-permute-start.1) | collective-permute-done | bytes 131104 | tf_op jit(solution)/shard_map/while/body/eval_jaxpr/ppermute | solution.py:9
  110.7 1.1 fusion.125
  111.8 0.6 dynamic_slice.151
  112.4 0.6 compare_convert_fusion.7
  113.0 5.2 %collective-permute-done.1 = f32[64,4,128]{2,1,0:T(4,128)S(1)} collective-permute-done((f32[64,4,128]{2,1,0:T(4,128)S(1)}, f32[64,4,128]{2,1,0:T(4,128)S(1)}, u32[]{:S(2)}, u32[]{:S(2)}) %collective-permute-start.1) | collective-permute-done | bytes 131104 | tf_op jit(solution)/shard_map/while/body/eval_jaxpr/ppermute | solution.py:9
  118.9 1.1 fusion.125
  120.6 0.6 compare_convert_fusion.7
  121.2 5.1 %collective-permute-done.1 = f32[64,4,128]{2,1,0:T(4,128)S(1)} collective-permute-done((f32[64,4,128]{2,1,0:T(4,128)S(1)}, f32[64,4,128]{2,1,0:T(4,128)S(1)}, u32[]{:S(2)}, u32[]{:S(2)}) %collective-permute-start.1) | collective-permute-done | bytes 131104 | tf_op jit(solution)/shard_map/while/body/eval_jaxpr/ppermute | solution.py:9
  127.0 1.1 fusion.125
  128.7 0.6 compare_convert_fusion.7
  129.3 5.3 %collective-permute-done.1 = f32[64,4,128]{2,1,0:T(4,128)S(1)} collective-permute-done((f32[64,4,128]{2,1,0:T(4,128)S(1)}, f32[64,4,128]{2,1,0:T(4,128)S(1)}, u32[]{:S(2)}, u32[]{:S(2)}) %collective-permute-start.1) | collective-permute-done | bytes 131104 | tf_op jit(solution)/shard_map/while/body/eval_jaxpr/ppermute | solution.py:9
  135.4 1.1 fusion.125
  137.0 0.6 compare_convert_fusion.7
  137.7 6.3 %collective-permute-done.1 = f32[64,4,128]{2,1,0:T(4,128)S(1)} collective-permute-done((f32[64,4,128]{2,1,0:T(4,128)S(1)}, f32[64,4,128]{2,1,0:T(4,128)S(1)}, u32[]{:S(2)}, u32[]{:S(2)}) %collective-permute-start.1) | collective-permute-done | bytes 131104 | tf_op jit(solution)/shard_map/while/body/eval_jaxpr/ppermute | solution.py:9
  144.7 1.1 fusion.125
  146.3 0.6 compare_convert_fusion.7
  147.0 5.2 %collective-permute-done.1 = f32[64,4,128]{2,1,0:T(4,128)S(1)} collective-permute-done((f32[64,4,128]{2,1,0:T(4,128)S(1)}, f32[64,4,128]{2,1,0:T(4,128)S(1)}, u32[]{:S(2)}, u32[]{:S(2)}) %collective-permute-start.1) | collective-permute-done | bytes 131104 | tf_op jit(solution)/shard_map/while/body/eval_jaxpr/ppermute | solution.py:9
  152.5 0.7 copy.72
  153.2 65.3 %all-reduce.2.cloned.1.call-done = f32[256,256]{1,0:T(8,128)} async-done(((f32[256,256]{1,0:T(8,128)}), f32[256,256]{1,0:T(8,128)}) %all-reduce.2.cloned.1.call-update) | async-done | bytes 262160 | tf_op jit(solution)/shard_map/psum | solution.py:79
  218.5 1.7 copy.99
  (105 shorter events, 20.1 us)
Async XLA Ops:
  7.2 76.6 %copy-start = (bf16[256,256]{1,0:T(8,128)(2,1)S(1)}, bf16[256,256]{1,0:T(8,128)(2,1)}, u32[]{:S(2)}) copy-start(bf16[256,256]{1,0:T(8,128)(2,1)} %param.16) | copy-start | bytes 393220
  8.1 0.7 copy-start.2
  8.7 0.7 copy-start.3
  9.5 0.7 copy-start.4
  12.9 8.3 %collective-permute-start = (bf16[64,512]{1,0:T(8,128)(2,1)S(1)}, bf16[64,512]{1,0:T(8,128)(2,1)S(1)}, u32[]{:S(2)}, u32[]{:S(2)}) collective-permute-start(bf16[64,512]{1,0:T(8,128)(2,1)S(1)} %get-tuple-element.610), channel_id=1, source_target_pairs={{0,4},{4,8},{8,12},{12,16},{16,20},{20,24},{24,28},{28,0},{1,5},{5... | collective-permute-start | bytes 196616 | tf_op jit(solution)/shard_map/while/body/eval_jaxpr/ppermute | solution.py:9
  23.0 7.0 %collective-permute-start = (bf16[64,512]{1,0:T(8,128)(2,1)S(1)}, bf16[64,512]{1,0:T(8,128)(2,1)S(1)}, u32[]{:S(2)}, u32[]{:S(2)}) collective-permute-start(bf16[64,512]{1,0:T(8,128)(2,1)S(1)} %get-tuple-element.610), channel_id=1, source_target_pairs={{0,4},{4,8},{8,12},{12,16},{16,20},{20,24},{24,28},{28,0},{1,5},{5... | collective-permute-start | bytes 196616 | tf_op jit(solution)/shard_map/while/body/eval_jaxpr/ppermute | solution.py:9
  31.7 7.0 %collective-permute-start = (bf16[64,512]{1,0:T(8,128)(2,1)S(1)}, bf16[64,512]{1,0:T(8,128)(2,1)S(1)}, u32[]{:S(2)}, u32[]{:S(2)}) collective-permute-start(bf16[64,512]{1,0:T(8,128)(2,1)S(1)} %get-tuple-element.610), channel_id=1, source_target_pairs={{0,4},{4,8},{8,12},{12,16},{16,20},{20,24},{24,28},{28,0},{1,5},{5... | collective-permute-start | bytes 196616 | tf_op jit(solution)/shard_map/while/body/eval_jaxpr/ppermute | solution.py:9
  40.5 7.0 %collective-permute-start = (bf16[64,512]{1,0:T(8,128)(2,1)S(1)}, bf16[64,512]{1,0:T(8,128)(2,1)S(1)}, u32[]{:S(2)}, u32[]{:S(2)}) collective-permute-start(bf16[64,512]{1,0:T(8,128)(2,1)S(1)} %get-tuple-element.610), channel_id=1, source_target_pairs={{0,4},{4,8},{8,12},{12,16},{16,20},{20,24},{24,28},{28,0},{1,5},{5... | collective-permute-start | bytes 196616 | tf_op jit(solution)/shard_map/while/body/eval_jaxpr/ppermute | solution.py:9
  49.3 7.0 %collective-permute-start = (bf16[64,512]{1,0:T(8,128)(2,1)S(1)}, bf16[64,512]{1,0:T(8,128)(2,1)S(1)}, u32[]{:S(2)}, u32[]{:S(2)}) collective-permute-start(bf16[64,512]{1,0:T(8,128)(2,1)S(1)} %get-tuple-element.610), channel_id=1, source_target_pairs={{0,4},{4,8},{8,12},{12,16},{16,20},{20,24},{24,28},{28,0},{1,5},{5... | collective-permute-start | bytes 196616 | tf_op jit(solution)/shard_map/while/body/eval_jaxpr/ppermute | solution.py:9
  58.1 7.0 %collective-permute-start = (bf16[64,512]{1,0:T(8,128)(2,1)S(1)}, bf16[64,512]{1,0:T(8,128)(2,1)S(1)}, u32[]{:S(2)}, u32[]{:S(2)}) collective-permute-start(bf16[64,512]{1,0:T(8,128)(2,1)S(1)} %get-tuple-element.610), channel_id=1, source_target_pairs={{0,4},{4,8},{8,12},{12,16},{16,20},{20,24},{24,28},{28,0},{1,5},{5... | collective-permute-start | bytes 196616 | tf_op jit(solution)/shard_map/while/body/eval_jaxpr/ppermute | solution.py:9
  66.8 7.0 %collective-permute-start = (bf16[64,512]{1,0:T(8,128)(2,1)S(1)}, bf16[64,512]{1,0:T(8,128)(2,1)S(1)}, u32[]{:S(2)}, u32[]{:S(2)}) collective-permute-start(bf16[64,512]{1,0:T(8,128)(2,1)S(1)} %get-tuple-element.610), channel_id=1, source_target_pairs={{0,4},{4,8},{8,12},{12,16},{16,20},{20,24},{24,28},{28,0},{1,5},{5... | collective-permute-start | bytes 196616 | tf_op jit(solution)/shard_map/while/body/eval_jaxpr/ppermute | solution.py:9
  76.2 4.1 %copy-start.1 = (bf16[256,128]{1,0:T(8,128)(2,1)S(1)}, bf16[256,128]{1,0:T(8,128)(2,1)}, u32[]{:S(2)}) copy-start(bf16[256,128]{1,0:T(8,128)(2,1)} %param.17) | copy-start | bytes 196612
  76.2 7.5 %all-to-all-start = ((bf16[64,4,128]{2,0,1:T(8,128)(2,1)}), bf16[64,4,128]{2,0,1:T(8,128)(2,1)S(1)}, u32[]{:S(2)}, u32[]{:S(2)}) async-start(bf16[64,4,128]{2,0,1:T(8,128)(2,1)} %copy.71), calls=%async_computation | async-start | bytes 131072 | tf_op jit(solution)/shard_map/all_to_all | solution.py:69
  84.9 7.4 %all-to-all-start.1 = ((bf16[4,64,128]{2,1,0:T(8,128)(2,1)}), bf16[4,64,128]{2,1,0:T(8,128)(2,1)S(1)}, u32[]{:S(2)}, u32[]{:S(2)}) async-start(bf16[4,64,128]{2,1,0:T(8,128)(2,1)} %bitcast.30), calls=%async_computation.1 | async-start | bytes 131072 | tf_op jit(solution)/shard_map/all_to_all | solution.py:81
  88.2 130.3 %all-reduce.2.cloned.1.call-start = ((), (), s32[]{:S(2)}) async-start(), calls=%async_computation.2 | async-start | bytes 524288 | tf_op jit(solution)/shard_map/psum | solution.py:79
  93.9 7.9 %collective-permute-start.1 = (f32[64,4,128]{2,1,0:T(4,128)S(1)}, f32[64,4,128]{2,1,0:T(4,128)S(1)}, u32[]{:S(2)}, u32[]{:S(2)}) collective-permute-start(f32[64,4,128]{2,1,0:T(4,128)S(1)} %get-tuple-element.652), channel_id=1, source_target_pairs={{0,4},{4,8},{8,12},{12,16},{16,20},{20,24},{24,28},{28,0},{1,5},{5... | collective-permute-start | bytes 393224 | tf_op jit(solution)/shard_map/while/body/eval_jaxpr/ppermute | solution.py:9
  102.1 7.9 %collective-permute-start.1 = (f32[64,4,128]{2,1,0:T(4,128)S(1)}, f32[64,4,128]{2,1,0:T(4,128)S(1)}, u32[]{:S(2)}, u32[]{:S(2)}) collective-permute-start(f32[64,4,128]{2,1,0:T(4,128)S(1)} %get-tuple-element.652), channel_id=1, source_target_pairs={{0,4},{4,8},{8,12},{12,16},{16,20},{20,24},{24,28},{28,0},{1,5},{5... | collective-permute-start | bytes 393224 | tf_op jit(solution)/shard_map/while/body/eval_jaxpr/ppermute | solution.py:9
  110.4 7.9 %collective-permute-start.1 = (f32[64,4,128]{2,1,0:T(4,128)S(1)}, f32[64,4,128]{2,1,0:T(4,128)S(1)}, u32[]{:S(2)}, u32[]{:S(2)}) collective-permute-start(f32[64,4,128]{2,1,0:T(4,128)S(1)} %get-tuple-element.652), channel_id=1, source_target_pairs={{0,4},{4,8},{8,12},{12,16},{16,20},{20,24},{24,28},{28,0},{1,5},{5... | collective-permute-start | bytes 393224 | tf_op jit(solution)/shard_map/while/body/eval_jaxpr/ppermute | solution.py:9
  118.6 7.7 %collective-permute-start.1 = (f32[64,4,128]{2,1,0:T(4,128)S(1)}, f32[64,4,128]{2,1,0:T(4,128)S(1)}, u32[]{:S(2)}, u32[]{:S(2)}) collective-permute-start(f32[64,4,128]{2,1,0:T(4,128)S(1)} %get-tuple-element.652), channel_id=1, source_target_pairs={{0,4},{4,8},{8,12},{12,16},{16,20},{20,24},{24,28},{28,0},{1,5},{5... | collective-permute-start | bytes 393224 | tf_op jit(solution)/shard_map/while/body/eval_jaxpr/ppermute | solution.py:9
  126.7 8.0 %collective-permute-start.1 = (f32[64,4,128]{2,1,0:T(4,128)S(1)}, f32[64,4,128]{2,1,0:T(4,128)S(1)}, u32[]{:S(2)}, u32[]{:S(2)}) collective-permute-start(f32[64,4,128]{2,1,0:T(4,128)S(1)} %get-tuple-element.652), channel_id=1, source_target_pairs={{0,4},{4,8},{8,12},{12,16},{16,20},{20,24},{24,28},{28,0},{1,5},{5... | collective-permute-start | bytes 393224 | tf_op jit(solution)/shard_map/while/body/eval_jaxpr/ppermute | solution.py:9
  135.0 8.9 %collective-permute-start.1 = (f32[64,4,128]{2,1,0:T(4,128)S(1)}, f32[64,4,128]{2,1,0:T(4,128)S(1)}, u32[]{:S(2)}, u32[]{:S(2)}) collective-permute-start(f32[64,4,128]{2,1,0:T(4,128)S(1)} %get-tuple-element.652), channel_id=1, source_target_pairs={{0,4},{4,8},{8,12},{12,16},{16,20},{20,24},{24,28},{28,0},{1,5},{5... | collective-permute-start | bytes 393224 | tf_op jit(solution)/shard_map/while/body/eval_jaxpr/ppermute | solution.py:9
  144.3 7.8 %collective-permute-start.1 = (f32[64,4,128]{2,1,0:T(4,128)S(1)}, f32[64,4,128]{2,1,0:T(4,128)S(1)}, u32[]{:S(2)}, u32[]{:S(2)}) collective-permute-start(f32[64,4,128]{2,1,0:T(4,128)S(1)} %get-tuple-element.652), channel_id=1, source_target_pairs={{0,4},{4,8},{8,12},{12,16},{16,20},{20,24},{24,28},{28,0},{1,5},{5... | collective-permute-start | bytes 393224 | tf_op jit(solution)/shard_map/while/body/eval_jaxpr/ppermute | solution.py:9
Sparse Core Ops, SparseCore 0:
  95.1 123.3 all-reduce.1
where the time goes:
time: 228 us; the launch traced here: 227 us
  waiting for transfers between devices  147 us (64%)
  matrix products  27.7 us (12%)
  local copies, waits for them, and re-layouts  16.8 us (7%)
  between operations  14.2 us (6%)
  starting transfers between devices  10.5 us (5%)
  other arithmetic  10.4 us (5%)
    ppermute x14, waiting for transfers between devices, passed_along(): return lax.ppermute(x, axis, [(i, (i + by) % count) for i in range(count)])  75.5 us
    psum x1, waiting for transfers between devices, per_device(): grad_weight = lax.psum(weight_part, ('node', 'feat'))  65.3 us
    convert_element_type x16, other arithmetic, select_pair(): live = (jnp.arange(slots) < number).astype(jnp.float32)  10.4 us
    dynamic_slice x15, local copies, waits for them, and re-layouts, select_pair(): number = lax.dynamic_index_in_dim(tile_counts, source, 0, keepdims=False)  8.87 us
    dot_general x8, matrix products, add_forward(): jnp.einsum('fsm,sjm->fsj', chosen, values, preferred_element_type=jnp.flo...  8.64 us
    dot_general x8, matrix products, add_backward(): jnp.einsum('fsj,sjm->fsm', chosen, values, preferred_element_type=jnp.flo...  8.47 us
    unnamed x15, local copies, waits for them, and re-layouts  5.78 us
  transfers between devices with their start and end apart: 17, of which 17 were waited for; matrix products, arithmetic and copies ran while one was open for 15% of the time, Pallas kernels for 0%

commit v1 on v0

v1 whole, which is shorter than its diff:
```python
import functools

import jax
import jax.numpy as jnp
from jax import lax
from jax.experimental import pallas as pl
from jax.experimental.pallas import tpu as pltpu
from jax.sharding import PartitionSpec as P

BF16 = jnp.bfloat16
F32 = jnp.float32
SMEM = pl.BlockSpec(memory_space=pltpu.SMEM)
VMEM = pl.BlockSpec(memory_space=pltpu.VMEM)


def swapped(x, axis, mask):
    return lax.ppermute(x, axis, [(i, i ^ mask) for i in range(lax.axis_size(axis))])


def dot(a, b, dims):
    return lax.dot_general(a, b, (dims, ((), ())), preferred_element_type=F32)


def each(count, body):
    if count <= 8:
        for k in range(count):
            body(k)
    else:

        def step(k, carry):
            body(k)
            return carry

        lax.fori_loop(0, count, step, 0)


def lanes(block, side):
    start = block * side
    return pl.ds(start if isinstance(start, int) else pl.multiple_of(start, side), side)


def tree_sum(terms):
    while len(terms) > 1:
        terms = [a + b for a, b in zip(terms[::2], terms[1::2])]
    return terms[0]


def call(body, inputs, outputs, scratch=()):
    scalars = sum(1 for x in inputs if x.dtype == jnp.int32)
    held = sum(x.size * x.dtype.itemsize for x in [*inputs, *outputs])
    return pl.pallas_call(
        body,
        in_specs=[SMEM] * scalars + [VMEM] * (len(inputs) - scalars),
        out_specs=[VMEM] * len(outputs),
        out_shape=list(outputs),
        scratch_shapes=list(scratch),
        compiler_params=pltpu.CompilerParams(vmem_limit_bytes=2 * held + (8 << 20)),
    )(*inputs)


def add_forward(rows, cols, counts, values, pieces, totals, flip):
    own = lax.axis_index("node") ^ flip
    slots = rows.shape[1]
    side = values.shape[1]
    dummy = totals.shape[0] - 1

    def one(k):
        source = own ^ (2 * k)
        for slot in range(slots):
            block = pieces[k, :, lanes(cols[source, slot], side)]
            product = dot(block, values[source * slots + slot], ((1,), (1,)))
            to = jnp.where(slot < counts[source], rows[source, slot], dummy)
            totals[to] += product

    each(pieces.shape[0], one)


def add_backward(rows, cols, counts, values, grads, partial, store, flip, count):
    own = lax.axis_index("node") ^ flip
    slots = rows.shape[1]
    side = values.shape[1]
    dummy = partial.shape[0] - 1

    def one(k):
        owner = own ^ (2 * k)
        partial[...] = jnp.zeros_like(partial)
        for slot in range(slots):
            block = grads[:, lanes(rows[owner, slot], side)]
            product = dot(block, values[owner * slots + slot], ((1,), (0,)))
            to = jnp.where(slot < counts[owner], cols[owner, slot], dummy)
            partial[to] += product
        store(k, partial)

    each(count, one)


def forward_near(rows, cols, counts, values, pieces, totals):
    totals[...] = jnp.zeros_like(totals)
    add_forward(rows, cols, counts, values, pieces, totals, 0)


def forward_far(rows, cols, counts, values, pieces, near, out, totals):
    totals[...] = near[...]
    add_forward(rows, cols, counts, values, pieces, totals, 1)
    side = values.shape[1]
    for r in range(out.shape[1] // side):
        out[:, r * side : (r + 1) * side] = totals[r].astype(BF16)


def middle(rows, cols, counts, values, weight, *refs, feat):
    aggs, cots = refs[:feat], refs[feat : 2 * feat]
    activated, grads, sent, kept_weight, agg_full, dpre_full, partial = refs[2 * feat :]
    index = lax.axis_index("feat")
    width, local = aggs[0].shape
    side = cots[0].shape[1]
    for m in range(feat):
        agg_full[lanes(index ^ m, width), :] = aggs[m][...]
    for m in range(feat):
        at = lanes(index ^ m, side)
        pre = dot(weight[...], agg_full[:, at], ((0,), (0,)))
        sigma = 1.0 / (1.0 + jnp.exp(-pre))
        if m == 0:
            activated[...] = (pre * sigma).astype(BF16)
        dpre = cots[m][...].astype(F32) * sigma * (1.0 + pre * (1.0 - sigma))
        dpre_full[:, at] = dpre.astype(BF16)
    dpre_all = dpre_full[...]
    grads[...] = dot(weight[lanes(index, width), :], dpre_all, ((1,), (0,))).astype(BF16)
    weight_part = dot(aggs[0][...], dpre_all, ((1,), (1,))).astype(BF16)
    count = (sent.shape[0] - kept_weight.shape[0]) // width
    fold = kept_weight.shape[0]
    wide = weight_part.shape[1]
    for part in range(width // fold):
        piece = weight_part[part * fold : (part + 1) * fold]
        kept_weight[:, part * wide : (part + 1) * wide] = piece
        sent[count * width :, part * wide : (part + 1) * wide] = piece

    def store(k, partial):
        for c in range(local // side):
            sent[lanes(k, width), c * side : (c + 1) * side] = partial[c].astype(BF16)

    add_backward(rows, cols, counts, values, grads, partial, store, 1, count)


def backward_near(rows, cols, counts, values, grads, out, partial):
    width, local = grads.shape
    side = values.shape[1]

    def store(k, partial):
        for c in range(local // side):
            out[lanes(k, width), c * side : (c + 1) * side] = partial[c]

    add_backward(rows, cols, counts, values, grads, partial, store, 0, out.shape[0] // width)


def add_pair(near, got, kept_weight, own, own_weight, *sent):
    width = own.shape[0]
    total_weight = kept_weight[...].astype(F32) + got[near.shape[0] :, :].astype(F32)
    own_weight[...] = total_weight.astype(BF16)
    own[...] = near[:width] + got[:width].astype(F32)
    for k, out in enumerate(sent, 1):
        rows = slice(k * width, (k + 1) * width)
        out[:width] = (near[rows] + got[rows].astype(F32)).astype(BF16)
        out[width:] = total_weight.astype(BF16)


def add_column(own, own_weight, *refs):
    got, (gradient, weight_slice) = refs[:-2], refs[-2:]
    width = own.shape[0]
    gradient[...] = tree_sum([own[...]] + [g[:width].astype(F32) for g in got])
    weights = tree_sum([own_weight[...].astype(F32)] + [g[width:].astype(F32) for g in got])
    fold = weights.shape[0]
    wide = weight_slice.shape[1]
    for part in range(width // fold):
        piece = weights[:, part * wide : (part + 1) * wide]
        weight_slice[part * fold : (part + 1) * fold, :] = piece.astype(BF16)


def lay_out(*refs):
    slices, out = refs[:-1], refs[-1]
    index = lax.axis_index("feat")
    width = slices[0].shape[0]
    for m, piece in enumerate(slices):
        out[lanes(index ^ m, width), :] = piece[...].astype(F32)


def per_device(features, tile_values, tile_rows, tile_cols, tile_counts, weight, cotangent):
    nodes = lax.axis_size("node")
    feat = lax.axis_size("feat")
    column = nodes // 2
    width, local = features.shape
    wide = weight.shape[0]
    side = tile_values.shape[1]
    blocks = local // side
    fold = width * wide // local
    meta = (tile_rows, tile_cols, tile_counts, tile_values)
    shape = jax.ShapeDtypeStruct
    totals = (blocks + 1, width, side)

    pieces = [features] + [swapped(features, "node", 2 * k) for k in range(1, column)]
    pieces = jnp.stack(pieces)
    far_pieces = swapped(pieces, "node", 1)
    cots = [cotangent] + [swapped(cotangent, "feat", m) for m in range(1, feat)]
    (near,) = call(forward_near, [*meta, pieces], [shape(totals, F32)])
    (aggregated,) = call(
        forward_far,
        [*meta, far_pieces, near],
        [shape((width, local), BF16)],
        [pltpu.VMEM(totals, F32)],
    )
    aggs = [aggregated] + [swapped(aggregated, "feat", m) for m in range(1, feat)]
    activated, grads, sent, kept_weight = call(
        functools.partial(middle, feat=feat),
        [*meta, weight, *aggs, *cots],
        [
            shape((wide, side), BF16),
            shape((width, local), BF16),
            shape((column * width + fold, local), BF16),
            shape((fold, local), BF16),
        ],
        [
            pltpu.VMEM((wide, local), BF16),
            pltpu.VMEM((wide, local), BF16),
            pltpu.VMEM(totals, F32),
        ],
    )
    got = swapped(sent, "node", 1)
    (near_grads,) = call(
        backward_near,
        [*meta, grads],
        [shape((column * width, local), F32)],
        [pltpu.VMEM(totals, F32)],
    )
    own, own_weight, *chunks = call(
        add_pair,
        [near_grads, got, kept_weight],
        [shape((width, local), F32), shape((fold, local), BF16)]
        + [shape((width + fold, local), BF16)] * (column - 1),
    )
    arrived = [swapped(c, "node", 2 * k) for k, c in enumerate(chunks, 1)]
    gradient, weight_slice = call(
        add_column,
        [own, own_weight, *arrived],
        [shape((width, local), F32), shape((width, wide), BF16)],
    )
    slices = [weight_slice] + [swapped(weight_slice, "feat", m) for m in range(1, feat)]
    (grad_weight,) = call(lay_out, slices, [shape((wide, wide), F32)])
    return (activated, grad_weight, gradient)


def solution(mesh):
    placed = (
        P("feat", "node"),
        P("node", None, None),
        P("node", None),
        P("node", None),
        P("node"),
        P(),
        P(None, ("node", "feat")),
    )
    return jax.shard_map(
        per_device,
        mesh=mesh,
        in_specs=placed,
        out_specs=(P(None, ("node", "feat")), P(), P("feat", "node")),
        check_vma=False,
    )
```

time: 228 us -> 56.3 us (0.25)
  waiting for transfers between devices: 147 us -> 26.5 us
  matrix products: 27.7 us -> 0 us
  local copies, waits for them, and re-layouts: 16.8 us -> 1.98 us
  between operations: 14.2 us -> 0.71 us
  other arithmetic: 10.4 us -> 0.91 us
  starting transfers between devices: 10.5 us -> 19.1 us
  Pallas kernels: 0 us -> 6.88 us
    psum x1 -> x0, waiting for transfers between devices: 65.3 us -> none  [per_device(): grad_weight = lax.psum(weight_part, ('node', 'feat'))]
    ppermute x14 -> x17, waiting for transfers between devices: 75.5 us -> 26.5 us  [swapped(): lax.ppermute(x, axis, [(i, i ^ mask) for i in range(lax.axis_size(axis))])]
    dot_general x51 -> x0, matrix products: 27.7 us -> none  [the longest x8 8.64 us: add_forward(): jnp.einsum('fsm,sjm->fsj', chosen, values, preferred_element_type=jnp.flo...]
    ppermute x14 -> x17, starting transfers between devices: 3.75 us -> 19.1 us  [swapped(): lax.ppermute(x, axis, [(i, i ^ mask) for i in range(lax.axis_size(axis))])]
    convert_element_type x16 -> x0, other arithmetic: 10.4 us -> none  [select_pair(): live = (jnp.arange(slots) < number).astype(jnp.float32)]
    dynamic_slice x16 -> x0, local copies, waits for them, and re-layouts: 9.09 us -> none  [the longest x15 8.87 us: select_pair(): number = lax.dynamic_index_in_dim(tile_counts, source, 0, keepdims=False)]
    pallas_call x0 -> x7, Pallas kernels: none -> 6.88 us  [call(): pl.pallas_call(body, in_specs=[SMEM] * scalars + [VMEM] * (len(inputs) -...]
    all_to_all x2 -> x0, starting transfers between devices: 6.7 us -> none  [the longest x1 3.42 us: per_device(): lax.all_to_all(aggregated, 'feat', split_axis=1, concat_axis=0, tiled=True)]
  transfers between devices with their start and end apart: 17 -> 17, of which waited for: 17 -> 10; matrix products, arithmetic and copies ran while one was open for 15% -> 0% of each run, Pallas kernels for 0% -> 6%
where the time goes in v1:
time: 56.3 us; the launch traced here: 56.1 us
  waiting for transfers between devices  26.5 us (47%)
  starting transfers between devices  19.1 us (34%)
  Pallas kernels  6.88 us (12%)
  local copies, waits for them, and re-layouts  1.98 us (4%)
  other arithmetic  0.91 us (2%)
  between operations  0.71 us (1%)
    ppermute x17, waiting for transfers between devices, swapped(): lax.ppermute(x, axis, [(i, i ^ mask) for i in range(lax.axis_size(axis))])  26.5 us
    ppermute x17, starting transfers between devices, swapped(): lax.ppermute(x, axis, [(i, i ^ mask) for i in range(lax.axis_size(axis))])  19.1 us
    pallas_call x7, Pallas kernels, call(): pl.pallas_call(body, in_specs=[SMEM] * scalars + [VMEM] * (len(inputs) -...  6.88 us
    unnamed x16, local copies, waits for them, and re-layouts  1.98 us
  transfers between devices with their start and end apart: 17, of which 10 were waited for; matrix products, arithmetic and copies ran while one was open for 0% of the time, Pallas kernels for 6%

profile of v1, /device:TPU:0, one launch (start us, length us, event | category | flops | bytes accessed | tf_op | source)
XLA Modules:
  0.0 56.1 jit_solution(18187463739593958000)
XLA Ops:
  0.6 3.1 %collective-permute-start = (bf16[64,512]{1,0:T(8,128)(2,1)}, bf16[64,512]{1,0:T(8,128)(2,1)S(1)}, u32[]{:S(2)}, u32[]{:S(2)}) collective-permute-start(bf16[64,512]{1,0:T(8,128)(2,1)} %param.7), channel_id=1, source_target_pairs={{0,8},{4,12},{8,0},{12,4},{16,24},{20,28},{24,16},{28,20},{1,9},{5... | collective-permute-start | bytes 196616 | tf_op jit(solution)/shard_map/ppermute | solution.py:17
  3.7 2.5 %collective-permute-start.2 = (bf16[64,512]{1,0:T(8,128)(2,1)}, bf16[64,512]{1,0:T(8,128)(2,1)S(1)}, u32[]{:S(2)}, u32[]{:S(2)}) collective-permute-start(bf16[64,512]{1,0:T(8,128)(2,1)} %param.7), channel_id=1, source_target_pairs={{0,24},{4,28},{8,16},{12,20},{16,8},{20,12},{24,0},{28,4},{1,25},{... | collective-permute-start | bytes 196616 | tf_op jit(solution)/shard_map/ppermute | solution.py:17
  6.2 0.1 collective-permute-start.1
  6.3 0.0 collective-permute-done
  6.3 4.5 %collective-permute-done.2 = bf16[64,512]{1,0:T(8,128)(2,1)S(1)} collective-permute-done((bf16[64,512]{1,0:T(8,128)(2,1)}, bf16[64,512]{1,0:T(8,128)(2,1)S(1)}, u32[]{:S(2)}, u32[]{:S(2)}) %collective-permute-start.2) | collective-permute-done | bytes 65568 | tf_op jit(solution)/shard_map/ppermute | solution.py:17
  10.8 2.1 %collective-permute-done.1 = bf16[64,512]{1,0:T(8,128)(2,1)S(1)} collective-permute-done((bf16[64,512]{1,0:T(8,128)(2,1)}, bf16[64,512]{1,0:T(8,128)(2,1)S(1)}, u32[]{:S(2)}, u32[]{:S(2)}) %collective-permute-start.1) | collective-permute-done | bytes 65568 | tf_op jit(solution)/shard_map/ppermute | solution.py:17
  12.9 0.0 copy-start.3
  12.9 0.0 copy-start.5
  12.9 0.9 %pad_maximum_fusion.pieces = bf16[4,64,512]{2,1,0:T(8,128)(2,1)S(1)} fusion(bf16[1,64,512]{2,1,0:T(8,128)(2,1)S(1)} %bitcast.6, bf16[1,64,512]{2,1,0:T(8,128)(2,1)S(1)} %bitcast.7, bf16[1,64,512]{2,1,0:T(8,128)(2,1)S(1)} %bitcast.5, bf16[1,64,512]{2,1,0:T(8,128)(2,1)} %bitcast.4), kind=kLoop, calls=%fused_computation | loop fusion | flops 393216 | bytes 524288 | tf_op jit(solution)/shard_map/stack | solution.py:200
  13.8 0.0 copy-start.6
  13.8 1.6 %collective-permute-start.3 = (bf16[4,64,512]{2,1,0:T(8,128)(2,1)S(1)}, bf16[4,64,512]{2,1,0:T(8,128)(2,1)S(1)}, u32[]{:S(2)}, u32[]{:S(2)}) collective-permute-start(bf16[4,64,512]{2,1,0:T(8,128)(2,1)S(1)} %pad_maximum_fusion.pieces), channel_id=1, source_target_pairs={{0,4},{4,0},{8,12},{12,8},{16,20},{20,16},{24,28},{28,24},{1,5},{5... | collective-permute-start | bytes 786440 | tf_op jit(solution)/shard_map/ppermute | solution.py:17
  15.4 0.0 copy-done.3
  15.4 1.5 %collective-permute-start.8 = (bf16[256,128]{1,0:T(8,128)(2,1)S(1)}, bf16[256,128]{1,0:T(8,128)(2,1)S(1)}, u32[]{:S(2)}, u32[]{:S(2)}) collective-permute-start(bf16[256,128]{1,0:T(8,128)(2,1)S(1)} %copy-done.3), channel_id=1, source_target_pairs={{0,2},{1,3},{2,0},{3,1},{4,6},{5,7},{6,4},{7,5},{8,10},{9,11},{10,... | collective-permute-start | bytes 196616 | tf_op jit(solution)/shard_map/ppermute | solution.py:17
  16.9 0.0 collective-permute-start.7
  16.9 0.6 %collective-permute-start.9 = (bf16[256,128]{1,0:T(8,128)(2,1)S(1)}, bf16[256,128]{1,0:T(8,128)(2,1)S(1)}, u32[]{:S(2)}, u32[]{:S(2)}) collective-permute-start(bf16[256,128]{1,0:T(8,128)(2,1)S(1)} %copy-done.3), channel_id=1, source_target_pairs={{0,3},{1,2},{2,1},{3,0},{4,7},{5,6},{6,5},{7,4},{8,11},{9,10},{10,... | collective-permute-start | bytes 196616 | tf_op jit(solution)/shard_map/ppermute | solution.py:17
  17.5 0.0 copy-done.5
  17.5 0.1 copy.14.rows
  17.6 0.0 copy-done.6
  17.6 0.0 copy-start.4
  17.6 0.1 copy.15.cols
  17.7 0.6 %copy-done.4 = s32[8]{0:T(128)S(1)} copy-done((s32[8]{0:T(128)S(1)}, s32[8]{0:T(128)}, u32[]{:S(2)}) %copy-start.4) | copy-done | bytes 56
  18.2 0.0 copy-start
  18.2 1.2 %copy-done = bf16[32,128,128]{2,1,0:T(8,128)(2,1)S(1)} copy-done((bf16[32,128,128]{2,1,0:T(8,128)(2,1)S(1)}, bf16[32,128,128]{2,1,0:T(8,128)(2,1)}, u32[]{:S(2)}) %copy-start) | copy-done | bytes 1048600
  19.5 0.0 copy-start.1
  19.5 1.1 %shard_map.94.near = f32[5,64,128]{2,1,0:T(8,128)S(1)} custom-call(s32[8,4]{1,0:T(8,128)S(1)} %copy.14.rows, s32[8,4]{1,0:T(8,128)S(1)} %copy.15.cols, s32[8]{0:T(128)S(1)} %copy-done.4, bf16[32,128,128]{2,1,0:T(8,128)(2,1)S(1)} %copy-done, bf16[4,64,512]{2,1,0:T(8,128)(2,1)S(1)} %pad_maximum_fusion.pieces), custom_call_target="tpu_custom_call" | custom-call | tf_op jit(solution)/shard_map/pallas_call | solution.py:51
  20.6 0.0 copy-start.2
  20.6 1.4 %collective-permute-done.3.pieces = bf16[4,64,512]{2,1,0:T(8,128)(2,1)S(1)} collective-permute-done((bf16[4,64,512]{2,1,0:T(8,128)(2,1)S(1)}, bf16[4,64,512]{2,1,0:T(8,128)(2,1)S(1)}, u32[]{:S(2)}, u32[]{:S(2)}) %collective-permute-start.3) | collective-permute-done | bytes 262176 | tf_op jit(solution)/shard_map/ppermute | solution.py:17
  22.0 0.0 copy-done.1
  22.0 1.2 %shard_map.95.refs_0_ = bf16[64,512]{1,0:T(8,128)(2,1)S(1)} custom-call(s32[8,4]{1,0:T(8,128)S(1)} %copy.14.rows, s32[8,4]{1,0:T(8,128)S(1)} %copy.15.cols, s32[8]{0:T(128)S(1)} %copy-done.4, bf16[32,128,128]{2,1,0:T(8,128)(2,1)S(1)} %copy-done.1, bf16[4,64,512]{2,1,0:T(8,128)(2,1)S(1)} %collective-permute-done.3.pieces, f32[5,64,128]{2,1,0:T(8,128)S(1)} %shard_map.94.near), custom_call_target="tpu_custom_call" | custom-call | tf_op jit(solution)/shard_map/pallas_call | solution.py:51
  23.2 0.3 collective-permute-start.6
  23.5 1.4 %collective-permute-start.5 = (bf16[64,512]{1,0:T(8,128)(2,1)S(1)}, bf16[64,512]{1,0:T(8,128)(2,1)S(1)}, u32[]{:S(2)}, u32[]{:S(2)}) collective-permute-start(bf16[64,512]{1,0:T(8,128)(2,1)S(1)} %shard_map.95.refs_0_), channel_id=1, source_target_pairs={{0,2},{1,3},{2,0},{3,1},{4,6},{5,7},{6,4},{7,5},{8,10},{9,11},{10,... | collective-permute-start | bytes 196616 | tf_op jit(solution)/shard_map/ppermute | solution.py:17
  24.9 0.0 collective-permute-done.8.refs_6_
  24.9 0.3 collective-permute-start.4
  25.1 0.0 collective-permute-done.7.refs_5_
  25.1 0.0 collective-permute-done.9.refs_7_
  25.1 2.4 %collective-permute-done.6.refs_3_ = bf16[64,512]{1,0:T(8,128)(2,1)S(1)} collective-permute-done((bf16[64,512]{1,0:T(8,128)(2,1)S(1)}, bf16[64,512]{1,0:T(8,128)(2,1)S(1)}, u32[]{:S(2)}, u32[]{:S(2)}) %collective-permute-start.6) | collective-permute-done | bytes 65568 | tf_op jit(solution)/shard_map/ppermute | solution.py:17
  27.6 1.5 %collective-permute-done.5.refs_2_ = bf16[64,512]{1,0:T(8,128)(2,1)S(1)} collective-permute-done((bf16[64,512]{1,0:T(8,128)(2,1)S(1)}, bf16[64,512]{1,0:T(8,128)(2,1)S(1)}, u32[]{:S(2)}, u32[]{:S(2)}) %collective-permute-start.5) | collective-permute-done | bytes 65568 | tf_op jit(solution)/shard_map/ppermute | solution.py:17
  29.1 0.0 collective-permute-done.4.refs_1_
  29.1 0.0 copy-done.2
  29.1 2.1 %shard_map.96 = (bf16[256,128]{1,0:T(8,128)(2,1)}, bf16[64,512]{1,0:T(8,128)(2,1)S(1)}, bf16[288,512]{1,0:T(8,128)(2,1)S(1)}, bf16[32,512]{1,0:T(8,128)(2,1)S(1)}) custom-call(s32[8,4]{1,0:T(8,128)S(1)} %copy.14.rows, s32[8,4]{1,0:T(8,128)S(1)} %copy.15.cols, s32[8]{0:T(128)S(1)} %copy-done.4, bf16[32,128,128]{2,1,0:T(8,128)(2,1)S(1)} %copy-done.1, ...), custom_call_target="tpu_custom_call" | custom-call | tf_op jit(solution)/shard_map/pallas_call | solution.py:51
  31.2 1.5 %collective-permute-start.10 = (bf16[288,512]{1,0:T(8,128)(2,1)S(1)}, bf16[288,512]{1,0:T(8,128)(2,1)S(1)}, u32[]{:S(2)}, u32[]{:S(2)}) collective-permute-start(bf16[288,512]{1,0:T(8,128)(2,1)S(1)} %get-tuple-element.16), channel_id=1, source_target_pairs={{0,4},{4,0},{8,12},{12,8},{16,20},{20,16},{24,28},{28,24},{1,5},{5... | collective-permute-start | bytes 884744 | tf_op jit(solution)/shard_map/ppermute | solution.py:17
  32.7 1.0 %shard_map.97.near = f32[256,512]{1,0:T(8,128)S(1)} custom-call(s32[8,4]{1,0:T(8,128)S(1)} %copy.14.rows, s32[8,4]{1,0:T(8,128)S(1)} %copy.15.cols, s32[8]{0:T(128)S(1)} %copy-done.4, bf16[32,128,128]{2,1,0:T(8,128)(2,1)S(1)} %copy-done.1, bf16[64,512]{1,0:T(8,128)(2,1)S(1)} %get-tuple-element.15.grads), custom_call_target="tpu_custom_call" | custom-call | tf_op jit(solution)/shard_map/pallas_call | solution.py:51
  33.7 6.4 %collective-permute-done.10.got = bf16[288,512]{1,0:T(8,128)(2,1)S(1)} collective-permute-done((bf16[288,512]{1,0:T(8,128)(2,1)S(1)}, bf16[288,512]{1,0:T(8,128)(2,1)S(1)}, u32[]{:S(2)}, u32[]{:S(2)}) %collective-permute-start.10) | collective-permute-done | bytes 294944 | tf_op jit(solution)/shard_map/ppermute | solution.py:17
  40.1 0.1 shard_map.98
  40.2 0.1 collective-permute-start.11
  40.3 2.1 %collective-permute-start.12 = (bf16[96,512]{1,0:T(8,128)(2,1)S(1)}, bf16[96,512]{1,0:T(8,128)(2,1)S(1)}, u32[]{:S(2)}, u32[]{:S(2)}) collective-permute-start(bf16[96,512]{1,0:T(8,128)(2,1)S(1)} %get-tuple-element.21), channel_id=1, source_target_pairs={{0,16},{4,20},{8,24},{12,28},{16,0},{20,4},{24,8},{28,12},{1,17},{... | collective-permute-start | bytes 294920 | tf_op jit(solution)/shard_map/ppermute | solution.py:17
  42.4 2.3 %collective-permute-start.13 = (bf16[96,512]{1,0:T(8,128)(2,1)S(1)}, bf16[96,512]{1,0:T(8,128)(2,1)S(1)}, u32[]{:S(2)}, u32[]{:S(2)}) collective-permute-start(bf16[96,512]{1,0:T(8,128)(2,1)S(1)} %get-tuple-element.22), channel_id=1, source_target_pairs={{0,24},{4,28},{8,16},{12,20},{16,8},{20,12},{24,0},{28,4},{1,25},{... | collective-permute-start | bytes 294920 | tf_op jit(solution)/shard_map/ppermute | solution.py:17
  44.7 0.5 collective-permute-done.11.refs_0_
  45.2 5.2 %collective-permute-done.12.refs_1_ = bf16[96,512]{1,0:T(8,128)(2,1)S(1)} collective-permute-done((bf16[96,512]{1,0:T(8,128)(2,1)S(1)}, bf16[96,512]{1,0:T(8,128)(2,1)S(1)}, u32[]{:S(2)}, u32[]{:S(2)}) %collective-permute-start.12) | collective-permute-done | bytes 98336 | tf_op jit(solution)/shard_map/ppermute | solution.py:17
  50.4 0.0 collective-permute-done.13.refs_2_
  50.4 0.7 %shard_map.99 = (f32[64,512]{1,0:T(8,128)}, bf16[64,256]{1,0:T(8,128)(2,1)S(1)}) custom-call(f32[64,512]{1,0:T(8,128)S(1)} %get-tuple-element.18.own, bf16[32,512]{1,0:T(8,128)(2,1)S(1)} %get-tuple-element.19.own_weight, bf16[96,512]{1,0:T(8,128)(2,1)S(1)} %collective-permute-done.11.refs_0_, bf16[96,512]{1,0:T(8,128)(2,1)S(1)} %collective-permute-done.12.refs_1_, ...), custom_call_target="tpu_custom_call" | custom-call | tf_op jit(solution)/shard_map/pallas_call | solution.py:51
  51.1 0.0 collective-permute-start.16
  51.1 0.9 %collective-permute-start.15 = (bf16[64,256]{1,0:T(8,128)(2,1)S(1)}, bf16[64,256]{1,0:T(8,128)(2,1)S(1)}, u32[]{:S(2)}, u32[]{:S(2)}) collective-permute-start(bf16[64,256]{1,0:T(8,128)(2,1)S(1)} %get-tuple-element.23.refs_0_), channel_id=1, source_target_pairs={{0,2},{1,3},{2,0},{3,1},{4,6},{5,7},{6,4},{7,5},{8,10},{9,11},{10,... | collective-permute-start | bytes 98312 | tf_op jit(solution)/shard_map/ppermute | solution.py:17
  52.0 0.9 %collective-permute-start.14 = (bf16[64,256]{1,0:T(8,128)(2,1)S(1)}, bf16[64,256]{1,0:T(8,128)(2,1)S(1)}, u32[]{:S(2)}, u32[]{:S(2)}) collective-permute-start(bf16[64,256]{1,0:T(8,128)(2,1)S(1)} %get-tuple-element.23.refs_0_), channel_id=1, source_target_pairs={{0,1},{1,0},{2,3},{3,2},{4,5},{5,4},{6,7},{7,6},{8,9},{9,8},{10,11... | collective-permute-start | bytes 98312 | tf_op jit(solution)/shard_map/ppermute | solution.py:17
  53.0 1.5 %collective-permute-done.16.refs_3_ = bf16[64,256]{1,0:T(8,128)(2,1)S(1)} collective-permute-done((bf16[64,256]{1,0:T(8,128)(2,1)S(1)}, bf16[64,256]{1,0:T(8,128)(2,1)S(1)}, u32[]{:S(2)}, u32[]{:S(2)}) %collective-permute-start.16) | collective-permute-done | bytes 32800 | tf_op jit(solution)/shard_map/ppermute | solution.py:17
  54.4 0.9 %collective-permute-done.15.refs_2_ = bf16[64,256]{1,0:T(8,128)(2,1)S(1)} collective-permute-done((bf16[64,256]{1,0:T(8,128)(2,1)S(1)}, bf16[64,256]{1,0:T(8,128)(2,1)S(1)}, u32[]{:S(2)}, u32[]{:S(2)}) %collective-permute-start.15) | collective-permute-done | bytes 32800 | tf_op jit(solution)/shard_map/ppermute | solution.py:17
  55.4 0.0 collective-permute-done.14.refs_1_
  55.4 0.7 %shard_map.100 = f32[256,256]{1,0:T(8,128)} custom-call(bf16[64,256]{1,0:T(8,128)(2,1)S(1)} %get-tuple-element.23.refs_0_, bf16[64,256]{1,0:T(8,128)(2,1)S(1)} %collective-permute-done.14.refs_1_, bf16[64,256]{1,0:T(8,128)(2,1)S(1)} %collective-permute-done.15.refs_2_, bf16[64,256]{1,0:T(8,128)(2,1)S(1)} %collective-permute-done.16.refs_3_), custom_call_target="tpu_custom_call" | custom-call | tf_op jit(solution)/shard_map/pallas_call | solution.py:51
Async XLA Ops:
  0.6 5.7 %collective-permute-start = (bf16[64,512]{1,0:T(8,128)(2,1)}, bf16[64,512]{1,0:T(8,128)(2,1)S(1)}, u32[]{:S(2)}, u32[]{:S(2)}) collective-permute-start(bf16[64,512]{1,0:T(8,128)(2,1)} %param.7), channel_id=1, source_target_pairs={{0,8},{4,12},{8,0},{12,4},{16,24},{20,28},{24,16},{28,20},{1,9},{5... | collective-permute-start | bytes 196616 | tf_op jit(solution)/shard_map/ppermute | solution.py:17
  3.7 7.1 %collective-permute-start.2 = (bf16[64,512]{1,0:T(8,128)(2,1)}, bf16[64,512]{1,0:T(8,128)(2,1)S(1)}, u32[]{:S(2)}, u32[]{:S(2)}) collective-permute-start(bf16[64,512]{1,0:T(8,128)(2,1)} %param.7), channel_id=1, source_target_pairs={{0,24},{4,28},{8,16},{12,20},{16,8},{20,12},{24,0},{28,4},{1,25},{... | collective-permute-start | bytes 196616 | tf_op jit(solution)/shard_map/ppermute | solution.py:17
  6.2 6.7 %collective-permute-start.1 = (bf16[64,512]{1,0:T(8,128)(2,1)}, bf16[64,512]{1,0:T(8,128)(2,1)S(1)}, u32[]{:S(2)}, u32[]{:S(2)}) collective-permute-start(bf16[64,512]{1,0:T(8,128)(2,1)} %param.7), channel_id=1, source_target_pairs={{0,16},{4,20},{8,24},{12,28},{16,0},{20,4},{24,8},{28,12},{1,17},{... | collective-permute-start | bytes 196616 | tf_op jit(solution)/shard_map/ppermute | solution.py:17
  12.9 2.5 %copy-start.3 = (bf16[256,128]{1,0:T(8,128)(2,1)S(1)}, bf16[256,128]{1,0:T(8,128)(2,1)}, u32[]{:S(2)}) copy-start(bf16[256,128]{1,0:T(8,128)(2,1)} %refs_4_.1) | copy-start | bytes 196612
  12.9 4.6 %copy-start.5 = (s32[8,4]{0,1:T(4,128)S(1)}, s32[8,4]{0,1:T(4,128)}, u32[]{:S(2)}) copy-start(s32[8,4]{0,1:T(4,128)} %param.9) | copy-start | bytes 388
  13.8 3.8 %copy-start.6 = (s32[8,4]{0,1:T(4,128)S(1)}, s32[8,4]{0,1:T(4,128)}, u32[]{:S(2)}) copy-start(s32[8,4]{0,1:T(4,128)} %param.10) | copy-start | bytes 388
  13.8 8.2 %collective-permute-start.3 = (bf16[4,64,512]{2,1,0:T(8,128)(2,1)S(1)}, bf16[4,64,512]{2,1,0:T(8,128)(2,1)S(1)}, u32[]{:S(2)}, u32[]{:S(2)}) collective-permute-start(bf16[4,64,512]{2,1,0:T(8,128)(2,1)S(1)} %pad_maximum_fusion.pieces), channel_id=1, source_target_pairs={{0,4},{4,0},{8,12},{12,8},{16,20},{20,16},{24,28},{28,24},{1,5},{5... | collective-permute-start | bytes 786440 | tf_op jit(solution)/shard_map/ppermute | solution.py:17
  15.4 9.5 %collective-permute-start.8 = (bf16[256,128]{1,0:T(8,128)(2,1)S(1)}, bf16[256,128]{1,0:T(8,128)(2,1)S(1)}, u32[]{:S(2)}, u32[]{:S(2)}) collective-permute-start(bf16[256,128]{1,0:T(8,128)(2,1)S(1)} %copy-done.3), channel_id=1, source_target_pairs={{0,2},{1,3},{2,0},{3,1},{4,6},{5,7},{6,4},{7,5},{8,10},{9,11},{10,... | collective-permute-start | bytes 196616 | tf_op jit(solution)/shard_map/ppermute | solution.py:17
  16.9 8.3 %collective-permute-start.7 = (bf16[256,128]{1,0:T(8,128)(2,1)S(1)}, bf16[256,128]{1,0:T(8,128)(2,1)S(1)}, u32[]{:S(2)}, u32[]{:S(2)}) collective-permute-start(bf16[256,128]{1,0:T(8,128)(2,1)S(1)} %copy-done.3), channel_id=1, source_target_pairs={{0,1},{1,0},{2,3},{3,2},{4,5},{5,4},{6,7},{7,6},{8,9},{9,8},{10,11... | collective-permute-start | bytes 196616 | tf_op jit(solution)/shard_map/ppermute | solution.py:17
  16.9 8.3 %collective-permute-start.9 = (bf16[256,128]{1,0:T(8,128)(2,1)S(1)}, bf16[256,128]{1,0:T(8,128)(2,1)S(1)}, u32[]{:S(2)}, u32[]{:S(2)}) collective-permute-start(bf16[256,128]{1,0:T(8,128)(2,1)S(1)} %copy-done.3), channel_id=1, source_target_pairs={{0,3},{1,2},{2,1},{3,0},{4,7},{5,6},{6,5},{7,4},{8,11},{9,10},{10,... | collective-permute-start | bytes 196616 | tf_op jit(solution)/shard_map/ppermute | solution.py:17
  17.6 0.7 %copy-start.4 = (s32[8]{0:T(128)S(1)}, s32[8]{0:T(128)}, u32[]{:S(2)}) copy-start(s32[8]{0:T(128)} %counts.7) | copy-start | bytes 100
  18.2 1.2 %copy-start = (bf16[32,128,128]{2,1,0:T(8,128)(2,1)S(1)}, bf16[32,128,128]{2,1,0:T(8,128)(2,1)}, u32[]{:S(2)}) copy-start(bf16[32,128,128]{2,1,0:T(8,128)(2,1)} %values.7) | copy-start | bytes 3145732
  19.5 2.6 %copy-start.1 = (bf16[32,128,128]{2,1,0:T(8,128)(2,1)S(1)}, bf16[32,128,128]{2,1,0:T(8,128)(2,1)}, u32[]{:S(2)}) copy-start(bf16[32,128,128]{2,1,0:T(8,128)(2,1)} %values.7) | copy-start | bytes 3145732
  20.6 8.4 %copy-start.2 = (bf16[256,256]{1,0:T(8,128)(2,1)S(1)}, bf16[256,256]{1,0:T(8,128)(2,1)}, u32[]{:S(2)}) copy-start(bf16[256,256]{1,0:T(8,128)(2,1)} %weight.1) | copy-start | bytes 393220
  23.2 4.4 %collective-permute-start.6 = (bf16[64,512]{1,0:T(8,128)(2,1)S(1)}, bf16[64,512]{1,0:T(8,128)(2,1)S(1)}, u32[]{:S(2)}, u32[]{:S(2)}) collective-permute-start(bf16[64,512]{1,0:T(8,128)(2,1)S(1)} %shard_map.95.refs_0_), channel_id=1, source_target_pairs={{0,3},{1,2},{2,1},{3,0},{4,7},{5,6},{6,5},{7,4},{8,11},{9,10},{10,... | collective-permute-start | bytes 196616 | tf_op jit(solution)/shard_map/ppermute | solution.py:17
  23.5 5.6 %collective-permute-start.5 = (bf16[64,512]{1,0:T(8,128)(2,1)S(1)}, bf16[64,512]{1,0:T(8,128)(2,1)S(1)}, u32[]{:S(2)}, u32[]{:S(2)}) collective-permute-start(bf16[64,512]{1,0:T(8,128)(2,1)S(1)} %shard_map.95.refs_0_), channel_id=1, source_target_pairs={{0,2},{1,3},{2,0},{3,1},{4,6},{5,7},{6,4},{7,5},{8,10},{9,11},{10,... | collective-permute-start | bytes 196616 | tf_op jit(solution)/shard_map/ppermute | solution.py:17
  24.9 4.2 %collective-permute-start.4 = (bf16[64,512]{1,0:T(8,128)(2,1)S(1)}, bf16[64,512]{1,0:T(8,128)(2,1)S(1)}, u32[]{:S(2)}, u32[]{:S(2)}) collective-permute-start(bf16[64,512]{1,0:T(8,128)(2,1)S(1)} %shard_map.95.refs_0_), channel_id=1, source_target_pairs={{0,1},{1,0},{2,3},{3,2},{4,5},{5,4},{6,7},{7,6},{8,9},{9,8},{10,11... | collective-permute-start | bytes 196616 | tf_op jit(solution)/shard_map/ppermute | solution.py:17
  31.2 8.9 %collective-permute-start.10 = (bf16[288,512]{1,0:T(8,128)(2,1)S(1)}, bf16[288,512]{1,0:T(8,128)(2,1)S(1)}, u32[]{:S(2)}, u32[]{:S(2)}) collective-permute-start(bf16[288,512]{1,0:T(8,128)(2,1)S(1)} %get-tuple-element.16), channel_id=1, source_target_pairs={{0,4},{4,0},{8,12},{12,8},{16,20},{20,16},{24,28},{28,24},{1,5},{5... | collective-permute-start | bytes 884744 | tf_op jit(solution)/shard_map/ppermute | solution.py:17
  40.2 5.0 %collective-permute-start.11 = (bf16[96,512]{1,0:T(8,128)(2,1)S(1)}, bf16[96,512]{1,0:T(8,128)(2,1)S(1)}, u32[]{:S(2)}, u32[]{:S(2)}) collective-permute-start(bf16[96,512]{1,0:T(8,128)(2,1)S(1)} %get-tuple-element.20), channel_id=1, source_target_pairs={{0,8},{4,12},{8,0},{12,4},{16,24},{20,28},{24,16},{28,20},{1,9},{5... | collective-permute-start | bytes 294920 | tf_op jit(solution)/shard_map/ppermute | solution.py:17
  40.3 10.1 %collective-permute-start.12 = (bf16[96,512]{1,0:T(8,128)(2,1)S(1)}, bf16[96,512]{1,0:T(8,128)(2,1)S(1)}, u32[]{:S(2)}, u32[]{:S(2)}) collective-permute-start(bf16[96,512]{1,0:T(8,128)(2,1)S(1)} %get-tuple-element.21), channel_id=1, source_target_pairs={{0,16},{4,20},{8,24},{12,28},{16,0},{20,4},{24,8},{28,12},{1,17},{... | collective-permute-start | bytes 294920 | tf_op jit(solution)/shard_map/ppermute | solution.py:17
  42.4 8.1 %collective-permute-start.13 = (bf16[96,512]{1,0:T(8,128)(2,1)S(1)}, bf16[96,512]{1,0:T(8,128)(2,1)S(1)}, u32[]{:S(2)}, u32[]{:S(2)}) collective-permute-start(bf16[96,512]{1,0:T(8,128)(2,1)S(1)} %get-tuple-element.22), channel_id=1, source_target_pairs={{0,24},{4,28},{8,16},{12,20},{16,8},{20,12},{24,0},{28,4},{1,25},{... | collective-permute-start | bytes 294920 | tf_op jit(solution)/shard_map/ppermute | solution.py:17
  51.1 3.3 %collective-permute-start.16 = (bf16[64,256]{1,0:T(8,128)(2,1)S(1)}, bf16[64,256]{1,0:T(8,128)(2,1)S(1)}, u32[]{:S(2)}, u32[]{:S(2)}) collective-permute-start(bf16[64,256]{1,0:T(8,128)(2,1)S(1)} %get-tuple-element.23.refs_0_), channel_id=1, source_target_pairs={{0,3},{1,2},{2,1},{3,0},{4,7},{5,6},{6,5},{7,4},{8,11},{9,10},{10,... | collective-permute-start | bytes 98312 | tf_op jit(solution)/shard_map/ppermute | solution.py:17
  51.1 4.3 %collective-permute-start.15 = (bf16[64,256]{1,0:T(8,128)(2,1)S(1)}, bf16[64,256]{1,0:T(8,128)(2,1)S(1)}, u32[]{:S(2)}, u32[]{:S(2)}) collective-permute-start(bf16[64,256]{1,0:T(8,128)(2,1)S(1)} %get-tuple-element.23.refs_0_), channel_id=1, source_target_pairs={{0,2},{1,3},{2,0},{3,1},{4,6},{5,7},{6,4},{7,5},{8,10},{9,11},{10,... | collective-permute-start | bytes 98312 | tf_op jit(solution)/shard_map/ppermute | solution.py:17
  52.0 3.3 %collective-permute-start.14 = (bf16[64,256]{1,0:T(8,128)(2,1)S(1)}, bf16[64,256]{1,0:T(8,128)(2,1)S(1)}, u32[]{:S(2)}, u32[]{:S(2)}) collective-permute-start(bf16[64,256]{1,0:T(8,128)(2,1)S(1)} %get-tuple-element.23.refs_0_), channel_id=1, source_target_pairs={{0,1},{1,0},{2,3},{3,2},{4,5},{5,4},{6,7},{7,6},{8,9},{9,8},{10,11... | collective-permute-start | bytes 98312 | tf_op jit(solution)/shard_map/ppermute | solution.py:17

commit v2 on v1

--- a/solution.py
+++ b/solution.py
@@ -107,9 +107,23 @@
         out[:, r * side : (r + 1) * side] = totals[r].astype(BF16)
 
 
+def gather_feat(x):
+    far = [swapped(x, "feat", m) for m in range(2, lax.axis_size("feat"), 2)]
+    held = []
+    for piece in [x, *far]:
+        held += [piece, swapped(piece, "feat", 1)]
+    return held
+
+
+def stack(*refs):
+    pieces, out = refs[:-1], refs[-1]
+    for k, piece in enumerate(pieces):
+        out[k] = piece[...]
+
+
 def middle(rows, cols, counts, values, weight, *refs, feat):
     aggs, cots = refs[:feat], refs[feat : 2 * feat]
-    activated, grads, sent, kept_weight, agg_full, dpre_full, partial = refs[2 * feat :]
+    activated, grads, sent, weight_part, agg_full, dpre_full, partial = refs[2 * feat :]
     index = lax.axis_index("feat")
     width, local = aggs[0].shape
     side = cots[0].shape[1]
@@ -125,20 +139,16 @@
         dpre_full[:, at] = dpre.astype(BF16)
     dpre_all = dpre_full[...]
     grads[...] = dot(weight[lanes(index, width), :], dpre_all, ((1,), (0,))).astype(BF16)
-    weight_part = dot(aggs[0][...], dpre_all, ((1,), (1,))).astype(BF16)
-    count = (sent.shape[0] - kept_weight.shape[0]) // width
-    fold = kept_weight.shape[0]
-    wide = weight_part.shape[1]
-    for part in range(width // fold):
-        piece = weight_part[part * fold : (part + 1) * fold]
-        kept_weight[:, part * wide : (part + 1) * wide] = piece
-        sent[count * width :, part * wide : (part + 1) * wide] = piece
+    mine = agg_full[lanes(index & 1, weight_part.shape[0]), :]
+    weight_part[...] = dot(mine, dpre_all, ((1,), (1,))).astype(BF16)
 
     def store(k, partial):
         for c in range(local // side):
             sent[lanes(k, width), c * side : (c + 1) * side] = partial[c].astype(BF16)
 
-    add_backward(rows, cols, counts, values, grads, partial, store, 1, count)
+    add_backward(
+        rows, cols, counts, values, grads, partial, store, 1, sent.shape[0] // width
+    )
 
 
 def backward_near(rows, cols, counts, values, grads, out, partial):
@@ -152,35 +162,30 @@
     add_backward(rows, cols, counts, values, grads, partial, store, 0, out.shape[0] // width)
 
 
-def add_pair(near, got, kept_weight, own, own_weight, *sent):
+def add_weights(one, other, out):
+    out[...] = (one[...].astype(F32) + other[...].astype(F32)).astype(BF16)
+
+
+def sum_weights(*refs):
+    refs[-1][...] = tree_sum([r[...].astype(F32) for r in refs[:-1]])
+
+
+def lay_out(mine, other, out):
+    core = lax.axis_index("feat") & 1
+    out[lanes(core, mine.shape[0]), :] = mine[...]
+    out[lanes(core ^ 1, mine.shape[0]), :] = other[...]
+
+
+def add_pair(near, got, own, *sent):
     width = own.shape[0]
-    total_weight = kept_weight[...].astype(F32) + got[near.shape[0] :, :].astype(F32)
-    own_weight[...] = total_weight.astype(BF16)
     own[...] = near[:width] + got[:width].astype(F32)
     for k, out in enumerate(sent, 1):
         rows = slice(k * width, (k + 1) * width)
-        out[:width] = (near[rows] + got[rows].astype(F32)).astype(BF16)
-        out[width:] = total_weight.astype(BF16)
-
-
-def add_column(own, own_weight, *refs):
-    got, (gradient, weight_slice) = refs[:-2], refs[-2:]
-    width = own.shape[0]
-    gradient[...] = tree_sum([own[...]] + [g[:width].astype(F32) for g in got])
-    weights = tree_sum([own_weight[...].astype(F32)] + [g[width:].astype(F32) for g in got])
-    fold = weights.shape[0]
-    wide = weight_slice.shape[1]
-    for part in range(width // fold):
-        piece = weights[:, part * wide : (part + 1) * wide]
-        weight_slice[part * fold : (part + 1) * fold, :] = piece.astype(BF16)
-
-
-def lay_out(*refs):
-    slices, out = refs[:-1], refs[-1]
-    index = lax.axis_index("feat")
-    width = slices[0].shape[0]
-    for m, piece in enumerate(slices):
-        out[lanes(index ^ m, width), :] = piece[...].astype(F32)
+        out[...] = (near[rows] + got[rows].astype(F32)).astype(BF16)
+
+
+def add_column(*refs):
+    refs[-1][...] = tree_sum([r[...].astype(F32) for r in refs[:-1]])
 
 
 def per_device(features, tile_values, tile_rows, tile_cols, tile_counts, weight, cotangent):
@@ -190,16 +195,14 @@
     width, local = features.shape
     wide = weight.shape[0]
     side = tile_values.shape[1]
-    blocks = local // side
-    fold = width * wide // local
     meta = (tile_rows, tile_cols, tile_counts, tile_values)
     shape = jax.ShapeDtypeStruct
-    totals = (blocks + 1, width, side)
+    totals = (local // side + 1, width, side)
 
     pieces = [features] + [swapped(features, "node", 2 * k) for k in range(1, column)]
-    pieces = jnp.stack(pieces)
+    (pieces,) = call(stack, pieces, [shape((column, width, local), BF16)])
     far_pieces = swapped(pieces, "node", 1)
-    cots = [cotangent] + [swapped(cotangent, "feat", m) for m in range(1, feat)]
+    cots = gather_feat(cotangent)
     (near,) = call(forward_near, [*meta, pieces], [shape(totals, F32)])
     (aggregated,) = call(
         forward_far,
@@ -207,15 +210,15 @@
         [shape((width, local), BF16)],
         [pltpu.VMEM(totals, F32)],
     )
-    aggs = [aggregated] + [swapped(aggregated, "feat", m) for m in range(1, feat)]
-    activated, grads, sent, kept_weight = call(
+    aggs = gather_feat(aggregated)
+    activated, grads, sent, weight_part = call(
         functools.partial(middle, feat=feat),
         [*meta, weight, *aggs, *cots],
         [
             shape((wide, side), BF16),
             shape((width, local), BF16),
-            shape((column * width + fold, local), BF16),
-            shape((fold, local), BF16),
+            shape((column * width, local), BF16),
+            shape((wide // 2, wide), BF16),
         ],
         [
             pltpu.VMEM((wide, local), BF16),
@@ -223,6 +226,7 @@
             pltpu.VMEM(totals, F32),
         ],
     )
+    other_part = swapped(weight_part, "node", 1)
     got = swapped(sent, "node", 1)
     (near_grads,) = call(
         backward_near,
@@ -230,20 +234,21 @@
         [shape((column * width, local), F32)],
         [pltpu.VMEM(totals, F32)],
     )
-    own, own_weight, *chunks = call(
+    other_part, near_grads = lax.optimization_barrier((other_part, near_grads))
+    (pair,) = call(add_weights, [weight_part, other_part], [shape((wide // 2, wide), BF16)])
+    pairs = [pair] + [swapped(pair, "node", 2 * k) for k in range(1, column)]
+    own, *chunks = call(
         add_pair,
-        [near_grads, got, kept_weight],
-        [shape((width, local), F32), shape((fold, local), BF16)]
-        + [shape((width + fold, local), BF16)] * (column - 1),
+        [near_grads, got],
+        [shape((width, local), F32)] + [shape((width, local), BF16)] * (column - 1),
     )
     arrived = [swapped(c, "node", 2 * k) for k, c in enumerate(chunks, 1)]
-    gradient, weight_slice = call(
-        add_column,
-        [own, own_weight, *arrived],
-        [shape((width, local), F32), shape((width, wide), BF16)],
-    )
-    slices = [weight_slice] + [swapped(weight_slice, "feat", m) for m in range(1, feat)]
-    (grad_weight,) = call(lay_out, slices, [shape((wide, wide), F32)])
+    *pairs, _ = lax.optimization_barrier((*pairs, chunks[0]))
+    (half,) = call(sum_weights, pairs, [shape((wide // 2, wide), F32)])
+    other_half = swapped(half, "feat", 1)
+    (grad_weight,) = call(lay_out, [half, other_half], [shape((wide, wide), F32)])
+    *arrived, grad_weight = lax.optimization_barrier((*arrived, grad_weight))
+    (gradient,) = call(add_column, [own, *arrived], [shape((width, local), F32)])
     return (activated, grad_weight, gradient)
 
 

time: 56.3 us -> 58 us (1.030)
  starting transfers between devices: 19.1 us -> 21 us
  other arithmetic: 0.91 us -> 0 us
  local copies, waits for them, and re-layouts: 1.98 us -> 2.82 us
    ppermute x17 -> x19, starting transfers between devices: 19.1 us -> 21 us  [swapped(): lax.ppermute(x, axis, [(i, i ^ mask) for i in range(lax.axis_size(axis))])]
    another operation x1 -> x0, other arithmetic: 0.91 us -> none  [per_device(): pieces = jnp.stack(pieces)]
    unnamed x16 -> x18, local copies, waits for them, and re-layouts: 1.98 us -> 2.82 us
    ppermute x17 -> x19, waiting for transfers between devices: 26.5 us -> 26.2 us  [swapped(): lax.ppermute(x, axis, [(i, i ^ mask) for i in range(lax.axis_size(axis))])]
    pallas_call x7 -> x10, Pallas kernels: 6.88 us -> 6.98 us  [call(): pl.pallas_call(body, in_specs=[SMEM] * scalars + [VMEM] * (len(inputs) -...]
  transfers between devices with their start and end apart: 17 -> 19, of which waited for: 10 -> 11; matrix products, arithmetic and copies ran while one was open for 0% -> 0% of each run, Pallas kernels for 6% -> 7%
where the time goes in v2:
time: 58 us; the launch traced here: 57.7 us
  waiting for transfers between devices  26.2 us (45%)
  starting transfers between devices  21 us (36%)
  Pallas kernels  6.98 us (12%)
  local copies, waits for them, and re-layouts  2.82 us (5%)
  between operations  0.74 us (1%)
    ppermute x19, waiting for transfers between devices, swapped(): lax.ppermute(x, axis, [(i, i ^ mask) for i in range(lax.axis_size(axis))])  26.2 us
    ppermute x19, starting transfers between devices, swapped(): lax.ppermute(x, axis, [(i, i ^ mask) for i in range(lax.axis_size(axis))])  21 us
    pallas_call x10, Pallas kernels, call(): pl.pallas_call(body, in_specs=[SMEM] * scalars + [VMEM] * (len(inputs) -...  6.98 us
    unnamed x18, local copies, waits for them, and re-layouts  2.82 us
  transfers between devices with their start and end apart: 19, of which 11 were waited for; matrix products, arithmetic and copies ran while one was open for 0% of the time, Pallas kernels for 7%

profile of v2, /device:TPU:0, one launch (start us, length us, event | category | flops | bytes accessed | tf_op | source)
XLA Modules:
  0.0 57.7 jit_solution(15233603796313889869)
XLA Ops:
  0.6 0.0 copy-start.3
  0.6 4.1 %collective-permute-start.1 = (bf16[64,512]{1,0:T(8,128)(2,1)}, bf16[64,512]{1,0:T(8,128)(2,1)S(1)}, u32[]{:S(2)}, u32[]{:S(2)}) collective-permute-start(bf16[64,512]{1,0:T(8,128)(2,1)} %refs_0_.1), channel_id=1, source_target_pairs={{0,16},{4,20},{8,24},{12,28},{16,0},{20,4},{24,8},{28,12},{1,17},{... | collective-permute-start | bytes 196616 | tf_op jit(solution)/shard_map/ppermute | solution.py:17
  4.7 1.6 %collective-permute-start = (bf16[64,512]{1,0:T(8,128)(2,1)}, bf16[64,512]{1,0:T(8,128)(2,1)S(1)}, u32[]{:S(2)}, u32[]{:S(2)}) collective-permute-start(bf16[64,512]{1,0:T(8,128)(2,1)} %refs_0_.1), channel_id=1, source_target_pairs={{0,8},{4,12},{8,0},{12,4},{16,24},{20,28},{24,16},{28,20},{1,9},{5... | collective-permute-start | bytes 196616 | tf_op jit(solution)/shard_map/ppermute | solution.py:17
  6.3 0.0 collective-permute-start.2
  6.3 1.7 %collective-permute-done.1.refs_2_ = bf16[64,512]{1,0:T(8,128)(2,1)S(1)} collective-permute-done((bf16[64,512]{1,0:T(8,128)(2,1)}, bf16[64,512]{1,0:T(8,128)(2,1)S(1)}, u32[]{:S(2)}, u32[]{:S(2)}) %collective-permute-start.1) | collective-permute-done | bytes 65568 | tf_op jit(solution)/shard_map/ppermute | solution.py:17
  8.0 1.2 %collective-permute-done.refs_1_ = bf16[64,512]{1,0:T(8,128)(2,1)S(1)} collective-permute-done((bf16[64,512]{1,0:T(8,128)(2,1)}, bf16[64,512]{1,0:T(8,128)(2,1)S(1)}, u32[]{:S(2)}, u32[]{:S(2)}) %collective-permute-start) | collective-permute-done | bytes 65568 | tf_op jit(solution)/shard_map/ppermute | solution.py:17
  9.2 3.4 %collective-permute-done.2.refs_3_ = bf16[64,512]{1,0:T(8,128)(2,1)S(1)} collective-permute-done((bf16[64,512]{1,0:T(8,128)(2,1)}, bf16[64,512]{1,0:T(8,128)(2,1)S(1)}, u32[]{:S(2)}, u32[]{:S(2)}) %collective-permute-start.2) | collective-permute-done | bytes 65568 | tf_op jit(solution)/shard_map/ppermute | solution.py:17
  12.6 0.0 copy-start.4
  12.6 0.8 %copy-done.4 = bf16[64,512]{1,0:T(8,128)(2,1)S(1)} copy-done((bf16[64,512]{1,0:T(8,128)(2,1)S(1)}, bf16[64,512]{1,0:T(8,128)(2,1)}, u32[]{:S(2)}) %copy-start.4) | copy-done | bytes 65560
  13.4 0.0 copy-start.6
  13.5 0.0 copy-start.7
  13.5 1.6 %collective-permute-start.3 = (bf16[4,64,512]{2,1,0:T(8,128)(2,1)S(1)}, bf16[4,64,512]{2,1,0:T(8,128)(2,1)S(1)}, u32[]{:S(2)}, u32[]{:S(2)}) collective-permute-start(bf16[4,64,512]{2,1,0:T(8,128)(2,1)S(1)} %shard_map.94.pieces), channel_id=1, source_target_pairs={{0,4},{4,0},{8,12},{12,8},{16,20},{20,16},{24,28},{28,24},{1,5},{5... | collective-permute-start | bytes 786440 | tf_op jit(solution)/shard_map/ppermute | solution.py:17
  15.0 0.0 copy-done.3
  15.0 1.5 %collective-permute-start.8 = (bf16[256,128]{1,0:T(8,128)(2,1)S(1)}, bf16[256,128]{1,0:T(8,128)(2,1)S(1)}, u32[]{:S(2)}, u32[]{:S(2)}) collective-permute-start(bf16[256,128]{1,0:T(8,128)(2,1)S(1)} %copy-done.3), channel_id=1, source_target_pairs={{0,2},{1,3},{2,0},{3,1},{4,6},{5,7},{6,4},{7,5},{8,10},{9,11},{10,... | collective-permute-start | bytes 196616 | tf_op jit(solution)/shard_map/ppermute | solution.py:17
  16.5 0.0 copy-done.6
  16.6 0.1 copy.14.rows
  16.6 0.0 copy-done.7
  16.6 0.0 copy-start.5
  16.6 0.1 copy.15.cols
  16.7 0.6 copy-done.5
  17.3 0.0 copy-start
  17.3 1.2 %copy-done = bf16[32,128,128]{2,1,0:T(8,128)(2,1)S(1)} copy-done((bf16[32,128,128]{2,1,0:T(8,128)(2,1)S(1)}, bf16[32,128,128]{2,1,0:T(8,128)(2,1)}, u32[]{:S(2)}) %copy-start) | copy-done | bytes 1048600
  18.5 0.0 copy-start.1
  18.5 1.1 %shard_map.95.near = f32[5,64,128]{2,1,0:T(8,128)S(1)} custom-call(s32[8,4]{1,0:T(8,128)S(1)} %copy.14.rows, s32[8,4]{1,0:T(8,128)S(1)} %copy.15.cols, s32[8]{0:T(128)S(1)} %copy-done.5, bf16[32,128,128]{2,1,0:T(8,128)(2,1)S(1)} %copy-done, bf16[4,64,512]{2,1,0:T(8,128)(2,1)S(1)} %shard_map.94.pieces), custom_call_target="tpu_custom_call" | custom-call | tf_op jit(solution)/shard_map/pallas_call | solution.py:51
  19.7 0.0 copy-start.2
  19.7 0.3 collective-permute-done.3.pieces
  20.0 0.0 copy-done.1
  20.0 1.1 %shard_map.96.refs_0_ = bf16[64,512]{1,0:T(8,128)(2,1)S(1)} custom-call(s32[8,4]{1,0:T(8,128)S(1)} %copy.14.rows, s32[8,4]{1,0:T(8,128)S(1)} %copy.15.cols, s32[8]{0:T(128)S(1)} %copy-done.5, bf16[32,128,128]{2,1,0:T(8,128)(2,1)S(1)} %copy-done.1, bf16[4,64,512]{2,1,0:T(8,128)(2,1)S(1)} %collective-permute-done.3.pieces, f32[5,64,128]{2,1,0:T(8,128)S(1)} %shard_map.95.near), custom_call_target="tpu_custom_call" | custom-call | tf_op jit(solution)/shard_map/pallas_call | solution.py:51
  21.1 1.6 %collective-permute-start.5 = (bf16[64,512]{1,0:T(8,128)(2,1)S(1)}, bf16[64,512]{1,0:T(8,128)(2,1)S(1)}, u32[]{:S(2)}, u32[]{:S(2)}) collective-permute-start(bf16[64,512]{1,0:T(8,128)(2,1)S(1)} %shard_map.96.refs_0_), channel_id=1, source_target_pairs={{0,2},{1,3},{2,0},{3,1},{4,6},{5,7},{6,4},{7,5},{8,10},{9,11},{10,... | collective-permute-start | bytes 196616 | tf_op jit(solution)/shard_map/ppermute | solution.py:17
  22.7 0.0 collective-permute-start.7
  22.7 0.0 collective-permute-done.8.refs_6_
  22.7 0.5 collective-permute-start.9
  23.2 0.0 collective-permute-start.4
  23.2 2.2 %collective-permute-done.5.refs_2_ = bf16[64,512]{1,0:T(8,128)(2,1)S(1)} collective-permute-done((bf16[64,512]{1,0:T(8,128)(2,1)S(1)}, bf16[64,512]{1,0:T(8,128)(2,1)S(1)}, u32[]{:S(2)}, u32[]{:S(2)}) %collective-permute-start.5) | collective-permute-done | bytes 65568 | tf_op jit(solution)/shard_map/ppermute | solution.py:17
  25.5 0.0 collective-permute-start.6
  25.5 0.0 collective-permute-done.7.refs_5_
  25.5 0.0 collective-permute-done.9.refs_7_
  25.5 0.0 collective-permute-done.4.refs_1_
  25.5 1.2 %collective-permute-done.6.refs_3_ = bf16[64,512]{1,0:T(8,128)(2,1)S(1)} collective-permute-done((bf16[64,512]{1,0:T(8,128)(2,1)S(1)}, bf16[64,512]{1,0:T(8,128)(2,1)S(1)}, u32[]{:S(2)}, u32[]{:S(2)}) %collective-permute-start.6) | collective-permute-done | bytes 65568 | tf_op jit(solution)/shard_map/ppermute | solution.py:17
  26.7 0.0 copy-done.2
  26.7 2.2 %shard_map.97 = (bf16[256,128]{1,0:T(8,128)(2,1)}, bf16[64,512]{1,0:T(8,128)(2,1)S(1)}, bf16[256,512]{1,0:T(8,128)(2,1)S(1)}, bf16[128,256]{1,0:T(8,128)(2,1)S(1)}) custom-call(s32[8,4]{1,0:T(8,128)S(1)} %copy.14.rows, s32[8,4]{1,0:T(8,128)S(1)} %copy.15.cols, s32[8]{0:T(128)S(1)} %copy-done.5, bf16[32,128,128]{2,1,0:T(8,128)(2,1)S(1)} %copy-done.1, ...), custom_call_target="tpu_custom_call" | custom-call | tf_op jit(solution)/shard_map/pallas_call | solution.py:51
  28.9 1.5 %collective-permute-start.11 = (bf16[256,512]{1,0:T(8,128)(2,1)S(1)}, bf16[256,512]{1,0:T(8,128)(2,1)S(1)}, u32[]{:S(2)}, u32[]{:S(2)}) collective-permute-start(bf16[256,512]{1,0:T(8,128)(2,1)S(1)} %get-tuple-element.25), channel_id=1, source_target_pairs={{0,4},{4,0},{8,12},{12,8},{16,20},{20,16},{24,28},{28,24},{1,5},{5... | collective-permute-start | bytes 786440 | tf_op jit(solution)/shard_map/ppermute | solution.py:17
  30.4 0.5 collective-permute-start.10
  30.9 1.0 %shard_map.98.near = f32[256,512]{1,0:T(8,128)S(1)} custom-call(s32[8,4]{1,0:T(8,128)S(1)} %copy.14.rows, s32[8,4]{1,0:T(8,128)S(1)} %copy.15.cols, s32[8]{0:T(128)S(1)} %copy-done.5, bf16[32,128,128]{2,1,0:T(8,128)(2,1)S(1)} %copy-done.1, bf16[64,512]{1,0:T(8,128)(2,1)S(1)} %get-tuple-element.23.grads), custom_call_target="tpu_custom_call" | custom-call | tf_op jit(solution)/shard_map/pallas_call | solution.py:51
  31.9 6.7 %collective-permute-done.10.other = bf16[128,256]{1,0:T(8,128)(2,1)S(1)} collective-permute-done((bf16[128,256]{1,0:T(8,128)(2,1)S(1)}, bf16[128,256]{1,0:T(8,128)(2,1)S(1)}, u32[]{:S(2)}, u32[]{:S(2)}) %collective-permute-start.10) | collective-permute-done | bytes 65568 | tf_op jit(solution)/shard_map/ppermute | solution.py:17
  38.7 2.0 %collective-permute-start.17 = (bf16[128,256]{1,0:T(8,128)(2,1)S(1)}, bf16[128,256]{1,0:T(8,128)(2,1)S(1)}, u32[]{:S(2)}, u32[]{:S(2)}) collective-permute-start(bf16[128,256]{1,0:T(8,128)(2,1)S(1)} %shard_map.100.refs_0_), channel_id=1, source_target_pairs={{0,24},{4,28},{8,16},{12,20},{16,8},{20,12},{24,0},{28,4},{1,25},{... | collective-permute-start | bytes 196616 | tf_op jit(solution)/shard_map/ppermute | solution.py:17
  40.7 0.9 %collective-permute-start.16 = (bf16[128,256]{1,0:T(8,128)(2,1)S(1)}, bf16[128,256]{1,0:T(8,128)(2,1)S(1)}, u32[]{:S(2)}, u32[]{:S(2)}) collective-permute-start(bf16[128,256]{1,0:T(8,128)(2,1)S(1)} %shard_map.100.refs_0_), channel_id=1, source_target_pairs={{0,16},{4,20},{8,24},{12,28},{16,0},{20,4},{24,8},{28,12},{1,17},{... | collective-permute-start | bytes 196616 | tf_op jit(solution)/shard_map/ppermute | solution.py:17
  41.6 1.6 %collective-permute-start.15 = (bf16[128,256]{1,0:T(8,128)(2,1)S(1)}, bf16[128,256]{1,0:T(8,128)(2,1)S(1)}, u32[]{:S(2)}, u32[]{:S(2)}) collective-permute-start(bf16[128,256]{1,0:T(8,128)(2,1)S(1)} %shard_map.100.refs_0_), channel_id=1, source_target_pairs={{0,8},{4,12},{8,0},{12,4},{16,24},{20,28},{24,16},{28,20},{1,9},{5... | collective-permute-start | bytes 196616 | tf_op jit(solution)/shard_map/ppermute | solution.py:17
  43.1 0.0 collective-permute-done.11.got
  43.2 2.5 %collective-permute-done.17.refs_3_ = bf16[128,256]{1,0:T(8,128)(2,1)S(1)} collective-permute-done((bf16[128,256]{1,0:T(8,128)(2,1)S(1)}, bf16[128,256]{1,0:T(8,128)(2,1)S(1)}, u32[]{:S(2)}, u32[]{:S(2)}) %collective-permute-start.17) | collective-permute-done | bytes 65568 | tf_op jit(solution)/shard_map/ppermute | solution.py:17
  45.7 1.7 %collective-permute-done.16.refs_2_ = bf16[128,256]{1,0:T(8,128)(2,1)S(1)} collective-permute-done((bf16[128,256]{1,0:T(8,128)(2,1)S(1)}, bf16[128,256]{1,0:T(8,128)(2,1)S(1)}, u32[]{:S(2)}, u32[]{:S(2)}) %collective-permute-start.16) | collective-permute-done | bytes 65568 | tf_op jit(solution)/shard_map/ppermute | solution.py:17
  47.4 0.0 collective-permute-done.15.refs_1_
  47.4 0.1 collective-permute-start.18
  47.5 0.8 %collective-permute-start.13 = (bf16[64,512]{1,0:T(8,128)(2,1)S(1)}, bf16[64,512]{1,0:T(8,128)(2,1)S(1)}, u32[]{:S(2)}, u32[]{:S(2)}) collective-permute-start(bf16[64,512]{1,0:T(8,128)(2,1)S(1)} %get-tuple-element.27), channel_id=1, source_target_pairs={{0,16},{4,20},{8,24},{12,28},{16,0},{20,4},{24,8},{28,12},{1,17},{... | collective-permute-start | bytes 196616 | tf_op jit(solution)/shard_map/ppermute | solution.py:17
  48.3 2.0 %collective-permute-start.14 = (bf16[64,512]{1,0:T(8,128)(2,1)S(1)}, bf16[64,512]{1,0:T(8,128)(2,1)S(1)}, u32[]{:S(2)}, u32[]{:S(2)}) collective-permute-start(bf16[64,512]{1,0:T(8,128)(2,1)S(1)} %get-tuple-element.28), channel_id=1, source_target_pairs={{0,24},{4,28},{8,16},{12,20},{16,8},{20,12},{24,0},{28,4},{1,25},{... | collective-permute-start | bytes 196616 | tf_op jit(solution)/shard_map/ppermute | solution.py:17
  50.4 0.7 %collective-permute-start.12 = (bf16[64,512]{1,0:T(8,128)(2,1)S(1)}, bf16[64,512]{1,0:T(8,128)(2,1)S(1)}, u32[]{:S(2)}, u32[]{:S(2)}) collective-permute-start(bf16[64,512]{1,0:T(8,128)(2,1)S(1)} %get-tuple-element.26), channel_id=1, source_target_pairs={{0,8},{4,12},{8,0},{12,4},{16,24},{20,28},{24,16},{28,20},{1,9},{5... | collective-permute-start | bytes 196616 | tf_op jit(solution)/shard_map/ppermute | solution.py:17
  51.1 0.0 collective-permute-done.18.other
  51.1 0.7 %shard_map.102 = f32[256,256]{1,0:T(8,128)} custom-call(f32[128,256]{1,0:T(8,128)S(1)} %shard_map.101.mine, f32[128,256]{1,0:T(8,128)S(1)} %collective-permute-done.18.other), custom_call_target="tpu_custom_call" | custom-call | tf_op jit(solution)/shard_map/pallas_call | solution.py:51
  51.8 4.1 %collective-permute-done.13.refs_2_ = bf16[64,512]{1,0:T(8,128)(2,1)S(1)} collective-permute-done((bf16[64,512]{1,0:T(8,128)(2,1)S(1)}, bf16[64,512]{1,0:T(8,128)(2,1)S(1)}, u32[]{:S(2)}, u32[]{:S(2)}) %collective-permute-start.13) | collective-permute-done | bytes 65568 | tf_op jit(solution)/shard_map/ppermute | solution.py:17
  55.9 0.0 collective-permute-done.14.refs_3_
  55.9 1.1 %collective-permute-done.12.refs_1_ = bf16[64,512]{1,0:T(8,128)(2,1)S(1)} collective-permute-done((bf16[64,512]{1,0:T(8,128)(2,1)S(1)}, bf16[64,512]{1,0:T(8,128)(2,1)S(1)}, u32[]{:S(2)}, u32[]{:S(2)}) %collective-permute-start.12) | collective-permute-done | bytes 65568 | tf_op jit(solution)/shard_map/ppermute | solution.py:17
  57.1 0.7 %shard_map.103 = f32[64,512]{1,0:T(8,128)} custom-call(f32[64,512]{1,0:T(8,128)S(1)} %get-tuple-element.35.refs_0_, bf16[64,512]{1,0:T(8,128)(2,1)S(1)} %collective-permute-done.12.refs_1_, bf16[64,512]{1,0:T(8,128)(2,1)S(1)} %collective-permute-done.13.refs_2_, bf16[64,512]{1,0:T(8,128)(2,1)S(1)} %collective-permute-done.14.refs_3_), custom_call_target="tpu_custom_call" | custom-call | tf_op jit(solution)/shard_map/pallas_call | solution.py:51
  (4 shorter events, 0.1 us)
Async XLA Ops:
  0.6 14.4 %copy-start.3 = (bf16[256,128]{1,0:T(8,128)(2,1)S(1)}, bf16[256,128]{1,0:T(8,128)(2,1)}, u32[]{:S(2)}) copy-start(bf16[256,128]{1,0:T(8,128)(2,1)} %refs_4_.1) | copy-start | bytes 196612
  0.6 7.4 %collective-permute-start.1 = (bf16[64,512]{1,0:T(8,128)(2,1)}, bf16[64,512]{1,0:T(8,128)(2,1)S(1)}, u32[]{:S(2)}, u32[]{:S(2)}) collective-permute-start(bf16[64,512]{1,0:T(8,128)(2,1)} %refs_0_.1), channel_id=1, source_target_pairs={{0,16},{4,20},{8,24},{12,28},{16,0},{20,4},{24,8},{28,12},{1,17},{... | collective-permute-start | bytes 196616 | tf_op jit(solution)/shard_map/ppermute | solution.py:17
  4.7 4.5 %collective-permute-start = (bf16[64,512]{1,0:T(8,128)(2,1)}, bf16[64,512]{1,0:T(8,128)(2,1)S(1)}, u32[]{:S(2)}, u32[]{:S(2)}) collective-permute-start(bf16[64,512]{1,0:T(8,128)(2,1)} %refs_0_.1), channel_id=1, source_target_pairs={{0,8},{4,12},{8,0},{12,4},{16,24},{20,28},{24,16},{28,20},{1,9},{5... | collective-permute-start | bytes 196616 | tf_op jit(solution)/shard_map/ppermute | solution.py:17
  6.3 6.3 %collective-permute-start.2 = (bf16[64,512]{1,0:T(8,128)(2,1)}, bf16[64,512]{1,0:T(8,128)(2,1)S(1)}, u32[]{:S(2)}, u32[]{:S(2)}) collective-permute-start(bf16[64,512]{1,0:T(8,128)(2,1)} %refs_0_.1), channel_id=1, source_target_pairs={{0,24},{4,28},{8,16},{12,20},{16,8},{20,12},{24,0},{28,4},{1,25},{... | collective-permute-start | bytes 196616 | tf_op jit(solution)/shard_map/ppermute | solution.py:17
  12.6 0.8 %copy-start.4 = (bf16[64,512]{1,0:T(8,128)(2,1)S(1)}, bf16[64,512]{1,0:T(8,128)(2,1)}, u32[]{:S(2)}) copy-start(bf16[64,512]{1,0:T(8,128)(2,1)} %refs_0_.1) | copy-start | bytes 196612
  13.4 3.1 %copy-start.6 = (s32[8,4]{0,1:T(4,128)S(1)}, s32[8,4]{0,1:T(4,128)}, u32[]{:S(2)}) copy-start(s32[8,4]{0,1:T(4,128)} %param.9) | copy-start | bytes 388
  13.5 3.2 %copy-start.7 = (s32[8,4]{0,1:T(4,128)S(1)}, s32[8,4]{0,1:T(4,128)}, u32[]{:S(2)}) copy-start(s32[8,4]{0,1:T(4,128)} %param.10) | copy-start | bytes 388
  13.5 6.5 %collective-permute-start.3 = (bf16[4,64,512]{2,1,0:T(8,128)(2,1)S(1)}, bf16[4,64,512]{2,1,0:T(8,128)(2,1)S(1)}, u32[]{:S(2)}, u32[]{:S(2)}) collective-permute-start(bf16[4,64,512]{2,1,0:T(8,128)(2,1)S(1)} %shard_map.94.pieces), channel_id=1, source_target_pairs={{0,4},{4,0},{8,12},{12,8},{16,20},{20,16},{24,28},{28,24},{1,5},{5... | collective-permute-start | bytes 786440 | tf_op jit(solution)/shard_map/ppermute | solution.py:17
  15.0 7.7 %collective-permute-start.8 = (bf16[256,128]{1,0:T(8,128)(2,1)S(1)}, bf16[256,128]{1,0:T(8,128)(2,1)S(1)}, u32[]{:S(2)}, u32[]{:S(2)}) collective-permute-start(bf16[256,128]{1,0:T(8,128)(2,1)S(1)} %copy-done.3), channel_id=1, source_target_pairs={{0,2},{1,3},{2,0},{3,1},{4,6},{5,7},{6,4},{7,5},{8,10},{9,11},{10,... | collective-permute-start | bytes 196616 | tf_op jit(solution)/shard_map/ppermute | solution.py:17
  16.6 0.7 %copy-start.5 = (s32[8]{0:T(128)S(1)}, s32[8]{0:T(128)}, u32[]{:S(2)}) copy-start(s32[8]{0:T(128)} %counts.7) | copy-start | bytes 100
  17.3 1.2 %copy-start = (bf16[32,128,128]{2,1,0:T(8,128)(2,1)S(1)}, bf16[32,128,128]{2,1,0:T(8,128)(2,1)}, u32[]{:S(2)}) copy-start(bf16[32,128,128]{2,1,0:T(8,128)(2,1)} %values.7) | copy-start | bytes 3145732
  18.5 1.5 %copy-start.1 = (bf16[32,128,128]{2,1,0:T(8,128)(2,1)S(1)}, bf16[32,128,128]{2,1,0:T(8,128)(2,1)}, u32[]{:S(2)}) copy-start(bf16[32,128,128]{2,1,0:T(8,128)(2,1)} %values.7) | copy-start | bytes 3145732
  19.7 7.1 %copy-start.2 = (bf16[256,256]{1,0:T(8,128)(2,1)S(1)}, bf16[256,256]{1,0:T(8,128)(2,1)}, u32[]{:S(2)}) copy-start(bf16[256,256]{1,0:T(8,128)(2,1)} %weight.1) | copy-start | bytes 393220
  21.1 4.3 %collective-permute-start.5 = (bf16[64,512]{1,0:T(8,128)(2,1)S(1)}, bf16[64,512]{1,0:T(8,128)(2,1)S(1)}, u32[]{:S(2)}, u32[]{:S(2)}) collective-permute-start(bf16[64,512]{1,0:T(8,128)(2,1)S(1)} %shard_map.96.refs_0_), channel_id=1, source_target_pairs={{0,2},{1,3},{2,0},{3,1},{4,6},{5,7},{6,4},{7,5},{8,10},{9,11},{10,... | collective-permute-start | bytes 196616 | tf_op jit(solution)/shard_map/ppermute | solution.py:17
  22.7 2.8 %collective-permute-start.7 = (bf16[256,128]{1,0:T(8,128)(2,1)S(1)}, bf16[256,128]{1,0:T(8,128)(2,1)S(1)}, u32[]{:S(2)}, u32[]{:S(2)}) collective-permute-start(bf16[256,128]{1,0:T(8,128)(2,1)S(1)} %copy-done.3), channel_id=1, source_target_pairs={{0,1},{1,0},{2,3},{3,2},{4,5},{5,4},{6,7},{7,6},{8,9},{9,8},{10,11... | collective-permute-start | bytes 196616 | tf_op jit(solution)/shard_map/ppermute | solution.py:17
  22.7 2.7 %collective-permute-start.9 = (bf16[256,128]{1,0:T(8,128)(2,1)S(1)}, bf16[256,128]{1,0:T(8,128)(2,1)S(1)}, u32[]{:S(2)}, u32[]{:S(2)}) collective-permute-start(bf16[256,128]{1,0:T(8,128)(2,1)S(1)} %collective-permute-done.8.refs_6_), channel_id=1, source_target_pairs={{0,1},{1,0},{2,3},{3,2},{4,5},{5,4},{6,7},{7,6},{8,9},{9,8},{10,11... | collective-permute-start | bytes 196616 | tf_op jit(solution)/shard_map/ppermute | solution.py:17
  23.2 2.2 %collective-permute-start.4 = (bf16[64,512]{1,0:T(8,128)(2,1)S(1)}, bf16[64,512]{1,0:T(8,128)(2,1)S(1)}, u32[]{:S(2)}, u32[]{:S(2)}) collective-permute-start(bf16[64,512]{1,0:T(8,128)(2,1)S(1)} %shard_map.96.refs_0_), channel_id=1, source_target_pairs={{0,1},{1,0},{2,3},{3,2},{4,5},{5,4},{6,7},{7,6},{8,9},{9,8},{10,11... | collective-permute-start | bytes 196616 | tf_op jit(solution)/shard_map/ppermute | solution.py:17
  25.5 1.3 %collective-permute-start.6 = (bf16[64,512]{1,0:T(8,128)(2,1)S(1)}, bf16[64,512]{1,0:T(8,128)(2,1)S(1)}, u32[]{:S(2)}, u32[]{:S(2)}) collective-permute-start(bf16[64,512]{1,0:T(8,128)(2,1)S(1)} %collective-permute-done.5.refs_2_), channel_id=1, source_target_pairs={{0,1},{1,0},{2,3},{3,2},{4,5},{5,4},{6,7},{7,6},{8,9},{9,8},{10,11... | collective-permute-start | bytes 196616 | tf_op jit(solution)/shard_map/ppermute | solution.py:17
  28.9 14.2 %collective-permute-start.11 = (bf16[256,512]{1,0:T(8,128)(2,1)S(1)}, bf16[256,512]{1,0:T(8,128)(2,1)S(1)}, u32[]{:S(2)}, u32[]{:S(2)}) collective-permute-start(bf16[256,512]{1,0:T(8,128)(2,1)S(1)} %get-tuple-element.25), channel_id=1, source_target_pairs={{0,4},{4,0},{8,12},{12,8},{16,20},{20,16},{24,28},{28,24},{1,5},{5... | collective-permute-start | bytes 786440 | tf_op jit(solution)/shard_map/ppermute | solution.py:17
  30.4 8.3 %collective-permute-start.10 = (bf16[128,256]{1,0:T(8,128)(2,1)S(1)}, bf16[128,256]{1,0:T(8,128)(2,1)S(1)}, u32[]{:S(2)}, u32[]{:S(2)}) collective-permute-start(bf16[128,256]{1,0:T(8,128)(2,1)S(1)} %get-tuple-element.22.one), channel_id=1, source_target_pairs={{0,4},{4,0},{8,12},{12,8},{16,20},{20,16},{24,28},{28,24},{1,5},{5... | collective-permute-start | bytes 196616 | tf_op jit(solution)/shard_map/ppermute | solution.py:17
  38.7 7.0 %collective-permute-start.17 = (bf16[128,256]{1,0:T(8,128)(2,1)S(1)}, bf16[128,256]{1,0:T(8,128)(2,1)S(1)}, u32[]{:S(2)}, u32[]{:S(2)}) collective-permute-start(bf16[128,256]{1,0:T(8,128)(2,1)S(1)} %shard_map.100.refs_0_), channel_id=1, source_target_pairs={{0,24},{4,28},{8,16},{12,20},{16,8},{20,12},{24,0},{28,4},{1,25},{... | collective-permute-start | bytes 196616 | tf_op jit(solution)/shard_map/ppermute | solution.py:17
  40.7 6.7 %collective-permute-start.16 = (bf16[128,256]{1,0:T(8,128)(2,1)S(1)}, bf16[128,256]{1,0:T(8,128)(2,1)S(1)}, u32[]{:S(2)}, u32[]{:S(2)}) collective-permute-start(bf16[128,256]{1,0:T(8,128)(2,1)S(1)} %shard_map.100.refs_0_), channel_id=1, source_target_pairs={{0,16},{4,20},{8,24},{12,28},{16,0},{20,4},{24,8},{28,12},{1,17},{... | collective-permute-start | bytes 196616 | tf_op jit(solution)/shard_map/ppermute | solution.py:17
  41.6 5.8 %collective-permute-start.15 = (bf16[128,256]{1,0:T(8,128)(2,1)S(1)}, bf16[128,256]{1,0:T(8,128)(2,1)S(1)}, u32[]{:S(2)}, u32[]{:S(2)}) collective-permute-start(bf16[128,256]{1,0:T(8,128)(2,1)S(1)} %shard_map.100.refs_0_), channel_id=1, source_target_pairs={{0,8},{4,12},{8,0},{12,4},{16,24},{20,28},{24,16},{28,20},{1,9},{5... | collective-permute-start | bytes 196616 | tf_op jit(solution)/shard_map/ppermute | solution.py:17
  47.4 3.6 %collective-permute-start.18 = (f32[128,256]{1,0:T(8,128)S(1)}, f32[128,256]{1,0:T(8,128)S(1)}, u32[]{:S(2)}, u32[]{:S(2)}) collective-permute-start(f32[128,256]{1,0:T(8,128)S(1)} %shard_map.101.mine), channel_id=1, source_target_pairs={{0,1},{1,0},{2,3},{3,2},{4,5},{5,4},{6,7},{7,6},{8,9},{9,8},{10,11... | collective-permute-start | bytes 393224 | tf_op jit(solution)/shard_map/ppermute | solution.py:17
  47.5 8.4 %collective-permute-start.13 = (bf16[64,512]{1,0:T(8,128)(2,1)S(1)}, bf16[64,512]{1,0:T(8,128)(2,1)S(1)}, u32[]{:S(2)}, u32[]{:S(2)}) collective-permute-start(bf16[64,512]{1,0:T(8,128)(2,1)S(1)} %get-tuple-element.27), channel_id=1, source_target_pairs={{0,16},{4,20},{8,24},{12,28},{16,0},{20,4},{24,8},{28,12},{1,17},{... | collective-permute-start | bytes 196616 | tf_op jit(solution)/shard_map/ppermute | solution.py:17
  48.3 7.6 %collective-permute-start.14 = (bf16[64,512]{1,0:T(8,128)(2,1)S(1)}, bf16[64,512]{1,0:T(8,128)(2,1)S(1)}, u32[]{:S(2)}, u32[]{:S(2)}) collective-permute-start(bf16[64,512]{1,0:T(8,128)(2,1)S(1)} %get-tuple-element.28), channel_id=1, source_target_pairs={{0,24},{4,28},{8,16},{12,20},{16,8},{20,12},{24,0},{28,4},{1,25},{... | collective-permute-start | bytes 196616 | tf_op jit(solution)/shard_map/ppermute | solution.py:17
  50.4 6.7 %collective-permute-start.12 = (bf16[64,512]{1,0:T(8,128)(2,1)S(1)}, bf16[64,512]{1,0:T(8,128)(2,1)S(1)}, u32[]{:S(2)}, u32[]{:S(2)}) collective-permute-start(bf16[64,512]{1,0:T(8,128)(2,1)S(1)} %get-tuple-element.26), channel_id=1, source_target_pairs={{0,8},{4,12},{8,0},{12,4},{16,24},{20,28},{24,16},{28,20},{1,9},{5... | collective-permute-start | bytes 196616 | tf_op jit(solution)/shard_map/ppermute | solution.py:17

commit v3 on v2

--- a/solution.py
+++ b/solution.py
@@ -58,21 +58,22 @@
     )(*inputs)
 
 
-def add_forward(rows, cols, counts, values, pieces, totals, flip):
+def add_forward(rows, cols, counts, values, first, rest, totals, flip):
     own = lax.axis_index("node") ^ flip
     slots = rows.shape[1]
     side = values.shape[1]
     dummy = totals.shape[0] - 1
 
-    def one(k):
+    def one(k, piece):
         source = own ^ (2 * k)
         for slot in range(slots):
-            block = pieces[k, :, lanes(cols[source, slot], side)]
+            block = piece[:, lanes(cols[source, slot], side)]
             product = dot(block, values[source * slots + slot], ((1,), (1,)))
             to = jnp.where(slot < counts[source], rows[source, slot], dummy)
             totals[to] += product
 
-    each(pieces.shape[0], one)
+    one(0, first)
+    each(rest.shape[0], lambda k: one(k + 1, rest.at[k]))
 
 
 def add_backward(rows, cols, counts, values, grads, partial, store, flip, count):
@@ -94,14 +95,14 @@
     each(count, one)
 
 
-def forward_near(rows, cols, counts, values, pieces, totals):
+def forward_near(rows, cols, counts, values, first, rest, totals):
     totals[...] = jnp.zeros_like(totals)
-    add_forward(rows, cols, counts, values, pieces, totals, 0)
-
-
-def forward_far(rows, cols, counts, values, pieces, near, out, totals):
+    add_forward(rows, cols, counts, values, first, rest, totals, 0)
+
+
+def forward_far(rows, cols, counts, values, first, rest, near, out, totals):
     totals[...] = near[...]
-    add_forward(rows, cols, counts, values, pieces, totals, 1)
+    add_forward(rows, cols, counts, values, first, rest, totals, 1)
     side = values.shape[1]
     for r in range(out.shape[1] // side):
         out[:, r * side : (r + 1) * side] = totals[r].astype(BF16)
@@ -121,9 +122,9 @@
         out[k] = piece[...]
 
 
-def middle(rows, cols, counts, values, weight, *refs, feat):
+def middle(weight, *refs, feat):
     aggs, cots = refs[:feat], refs[feat : 2 * feat]
-    activated, grads, sent, weight_part, agg_full, dpre_full, partial = refs[2 * feat :]
+    activated, grads, weight_part, agg_full, dpre_full = refs[2 * feat :]
     index = lax.axis_index("feat")
     width, local = aggs[0].shape
     side = cots[0].shape[1]
@@ -142,24 +143,18 @@
     mine = agg_full[lanes(index & 1, weight_part.shape[0]), :]
     weight_part[...] = dot(mine, dpre_all, ((1,), (1,))).astype(BF16)
 
+
+def backward(rows, cols, counts, values, grads, out, partial, *, flip):
+    width, local = grads.shape
+    side = values.shape[1]
+
     def store(k, partial):
         for c in range(local // side):
-            sent[lanes(k, width), c * side : (c + 1) * side] = partial[c].astype(BF16)
+            out[lanes(k, width), c * side : (c + 1) * side] = partial[c].astype(out.dtype)
 
     add_backward(
-        rows, cols, counts, values, grads, partial, store, 1, sent.shape[0] // width
-    )
-
-
-def backward_near(rows, cols, counts, values, grads, out, partial):
-    width, local = grads.shape
-    side = values.shape[1]
-
-    def store(k, partial):
-        for c in range(local // side):
-            out[lanes(k, width), c * side : (c + 1) * side] = partial[c]
-
-    add_backward(rows, cols, counts, values, grads, partial, store, 0, out.shape[0] // width)
+        rows, cols, counts, values, grads, partial, store, flip, out.shape[0] // width
+    )
 
 
 def add_weights(one, other, out):
@@ -199,42 +194,45 @@
     shape = jax.ShapeDtypeStruct
     totals = (local // side + 1, width, side)
 
-    pieces = [features] + [swapped(features, "node", 2 * k) for k in range(1, column)]
-    (pieces,) = call(stack, pieces, [shape((column, width, local), BF16)])
+    own_across = swapped(features, "node", 1)
+    pieces = [swapped(features, "node", 2 * k) for k in range(1, column)]
+    *pieces, own_across = lax.optimization_barrier((*pieces, own_across))
+    (pieces,) = call(stack, pieces, [shape((column - 1, width, local), BF16)])
     far_pieces = swapped(pieces, "node", 1)
     cots = gather_feat(cotangent)
-    (near,) = call(forward_near, [*meta, pieces], [shape(totals, F32)])
+    (near,) = call(forward_near, [*meta, features, pieces], [shape(totals, F32)])
     (aggregated,) = call(
         forward_far,
-        [*meta, far_pieces, near],
+        [*meta, own_across, far_pieces, near],
         [shape((width, local), BF16)],
         [pltpu.VMEM(totals, F32)],
     )
     aggs = gather_feat(aggregated)
-    activated, grads, sent, weight_part = call(
+    activated, grads, weight_part = call(
         functools.partial(middle, feat=feat),
-        [*meta, weight, *aggs, *cots],
+        [weight, *aggs, *cots],
         [
             shape((wide, side), BF16),
             shape((width, local), BF16),
-            shape((column * width, local), BF16),
             shape((wide // 2, wide), BF16),
         ],
-        [
-            pltpu.VMEM((wide, local), BF16),
-            pltpu.VMEM((wide, local), BF16),
-            pltpu.VMEM(totals, F32),
-        ],
+        [pltpu.VMEM((wide, local), BF16), pltpu.VMEM((wide, local), BF16)],
     )
     other_part = swapped(weight_part, "node", 1)
-    got = swapped(sent, "node", 1)
+    (sent,) = call(
+        functools.partial(backward, flip=1),
+        [*meta, grads],
+        [shape((column * width, local), BF16)],
+        [pltpu.VMEM(totals, F32)],
+    )
     (near_grads,) = call(
-        backward_near,
+        functools.partial(backward, flip=0),
         [*meta, grads],
         [shape((column * width, local), F32)],
         [pltpu.VMEM(totals, F32)],
     )
-    other_part, near_grads = lax.optimization_barrier((other_part, near_grads))
+    sent, near_grads, other_part = lax.optimization_barrier((sent, near_grads, other_part))
+    got = swapped(sent, "node", 1)
     (pair,) = call(add_weights, [weight_part, other_part], [shape((wide // 2, wide), BF16)])
     pairs = [pair] + [swapped(pair, "node", 2 * k) for k in range(1, column)]
     own, *chunks = call(

time: 58 us -> 50.2 us (0.87)
  waiting for transfers between devices: 26.2 us -> 17.6 us
  starting transfers between devices: 21 us -> 22.9 us
  local copies, waits for them, and re-layouts: 2.82 us -> 2.04 us
    ppermute x19 -> x20, waiting for transfers between devices: 26.2 us -> 17.6 us  [swapped(): lax.ppermute(x, axis, [(i, i ^ mask) for i in range(lax.axis_size(axis))])]
    ppermute x19 -> x20, starting transfers between devices: 21 us -> 22.9 us  [swapped(): lax.ppermute(x, axis, [(i, i ^ mask) for i in range(lax.axis_size(axis))])]
    unnamed x18, local copies, waits for them, and re-layouts: 2.82 us -> 2.04 us
    pallas_call x10 -> x11, Pallas kernels: 6.98 us -> 6.69 us  [call(): pl.pallas_call(body, in_specs=[SMEM] * scalars + [VMEM] * (len(inputs) -...]
  transfers between devices with their start and end apart: 19 -> 20, of which waited for: 11 -> 11; matrix products, arithmetic and copies ran while one was open for 0% -> 0% of each run, Pallas kernels for 7% -> 10%
where the time goes in v3:
time: 50.2 us; the launch traced here: 50 us
  starting transfers between devices  22.9 us (46%)
  waiting for transfers between devices  17.6 us (35%)
  Pallas kernels  6.69 us (13%)
  local copies, waits for them, and re-layouts  2.04 us (4%)
  between operations  0.78 us (2%)
    ppermute x20, starting transfers between devices, swapped(): lax.ppermute(x, axis, [(i, i ^ mask) for i in range(lax.axis_size(axis))])  22.9 us
    ppermute x20, waiting for transfers between devices, swapped(): lax.ppermute(x, axis, [(i, i ^ mask) for i in range(lax.axis_size(axis))])  17.6 us
    pallas_call x11, Pallas kernels, call(): pl.pallas_call(body, in_specs=[SMEM] * scalars + [VMEM] * (len(inputs) -...  6.69 us
    unnamed x18, local copies, waits for them, and re-layouts  2.04 us
  transfers between devices with their start and end apart: 20, of which 11 were waited for; matrix products, arithmetic and copies ran while one was open for 0% of the time, Pallas kernels for 10%

profile of v3, /device:TPU:0, one launch (start us, length us, event | category | flops | bytes accessed | tf_op | source)
XLA Modules:
  0.0 50.0 jit_solution(18274428050050278875)
XLA Ops:
  0.6 0.0 copy-start.4
  0.6 0.0 copy-start.3
  0.7 0.0 copy-start.6
  0.7 3.1 %collective-permute-start = (bf16[64,512]{1,0:T(8,128)(2,1)}, bf16[64,512]{1,0:T(8,128)(2,1)S(1)}, u32[]{:S(2)}, u32[]{:S(2)}) collective-permute-start(bf16[64,512]{1,0:T(8,128)(2,1)} %first.1), channel_id=1, source_target_pairs={{0,8},{4,12},{8,0},{12,4},{16,24},{20,28},{24,16},{28,20},{1,9},{5... | collective-permute-start | bytes 196616 | tf_op jit(solution)/shard_map/ppermute | solution.py:17
  3.7 2.6 %collective-permute-start.1 = (bf16[64,512]{1,0:T(8,128)(2,1)}, bf16[64,512]{1,0:T(8,128)(2,1)S(1)}, u32[]{:S(2)}, u32[]{:S(2)}) collective-permute-start(bf16[64,512]{1,0:T(8,128)(2,1)} %first.1), channel_id=1, source_target_pairs={{0,16},{4,20},{8,24},{12,28},{16,0},{20,4},{24,8},{28,12},{1,17},{... | collective-permute-start | bytes 196616 | tf_op jit(solution)/shard_map/ppermute | solution.py:17
  6.3 0.0 collective-permute-start.2
  6.3 1.7 %collective-permute-start.3 = (bf16[64,512]{1,0:T(8,128)(2,1)}, bf16[64,512]{1,0:T(8,128)(2,1)S(1)}, u32[]{:S(2)}, u32[]{:S(2)}) collective-permute-start(bf16[64,512]{1,0:T(8,128)(2,1)} %first.1), channel_id=1, source_target_pairs={{0,4},{4,0},{8,12},{12,8},{16,20},{20,16},{24,28},{28,24},{1,5},{5... | collective-permute-start | bytes 196616 | tf_op jit(solution)/shard_map/ppermute | solution.py:17
  8.1 0.0 collective-permute-done.refs_0_
  8.1 3.2 %collective-permute-done.1.refs_1_ = bf16[64,512]{1,0:T(8,128)(2,1)S(1)} collective-permute-done((bf16[64,512]{1,0:T(8,128)(2,1)}, bf16[64,512]{1,0:T(8,128)(2,1)S(1)}, u32[]{:S(2)}, u32[]{:S(2)}) %collective-permute-start.1) | collective-permute-done | bytes 65568 | tf_op jit(solution)/shard_map/ppermute | solution.py:17
  11.2 1.4 %collective-permute-done.2.refs_2_ = bf16[64,512]{1,0:T(8,128)(2,1)S(1)} collective-permute-done((bf16[64,512]{1,0:T(8,128)(2,1)}, bf16[64,512]{1,0:T(8,128)(2,1)S(1)}, u32[]{:S(2)}, u32[]{:S(2)}) %collective-permute-start.2) | collective-permute-done | bytes 65568 | tf_op jit(solution)/shard_map/ppermute | solution.py:17
  12.6 0.0 collective-permute-done.3.first
  12.7 0.0 copy-start.7
  12.7 1.6 %collective-permute-start.4 = (bf16[3,64,512]{2,1,0:T(8,128)(2,1)S(1)}, bf16[3,64,512]{2,1,0:T(8,128)(2,1)S(1)}, u32[]{:S(2)}, u32[]{:S(2)}) collective-permute-start(bf16[3,64,512]{2,1,0:T(8,128)(2,1)S(1)} %shard_map.94.rest), channel_id=1, source_target_pairs={{0,4},{4,0},{8,12},{12,8},{16,20},{20,16},{24,28},{28,24},{1,5},{5... | collective-permute-start | bytes 589832 | tf_op jit(solution)/shard_map/ppermute | solution.py:17
  14.2 0.0 copy-done.3
  14.2 1.5 %collective-permute-start.9 = (bf16[256,128]{1,0:T(8,128)(2,1)S(1)}, bf16[256,128]{1,0:T(8,128)(2,1)S(1)}, u32[]{:S(2)}, u32[]{:S(2)}) collective-permute-start(bf16[256,128]{1,0:T(8,128)(2,1)S(1)} %copy-done.3), channel_id=1, source_target_pairs={{0,2},{1,3},{2,0},{3,1},{4,6},{5,7},{6,4},{7,5},{8,10},{9,11},{10,... | collective-permute-start | bytes 196616 | tf_op jit(solution)/shard_map/ppermute | solution.py:17
  15.8 0.0 copy-done.6
  15.8 0.1 copy.12.rows
  15.8 0.0 copy-done.7
  15.8 0.0 copy-start.5
  15.8 0.1 copy.13.cols
  15.9 0.0 copy-done.4
  15.9 0.6 %copy-done.5 = s32[8]{0:T(128)S(1)} copy-done((s32[8]{0:T(128)S(1)}, s32[8]{0:T(128)}, u32[]{:S(2)}) %copy-start.5) | copy-done | bytes 56
  16.5 0.0 copy-start
  16.5 1.2 %copy-done = bf16[32,128,128]{2,1,0:T(8,128)(2,1)S(1)} copy-done((bf16[32,128,128]{2,1,0:T(8,128)(2,1)S(1)}, bf16[32,128,128]{2,1,0:T(8,128)(2,1)}, u32[]{:S(2)}) %copy-start) | copy-done | bytes 1048600
  17.7 1.1 %shard_map.95.near = f32[5,64,128]{2,1,0:T(8,128)S(1)} custom-call(s32[8,4]{1,0:T(8,128)S(1)} %copy.12.rows, s32[8,4]{1,0:T(8,128)S(1)} %copy.13.cols, s32[8]{0:T(128)S(1)} %copy-done.5, bf16[32,128,128]{2,1,0:T(8,128)(2,1)S(1)} %copy-done, bf16[64,512]{1,0:T(8,128)(2,1)S(1)} %copy-done.4, bf16[3,64,512]{2,1,0:T(8,128)(2,1)S(1)} %shard_map.94.rest), custom_call_target="tpu_custom_call" | custom-call | tf_op jit(solution)/shard_map/pallas_call | solution.py:51
  18.9 0.0 copy-start.2
  18.9 0.0 collective-permute-done.4.rest
  18.9 0.1 copy-done.1
  18.9 1.2 %shard_map.96.refs_0_ = bf16[64,512]{1,0:T(8,128)(2,1)S(1)} custom-call(s32[8,4]{1,0:T(8,128)S(1)} %copy.12.rows, s32[8,4]{1,0:T(8,128)S(1)} %copy.13.cols, s32[8]{0:T(128)S(1)} %copy-done.5, bf16[32,128,128]{2,1,0:T(8,128)(2,1)S(1)} %copy-done.1, bf16[64,512]{1,0:T(8,128)(2,1)S(1)} %collective-permute-done.3.first, ...), custom_call_target="tpu_custom_call" | custom-call | tf_op jit(solution)/shard_map/pallas_call | solution.py:51
  20.1 1.0 %collective-permute-start.6 = (bf16[64,512]{1,0:T(8,128)(2,1)S(1)}, bf16[64,512]{1,0:T(8,128)(2,1)S(1)}, u32[]{:S(2)}, u32[]{:S(2)}) collective-permute-start(bf16[64,512]{1,0:T(8,128)(2,1)S(1)} %shard_map.96.refs_0_), channel_id=1, source_target_pairs={{0,2},{1,3},{2,0},{3,1},{4,6},{5,7},{6,4},{7,5},{8,10},{9,11},{10,... | collective-permute-start | bytes 196616 | tf_op jit(solution)/shard_map/ppermute | solution.py:17
  21.2 0.0 collective-permute-start.8
  21.2 0.0 collective-permute-done.9.refs_6_
  21.2 0.5 %collective-permute-start.10 = (bf16[256,128]{1,0:T(8,128)(2,1)S(1)}, bf16[256,128]{1,0:T(8,128)(2,1)S(1)}, u32[]{:S(2)}, u32[]{:S(2)}) collective-permute-start(bf16[256,128]{1,0:T(8,128)(2,1)S(1)} %collective-permute-done.9.refs_6_), channel_id=1, source_target_pairs={{0,1},{1,0},{2,3},{3,2},{4,5},{5,4},{6,7},{7,6},{8,9},{9,8},{10,11... | collective-permute-start | bytes 196616 | tf_op jit(solution)/shard_map/ppermute | solution.py:17
  21.7 0.0 collective-permute-start.5
  21.7 2.8 %collective-permute-done.6.refs_2_ = bf16[64,512]{1,0:T(8,128)(2,1)S(1)} collective-permute-done((bf16[64,512]{1,0:T(8,128)(2,1)S(1)}, bf16[64,512]{1,0:T(8,128)(2,1)S(1)}, u32[]{:S(2)}, u32[]{:S(2)}) %collective-permute-start.6) | collective-permute-done | bytes 65568 | tf_op jit(solution)/shard_map/ppermute | solution.py:17
  24.4 0.0 collective-permute-start.7
  24.4 0.0 collective-permute-done.8.refs_5_
  24.4 0.0 collective-permute-done.10.refs_7_
  24.5 0.0 collective-permute-done.5.refs_1_
  24.5 1.2 %collective-permute-done.7.refs_3_ = bf16[64,512]{1,0:T(8,128)(2,1)S(1)} collective-permute-done((bf16[64,512]{1,0:T(8,128)(2,1)S(1)}, bf16[64,512]{1,0:T(8,128)(2,1)S(1)}, u32[]{:S(2)}, u32[]{:S(2)}) %collective-permute-start.7) | collective-permute-done | bytes 65568 | tf_op jit(solution)/shard_map/ppermute | solution.py:17
  25.7 0.0 copy-done.2
  25.7 0.9 %shard_map.97 = (bf16[256,128]{1,0:T(8,128)(2,1)}, bf16[64,512]{1,0:T(8,128)(2,1)S(1)}, bf16[128,256]{1,0:T(8,128)(2,1)S(1)}) custom-call(bf16[256,256]{1,0:T(8,128)(2,1)S(1)} %copy-done.2, bf16[64,512]{1,0:T(8,128)(2,1)S(1)} %shard_map.96.refs_0_, bf16[64,512]{1,0:T(8,128)(2,1)S(1)} %collective-permute-done.5.refs_1_, ...), custom_call_target="tpu_custom_call" | custom-call | tf_op jit(solution)/shard_map/pallas_call | solution.py:51
  26.6 1.0 %collective-permute-start.11 = (bf16[128,256]{1,0:T(8,128)(2,1)S(1)}, bf16[128,256]{1,0:T(8,128)(2,1)S(1)}, u32[]{:S(2)}, u32[]{:S(2)}) collective-permute-start(bf16[128,256]{1,0:T(8,128)(2,1)S(1)} %get-tuple-element.31.one), channel_id=1, source_target_pairs={{0,4},{4,0},{8,12},{12,8},{16,20},{20,16},{24,28},{28,24},{1,5},{5... | collective-permute-start | bytes 196616 | tf_op jit(solution)/shard_map/ppermute | solution.py:17
  27.6 1.0 %shard_map.98 = bf16[256,512]{1,0:T(8,128)(2,1)S(1)} custom-call(s32[8,4]{1,0:T(8,128)S(1)} %copy.12.rows, s32[8,4]{1,0:T(8,128)S(1)} %copy.13.cols, s32[8]{0:T(128)S(1)} %copy-done.5, bf16[32,128,128]{2,1,0:T(8,128)(2,1)S(1)} %copy-done.1, bf16[64,512]{1,0:T(8,128)(2,1)S(1)} %get-tuple-element.30.grads), custom_call_target="tpu_custom_call" | custom-call | tf_op jit(solution)/shard_map/pallas_call | solution.py:51
  28.5 1.0 %shard_map.99.near = f32[256,512]{1,0:T(8,128)S(1)} custom-call(s32[8,4]{1,0:T(8,128)S(1)} %copy.12.rows, s32[8,4]{1,0:T(8,128)S(1)} %copy.13.cols, s32[8]{0:T(128)S(1)} %copy-done.5, bf16[32,128,128]{2,1,0:T(8,128)(2,1)S(1)} %copy-done.1, bf16[64,512]{1,0:T(8,128)(2,1)S(1)} %get-tuple-element.30.grads), custom_call_target="tpu_custom_call" | custom-call | tf_op jit(solution)/shard_map/pallas_call | solution.py:51
  29.5 1.3 %collective-permute-done.11.other = bf16[128,256]{1,0:T(8,128)(2,1)S(1)} collective-permute-done((bf16[128,256]{1,0:T(8,128)(2,1)S(1)}, bf16[128,256]{1,0:T(8,128)(2,1)S(1)}, u32[]{:S(2)}, u32[]{:S(2)}) %collective-permute-start.11) | collective-permute-done | bytes 65568 | tf_op jit(solution)/shard_map/ppermute | solution.py:17
  30.9 1.0 %collective-permute-start.12 = (bf16[256,512]{1,0:T(8,128)(2,1)S(1)}, bf16[256,512]{1,0:T(8,128)(2,1)S(1)}, u32[]{:S(2)}, u32[]{:S(2)}) collective-permute-start(bf16[256,512]{1,0:T(8,128)(2,1)S(1)} %shard_map.98), channel_id=1, source_target_pairs={{0,4},{4,0},{8,12},{12,8},{16,20},{20,16},{24,28},{28,24},{1,5},{5... | collective-permute-start | bytes 786440 | tf_op jit(solution)/shard_map/ppermute | solution.py:17
  31.8 0.4 collective-permute-start.16
  32.2 2.2 %collective-permute-start.17 = (bf16[128,256]{1,0:T(8,128)(2,1)S(1)}, bf16[128,256]{1,0:T(8,128)(2,1)S(1)}, u32[]{:S(2)}, u32[]{:S(2)}) collective-permute-start(bf16[128,256]{1,0:T(8,128)(2,1)S(1)} %shard_map.101.refs_0_), channel_id=1, source_target_pairs={{0,16},{4,20},{8,24},{12,28},{16,0},{20,4},{24,8},{28,12},{1,17},{... | collective-permute-start | bytes 196616 | tf_op jit(solution)/shard_map/ppermute | solution.py:17
  34.5 1.8 %collective-permute-start.18 = (bf16[128,256]{1,0:T(8,128)(2,1)S(1)}, bf16[128,256]{1,0:T(8,128)(2,1)S(1)}, u32[]{:S(2)}, u32[]{:S(2)}) collective-permute-start(bf16[128,256]{1,0:T(8,128)(2,1)S(1)} %shard_map.101.refs_0_), channel_id=1, source_target_pairs={{0,24},{4,28},{8,16},{12,20},{16,8},{20,12},{24,0},{28,4},{1,25},{... | collective-permute-start | bytes 196616 | tf_op jit(solution)/shard_map/ppermute | solution.py:17
  36.3 1.8 %collective-permute-done.12.got = bf16[256,512]{1,0:T(8,128)(2,1)S(1)} collective-permute-done((bf16[256,512]{1,0:T(8,128)(2,1)S(1)}, bf16[256,512]{1,0:T(8,128)(2,1)S(1)}, u32[]{:S(2)}, u32[]{:S(2)}) %collective-permute-start.12) | collective-permute-done | bytes 262176 | tf_op jit(solution)/shard_map/ppermute | solution.py:17
  38.1 0.0 collective-permute-done.16.refs_1_
  38.1 0.7 %collective-permute-done.17.refs_2_ = bf16[128,256]{1,0:T(8,128)(2,1)S(1)} collective-permute-done((bf16[128,256]{1,0:T(8,128)(2,1)S(1)}, bf16[128,256]{1,0:T(8,128)(2,1)S(1)}, u32[]{:S(2)}, u32[]{:S(2)}) %collective-permute-start.17) | collective-permute-done | bytes 65568 | tf_op jit(solution)/shard_map/ppermute | solution.py:17
  38.8 1.7 %collective-permute-done.18.refs_3_ = bf16[128,256]{1,0:T(8,128)(2,1)S(1)} collective-permute-done((bf16[128,256]{1,0:T(8,128)(2,1)S(1)}, bf16[128,256]{1,0:T(8,128)(2,1)S(1)}, u32[]{:S(2)}, u32[]{:S(2)}) %collective-permute-start.18) | collective-permute-done | bytes 65568 | tf_op jit(solution)/shard_map/ppermute | solution.py:17
  40.6 0.1 collective-permute-start.19
  40.6 0.1 collective-permute-start.13
  40.7 2.5 %collective-permute-start.14 = (bf16[64,512]{1,0:T(8,128)(2,1)S(1)}, bf16[64,512]{1,0:T(8,128)(2,1)S(1)}, u32[]{:S(2)}, u32[]{:S(2)}) collective-permute-start(bf16[64,512]{1,0:T(8,128)(2,1)S(1)} %get-tuple-element.35), channel_id=1, source_target_pairs={{0,16},{4,20},{8,24},{12,28},{16,0},{20,4},{24,8},{28,12},{1,17},{... | collective-permute-start | bytes 196616 | tf_op jit(solution)/shard_map/ppermute | solution.py:17
  43.2 1.9 %collective-permute-start.15 = (bf16[64,512]{1,0:T(8,128)(2,1)S(1)}, bf16[64,512]{1,0:T(8,128)(2,1)S(1)}, u32[]{:S(2)}, u32[]{:S(2)}) collective-permute-start(bf16[64,512]{1,0:T(8,128)(2,1)S(1)} %get-tuple-element.36), channel_id=1, source_target_pairs={{0,24},{4,28},{8,16},{12,20},{16,8},{20,12},{24,0},{28,4},{1,25},{... | collective-permute-start | bytes 196616 | tf_op jit(solution)/shard_map/ppermute | solution.py:17
  45.1 0.0 collective-permute-done.19.other
  45.1 0.7 %shard_map.103 = f32[256,256]{1,0:T(8,128)} custom-call(f32[128,256]{1,0:T(8,128)S(1)} %shard_map.102.mine, f32[128,256]{1,0:T(8,128)S(1)} %collective-permute-done.19.other), custom_call_target="tpu_custom_call" | custom-call | tf_op jit(solution)/shard_map/pallas_call | solution.py:51
  45.8 0.5 collective-permute-done.13.refs_1_
  46.3 2.3 %collective-permute-done.14.refs_2_ = bf16[64,512]{1,0:T(8,128)(2,1)S(1)} collective-permute-done((bf16[64,512]{1,0:T(8,128)(2,1)S(1)}, bf16[64,512]{1,0:T(8,128)(2,1)S(1)}, u32[]{:S(2)}, u32[]{:S(2)}) %collective-permute-start.14) | collective-permute-done | bytes 65568 | tf_op jit(solution)/shard_map/ppermute | solution.py:17
  48.6 0.8 %collective-permute-done.15.refs_3_ = bf16[64,512]{1,0:T(8,128)(2,1)S(1)} collective-permute-done((bf16[64,512]{1,0:T(8,128)(2,1)S(1)}, bf16[64,512]{1,0:T(8,128)(2,1)S(1)}, u32[]{:S(2)}, u32[]{:S(2)}) %collective-permute-start.15) | collective-permute-done | bytes 65568 | tf_op jit(solution)/shard_map/ppermute | solution.py:17
  49.3 0.7 %shard_map.104 = f32[64,512]{1,0:T(8,128)} custom-call(f32[64,512]{1,0:T(8,128)S(1)} %get-tuple-element.43.refs_0_, bf16[64,512]{1,0:T(8,128)(2,1)S(1)} %collective-permute-done.13.refs_1_, bf16[64,512]{1,0:T(8,128)(2,1)S(1)} %collective-permute-done.14.refs_2_, bf16[64,512]{1,0:T(8,128)(2,1)S(1)} %collective-permute-done.15.refs_3_), custom_call_target="tpu_custom_call" | custom-call | tf_op jit(solution)/shard_map/pallas_call | solution.py:51
  (5 shorter events, 0.1 us)
Async XLA Ops:
  0.6 15.3 %copy-start.4 = (bf16[64,512]{1,0:T(8,128)(2,1)S(1)}, bf16[64,512]{1,0:T(8,128)(2,1)}, u32[]{:S(2)}) copy-start(bf16[64,512]{1,0:T(8,128)(2,1)} %first.1) | copy-start | bytes 196612
  0.6 13.6 %copy-start.3 = (bf16[256,128]{1,0:T(8,128)(2,1)S(1)}, bf16[256,128]{1,0:T(8,128)(2,1)}, u32[]{:S(2)}) copy-start(bf16[256,128]{1,0:T(8,128)(2,1)} %refs_4_.1) | copy-start | bytes 196612
  0.7 15.1 %copy-start.6 = (s32[8,4]{0,1:T(4,128)S(1)}, s32[8,4]{0,1:T(4,128)}, u32[]{:S(2)}) copy-start(s32[8,4]{0,1:T(4,128)} %param.9) | copy-start | bytes 388
  0.7 7.4 %collective-permute-start = (bf16[64,512]{1,0:T(8,128)(2,1)}, bf16[64,512]{1,0:T(8,128)(2,1)S(1)}, u32[]{:S(2)}, u32[]{:S(2)}) collective-permute-start(bf16[64,512]{1,0:T(8,128)(2,1)} %first.1), channel_id=1, source_target_pairs={{0,8},{4,12},{8,0},{12,4},{16,24},{20,28},{24,16},{28,20},{1,9},{5... | collective-permute-start | bytes 196616 | tf_op jit(solution)/shard_map/ppermute | solution.py:17
  3.7 7.5 %collective-permute-start.1 = (bf16[64,512]{1,0:T(8,128)(2,1)}, bf16[64,512]{1,0:T(8,128)(2,1)S(1)}, u32[]{:S(2)}, u32[]{:S(2)}) collective-permute-start(bf16[64,512]{1,0:T(8,128)(2,1)} %first.1), channel_id=1, source_target_pairs={{0,16},{4,20},{8,24},{12,28},{16,0},{20,4},{24,8},{28,12},{1,17},{... | collective-permute-start | bytes 196616 | tf_op jit(solution)/shard_map/ppermute | solution.py:17
  6.3 6.3 %collective-permute-start.2 = (bf16[64,512]{1,0:T(8,128)(2,1)}, bf16[64,512]{1,0:T(8,128)(2,1)S(1)}, u32[]{:S(2)}, u32[]{:S(2)}) collective-permute-start(bf16[64,512]{1,0:T(8,128)(2,1)} %first.1), channel_id=1, source_target_pairs={{0,24},{4,28},{8,16},{12,20},{16,8},{20,12},{24,0},{28,4},{1,25},{... | collective-permute-start | bytes 196616 | tf_op jit(solution)/shard_map/ppermute | solution.py:17
  6.3 6.3 %collective-permute-start.3 = (bf16[64,512]{1,0:T(8,128)(2,1)}, bf16[64,512]{1,0:T(8,128)(2,1)S(1)}, u32[]{:S(2)}, u32[]{:S(2)}) collective-permute-start(bf16[64,512]{1,0:T(8,128)(2,1)} %first.1), channel_id=1, source_target_pairs={{0,4},{4,0},{8,12},{12,8},{16,20},{20,16},{24,28},{28,24},{1,5},{5... | collective-permute-start | bytes 196616 | tf_op jit(solution)/shard_map/ppermute | solution.py:17
  12.7 3.2 %copy-start.7 = (s32[8,4]{0,1:T(4,128)S(1)}, s32[8,4]{0,1:T(4,128)}, u32[]{:S(2)}) copy-start(s32[8,4]{0,1:T(4,128)} %param.10) | copy-start | bytes 388
  12.7 6.2 %collective-permute-start.4 = (bf16[3,64,512]{2,1,0:T(8,128)(2,1)S(1)}, bf16[3,64,512]{2,1,0:T(8,128)(2,1)S(1)}, u32[]{:S(2)}, u32[]{:S(2)}) collective-permute-start(bf16[3,64,512]{2,1,0:T(8,128)(2,1)S(1)} %shard_map.94.rest), channel_id=1, source_target_pairs={{0,4},{4,0},{8,12},{12,8},{16,20},{20,16},{24,28},{28,24},{1,5},{5... | collective-permute-start | bytes 589832 | tf_op jit(solution)/shard_map/ppermute | solution.py:17
  14.2 6.9 %collective-permute-start.9 = (bf16[256,128]{1,0:T(8,128)(2,1)S(1)}, bf16[256,128]{1,0:T(8,128)(2,1)S(1)}, u32[]{:S(2)}, u32[]{:S(2)}) collective-permute-start(bf16[256,128]{1,0:T(8,128)(2,1)S(1)} %copy-done.3), channel_id=1, source_target_pairs={{0,2},{1,3},{2,0},{3,1},{4,6},{5,7},{6,4},{7,5},{8,10},{9,11},{10,... | collective-permute-start | bytes 196616 | tf_op jit(solution)/shard_map/ppermute | solution.py:17
  15.8 0.7 %copy-start.5 = (s32[8]{0:T(128)S(1)}, s32[8]{0:T(128)}, u32[]{:S(2)}) copy-start(s32[8]{0:T(128)} %counts.7) | copy-start | bytes 100
  16.5 1.2 %copy-start = (bf16[32,128,128]{2,1,0:T(8,128)(2,1)S(1)}, bf16[32,128,128]{2,1,0:T(8,128)(2,1)}, u32[]{:S(2)}) copy-start(bf16[32,128,128]{2,1,0:T(8,128)(2,1)} %values.7) | copy-start | bytes 3145732
  17.7 1.2 %copy-start.1 = (bf16[32,128,128]{2,1,0:T(8,128)(2,1)S(1)}, bf16[32,128,128]{2,1,0:T(8,128)(2,1)}, u32[]{:S(2)}) copy-start(bf16[32,128,128]{2,1,0:T(8,128)(2,1)} %values.7) | copy-start | bytes 3145732
  18.9 6.8 %copy-start.2 = (bf16[256,256]{1,0:T(8,128)(2,1)S(1)}, bf16[256,256]{1,0:T(8,128)(2,1)}, u32[]{:S(2)}) copy-start(bf16[256,256]{1,0:T(8,128)(2,1)} %weight.1) | copy-start | bytes 393220
  20.1 4.3 %collective-permute-start.6 = (bf16[64,512]{1,0:T(8,128)(2,1)S(1)}, bf16[64,512]{1,0:T(8,128)(2,1)S(1)}, u32[]{:S(2)}, u32[]{:S(2)}) collective-permute-start(bf16[64,512]{1,0:T(8,128)(2,1)S(1)} %shard_map.96.refs_0_), channel_id=1, source_target_pairs={{0,2},{1,3},{2,0},{3,1},{4,6},{5,7},{6,4},{7,5},{8,10},{9,11},{10,... | collective-permute-start | bytes 196616 | tf_op jit(solution)/shard_map/ppermute | solution.py:17
  21.2 3.3 %collective-permute-start.8 = (bf16[256,128]{1,0:T(8,128)(2,1)S(1)}, bf16[256,128]{1,0:T(8,128)(2,1)S(1)}, u32[]{:S(2)}, u32[]{:S(2)}) collective-permute-start(bf16[256,128]{1,0:T(8,128)(2,1)S(1)} %copy-done.3), channel_id=1, source_target_pairs={{0,1},{1,0},{2,3},{3,2},{4,5},{5,4},{6,7},{7,6},{8,9},{9,8},{10,11... | collective-permute-start | bytes 196616 | tf_op jit(solution)/shard_map/ppermute | solution.py:17
  21.2 3.3 %collective-permute-start.10 = (bf16[256,128]{1,0:T(8,128)(2,1)S(1)}, bf16[256,128]{1,0:T(8,128)(2,1)S(1)}, u32[]{:S(2)}, u32[]{:S(2)}) collective-permute-start(bf16[256,128]{1,0:T(8,128)(2,1)S(1)} %collective-permute-done.9.refs_6_), channel_id=1, source_target_pairs={{0,1},{1,0},{2,3},{3,2},{4,5},{5,4},{6,7},{7,6},{8,9},{9,8},{10,11... | collective-permute-start | bytes 196616 | tf_op jit(solution)/shard_map/ppermute | solution.py:17
  21.7 2.8 %collective-permute-start.5 = (bf16[64,512]{1,0:T(8,128)(2,1)S(1)}, bf16[64,512]{1,0:T(8,128)(2,1)S(1)}, u32[]{:S(2)}, u32[]{:S(2)}) collective-permute-start(bf16[64,512]{1,0:T(8,128)(2,1)S(1)} %shard_map.96.refs_0_), channel_id=1, source_target_pairs={{0,1},{1,0},{2,3},{3,2},{4,5},{5,4},{6,7},{7,6},{8,9},{9,8},{10,11... | collective-permute-start | bytes 196616 | tf_op jit(solution)/shard_map/ppermute | solution.py:17
  24.4 1.3 %collective-permute-start.7 = (bf16[64,512]{1,0:T(8,128)(2,1)S(1)}, bf16[64,512]{1,0:T(8,128)(2,1)S(1)}, u32[]{:S(2)}, u32[]{:S(2)}) collective-permute-start(bf16[64,512]{1,0:T(8,128)(2,1)S(1)} %collective-permute-done.6.refs_2_), channel_id=1, source_target_pairs={{0,1},{1,0},{2,3},{3,2},{4,5},{5,4},{6,7},{7,6},{8,9},{9,8},{10,11... | collective-permute-start | bytes 196616 | tf_op jit(solution)/shard_map/ppermute | solution.py:17
  26.6 4.3 %collective-permute-start.11 = (bf16[128,256]{1,0:T(8,128)(2,1)S(1)}, bf16[128,256]{1,0:T(8,128)(2,1)S(1)}, u32[]{:S(2)}, u32[]{:S(2)}) collective-permute-start(bf16[128,256]{1,0:T(8,128)(2,1)S(1)} %get-tuple-element.31.one), channel_id=1, source_target_pairs={{0,4},{4,0},{8,12},{12,8},{16,20},{20,16},{24,28},{28,24},{1,5},{5... | collective-permute-start | bytes 196616 | tf_op jit(solution)/shard_map/ppermute | solution.py:17
  30.9 7.2 %collective-permute-start.12 = (bf16[256,512]{1,0:T(8,128)(2,1)S(1)}, bf16[256,512]{1,0:T(8,128)(2,1)S(1)}, u32[]{:S(2)}, u32[]{:S(2)}) collective-permute-start(bf16[256,512]{1,0:T(8,128)(2,1)S(1)} %shard_map.98), channel_id=1, source_target_pairs={{0,4},{4,0},{8,12},{12,8},{16,20},{20,16},{24,28},{28,24},{1,5},{5... | collective-permute-start | bytes 786440 | tf_op jit(solution)/shard_map/ppermute | solution.py:17
  31.8 6.3 %collective-permute-start.16 = (bf16[128,256]{1,0:T(8,128)(2,1)S(1)}, bf16[128,256]{1,0:T(8,128)(2,1)S(1)}, u32[]{:S(2)}, u32[]{:S(2)}) collective-permute-start(bf16[128,256]{1,0:T(8,128)(2,1)S(1)} %shard_map.101.refs_0_), channel_id=1, source_target_pairs={{0,8},{4,12},{8,0},{12,4},{16,24},{20,28},{24,16},{28,20},{1,9},{5... | collective-permute-start | bytes 196616 | tf_op jit(solution)/shard_map/ppermute | solution.py:17
  32.2 6.6 %collective-permute-start.17 = (bf16[128,256]{1,0:T(8,128)(2,1)S(1)}, bf16[128,256]{1,0:T(8,128)(2,1)S(1)}, u32[]{:S(2)}, u32[]{:S(2)}) collective-permute-start(bf16[128,256]{1,0:T(8,128)(2,1)S(1)} %shard_map.101.refs_0_), channel_id=1, source_target_pairs={{0,16},{4,20},{8,24},{12,28},{16,0},{20,4},{24,8},{28,12},{1,17},{... | collective-permute-start | bytes 196616 | tf_op jit(solution)/shard_map/ppermute | solution.py:17
  34.5 6.1 %collective-permute-start.18 = (bf16[128,256]{1,0:T(8,128)(2,1)S(1)}, bf16[128,256]{1,0:T(8,128)(2,1)S(1)}, u32[]{:S(2)}, u32[]{:S(2)}) collective-permute-start(bf16[128,256]{1,0:T(8,128)(2,1)S(1)} %shard_map.101.refs_0_), channel_id=1, source_target_pairs={{0,24},{4,28},{8,16},{12,20},{16,8},{20,12},{24,0},{28,4},{1,25},{... | collective-permute-start | bytes 196616 | tf_op jit(solution)/shard_map/ppermute | solution.py:17
  40.6 4.5 %collective-permute-start.19 = (f32[128,256]{1,0:T(8,128)S(1)}, f32[128,256]{1,0:T(8,128)S(1)}, u32[]{:S(2)}, u32[]{:S(2)}) collective-permute-start(f32[128,256]{1,0:T(8,128)S(1)} %shard_map.102.mine), channel_id=1, source_target_pairs={{0,1},{1,0},{2,3},{3,2},{4,5},{5,4},{6,7},{7,6},{8,9},{9,8},{10,11... | collective-permute-start | bytes 393224 | tf_op jit(solution)/shard_map/ppermute | solution.py:17
  40.6 5.6 %collective-permute-start.13 = (bf16[64,512]{1,0:T(8,128)(2,1)S(1)}, bf16[64,512]{1,0:T(8,128)(2,1)S(1)}, u32[]{:S(2)}, u32[]{:S(2)}) collective-permute-start(bf16[64,512]{1,0:T(8,128)(2,1)S(1)} %get-tuple-element.34), channel_id=1, source_target_pairs={{0,8},{4,12},{8,0},{12,4},{16,24},{20,28},{24,16},{28,20},{1,9},{5... | collective-permute-start | bytes 196616 | tf_op jit(solution)/shard_map/ppermute | solution.py:17
  40.7 7.8 %collective-permute-start.14 = (bf16[64,512]{1,0:T(8,128)(2,1)S(1)}, bf16[64,512]{1,0:T(8,128)(2,1)S(1)}, u32[]{:S(2)}, u32[]{:S(2)}) collective-permute-start(bf16[64,512]{1,0:T(8,128)(2,1)S(1)} %get-tuple-element.35), channel_id=1, source_target_pairs={{0,16},{4,20},{8,24},{12,28},{16,0},{20,4},{24,8},{28,12},{1,17},{... | collective-permute-start | bytes 196616 | tf_op jit(solution)/shard_map/ppermute | solution.py:17
  43.2 6.1 %collective-permute-start.15 = (bf16[64,512]{1,0:T(8,128)(2,1)S(1)}, bf16[64,512]{1,0:T(8,128)(2,1)S(1)}, u32[]{:S(2)}, u32[]{:S(2)}) collective-permute-start(bf16[64,512]{1,0:T(8,128)(2,1)S(1)} %get-tuple-element.36), channel_id=1, source_target_pairs={{0,24},{4,28},{8,16},{12,20},{16,8},{20,12},{24,0},{28,4},{1,25},{... | collective-permute-start | bytes 196616 | tf_op jit(solution)/shard_map/ppermute | solution.py:17

commit v4 on v3

v4 whole, which is shorter than its diff:
```python
import functools

import jax
import jax.numpy as jnp
from jax import lax
from jax.experimental import pallas as pl
from jax.experimental.pallas import tpu as pltpu
from jax.sharding import PartitionSpec as P

BF16 = jnp.bfloat16
F32 = jnp.float32
SMEM = pl.BlockSpec(memory_space=pltpu.SMEM)
VMEM = pl.BlockSpec(memory_space=pltpu.VMEM)
LARGE = pl.CostEstimate(flops=10**10, transcendentals=0, bytes_accessed=1 << 20)
SMALL = pl.CostEstimate(flops=1 << 10, transcendentals=0, bytes_accessed=1 << 10)


def swapped(x, axis, mask):
    return lax.ppermute(x, axis, [(i, i ^ mask) for i in range(lax.axis_size(axis))])


def dot(a, b, dims):
    return lax.dot_general(a, b, (dims, ((), ())), preferred_element_type=F32)


def each(count, body):
    if count <= 8:
        for k in range(count):
            body(k)
    else:

        def step(k, carry):
            body(k)
            return carry

        lax.fori_loop(0, count, step, 0)


def lanes(block, side):
    start = block * side
    return pl.ds(start if isinstance(start, int) else pl.multiple_of(start, side), side)


def tree_sum(terms):
    while len(terms) > 1:
        terms = [a + b for a, b in zip(terms[::2], terms[1::2])]
    return terms[0]


def call(body, inputs, outputs, scratch=(), cost=None, spec=VMEM):
    scalars = sum(1 for x in inputs if x.dtype == jnp.int32)
    held = sum(x.size * x.dtype.itemsize for x in [*inputs, *outputs])
    return pl.pallas_call(
        body,
        in_specs=[SMEM] * scalars + [spec] * (len(inputs) - scalars),
        out_specs=[VMEM] * len(outputs),
        out_shape=list(outputs),
        scratch_shapes=list(scratch),
        cost_estimate=cost,
        compiler_params=pltpu.CompilerParams(vmem_limit_bytes=2 * held + (8 << 20)),
    )(*inputs)


def prepare(rows, cols, counts, source, values, row_masks, col_masks, arrival):
    copy = pltpu.make_async_copy(source, values, arrival)
    copy.start()
    slots = rows.shape[0]
    shape = row_masks.shape[2:]

    def one(k):
        for slot in range(slots):
            live = slot < counts[k]
            for ids, masks in ((rows, row_masks), (cols, col_masks)):
                block = jnp.full(shape, jnp.where(live, ids[slot, k], -1), jnp.int32)
                for b in range(masks.shape[1]):
                    masks[k * slots + slot, b] = jnp.where(block == b, 1.0, 0.0).astype(BF16)

    each(rows.shape[1], one)
    copy.wait()


def tile_sums(values, pick, place, piece, pair, transposed):
    blocks = pick.shape[1]
    slots = values.shape[0] // lax.axis_size("node")
    side = values.shape[1]
    high = pick.shape[2]
    loaded = [piece[:, b * side : (b + 1) * side] for b in range(blocks)]
    fold = (-1, high, side)
    sums = [[] for _ in range(blocks)]
    for slot in range(slots):
        at = pair * slots + slot
        chosen = tree_sum([loaded[b].reshape(fold) * pick[at, b] for b in range(blocks)])
        chosen = chosen.reshape(loaded[0].shape)
        product = dot(chosen, values[at], ((1,), (1 if transposed else 0,))).reshape(fold)
        for b in range(blocks):
            sums[b].append(product * place[at, b].astype(F32))
    return [tree_sum(s).reshape(loaded[0].shape) for s in sums]


def forward_near(values, row_masks, col_masks, first, rest, across, totals):
    own = lax.axis_index("node")

    def one(k, piece):
        sums = tile_sums(values, col_masks, row_masks, piece, own ^ k, True)
        for r, part in enumerate(sums):
            totals[r] = part if piece is first else totals[r] + part

    one(0, first)
    one(1, across)
    each(rest.shape[0], lambda k: one(2 * k + 2, rest.at[k]))


def forward_far(values, row_masks, col_masks, rest, near, out, totals):
    own = lax.axis_index("node") ^ 1
    side = values.shape[1]
    totals[...] = near[...]

    def one(k):
        pair = own ^ (2 * k + 2)
        sums = tile_sums(values, col_masks, row_masks, rest.at[k], pair, True)
        for r, part in enumerate(sums):
            totals[r] += part

    each(rest.shape[0], one)
    for r in range(totals.shape[0]):
        out[:, r * side : (r + 1) * side] = totals[r].astype(BF16)


def add_backward(values, row_masks, col_masks, grads, out, flip):
    own = lax.axis_index("node") ^ flip
    width = grads.shape[0]
    side = values.shape[1]

    def one(k):
        sums = tile_sums(values, row_masks, col_masks, grads, own ^ (2 * k), False)
        for c, part in enumerate(sums):
            out[lanes(k, width), c * side : (c + 1) * side] = part.astype(out.dtype)

    each(out.shape[0] // width, one)


def gather_feat(x):
    far = [swapped(x, "feat", m) for m in range(2, lax.axis_size("feat"), 2)]
    held = []
    for piece in [x, *far]:
        held += [piece, swapped(piece, "feat", 1)]
    return held


def stack(*refs):
    pieces, out = refs[:-1], refs[-1]
    for k, piece in enumerate(pieces):
        out[k] = piece[...]


def middle(values, row_masks, col_masks, weight, *refs, feat):
    aggs, cots = refs[:feat], refs[feat : 2 * feat]
    activated, grads, weight_part, sent, agg_full, dpre_full = refs[2 * feat :]
    index = lax.axis_index("feat")
    width, local = aggs[0].shape
    side = cots[0].shape[1]
    for m in range(feat):
        agg_full[lanes(index ^ m, width), :] = aggs[m][...]
    for m in range(feat):
        at = lanes(index ^ m, side)
        pre = dot(weight[...], agg_full[:, at], ((0,), (0,)))
        sigma = 1.0 / (1.0 + jnp.exp(-pre))
        if m == 0:
            activated[...] = (pre * sigma).astype(BF16)
        dpre = cots[m][...].astype(F32) * sigma * (1.0 + pre * (1.0 - sigma))
        dpre_full[:, at] = dpre.astype(BF16)
    dpre_all = dpre_full[...]
    grads[...] = dot(weight[lanes(index, width), :], dpre_all, ((1,), (0,))).astype(BF16)
    mine = agg_full[lanes(index & 1, weight_part.shape[0]), :]
    weight_part[...] = dot(mine, dpre_all, ((1,), (1,))).astype(BF16)
    add_backward(values, row_masks, col_masks, grads, sent, 1)


def backward_near(values, row_masks, col_masks, grads, out):
    add_backward(values, row_masks, col_masks, grads, out, 0)


def add_weights(one, other, out):
    out[...] = (one[...].astype(F32) + other[...].astype(F32)).astype(BF16)


def sum_weights(*refs):
    refs[-1][...] = tree_sum([r[...].astype(F32) for r in refs[:-1]])


def lay_out(mine, other, activated, out, activated_out):
    activated_out[...] = activated[...]
    core = lax.axis_index("feat") & 1
    out[lanes(core, mine.shape[0]), :] = mine[...]
    out[lanes(core ^ 1, mine.shape[0]), :] = other[...]


def add_pair(near, got, own, *sent):
    width = own.shape[0]
    own[...] = near[:width] + got[:width].astype(F32)
    for k, out in enumerate(sent, 1):
        rows = slice(k * width, (k + 1) * width)
        out[...] = (near[rows] + got[rows].astype(F32)).astype(BF16)


def add_column(*refs):
    refs[-1][...] = tree_sum([r[...].astype(F32) for r in refs[:-1]])


def per_device(features, tile_values, tile_rows, tile_cols, tile_counts, weight, cotangent):
    nodes = lax.axis_size("node")
    feat = lax.axis_size("feat")
    column = nodes // 2
    width, local = features.shape
    wide = weight.shape[0]
    side = tile_values.shape[1]
    shape = jax.ShapeDtypeStruct
    totals = (local // side, width, side)

    own_across = swapped(features, "node", 1)
    pieces = [swapped(features, "node", 2 * k) for k in range(1, column)]
    masks = shape((tile_values.shape[0], local // side, 16, side), BF16)
    tiles = call(
        prepare,
        [tile_rows.T, tile_cols.T, tile_counts, tile_values],
        [shape(tile_values.shape, BF16), masks, masks],
        [pltpu.SemaphoreType.DMA],
        spec=pl.BlockSpec(memory_space=pltpu.HBM),
    )
    *pieces, own_across, t0, t1, t2 = lax.optimization_barrier((*pieces, own_across, *tiles))
    tiles = (t0, t1, t2)
    (pieces,) = call(stack, pieces, [shape((column - 1, width, local), BF16)])
    far_pieces = swapped(pieces, "node", 1)
    cots = gather_feat(cotangent)
    (near,) = call(
        forward_near, [*tiles, features, pieces, own_across], [shape(totals, F32)]
    )
    (aggregated,) = call(
        forward_far,
        [*tiles, far_pieces, near],
        [shape((width, local), BF16)],
        [pltpu.VMEM(totals, F32)],
    )
    aggs = gather_feat(aggregated)
    activated, grads, weight_part, sent = call(
        functools.partial(middle, feat=feat),
        [*tiles, weight, *aggs, *cots],
        [
            shape((wide, side), BF16),
            shape((width, local), BF16),
            shape((wide // 2, wide), BF16),
            shape((column * width, local), BF16),
        ],
        [pltpu.VMEM((wide, local), BF16), pltpu.VMEM((wide, local), BF16)],
    )
    other_part = swapped(weight_part, "node", 1)
    got = swapped(sent, "node", 1)
    (pair,) = call(
        add_weights, [weight_part, other_part], [shape((wide // 2, wide), BF16)], cost=SMALL
    )
    pair, grads = lax.optimization_barrier((pair, grads))
    (near_grads,) = call(
        backward_near,
        [*tiles, grads],
        [shape((column * width, local), F32)],
        cost=LARGE,
    )
    pairs = [pair] + [swapped(pair, "node", 2 * k) for k in range(1, column)]
    own, *chunks = call(
        add_pair,
        [near_grads, got],
        [shape((width, local), F32)] + [shape((width, local), BF16)] * (column - 1),
        cost=SMALL,
    )
    arrived = [swapped(c, "node", 2 * k) for k, c in enumerate(chunks, 1)]
    count = len(arrived)
    held = lax.optimization_barrier((*arrived, *pairs))
    arrived, pairs = held[:count], held[count:]
    (half,) = call(sum_weights, pairs, [shape((wide // 2, wide), F32)], cost=SMALL)
    other_half = swapped(half, "feat", 1)
    (gradient,) = call(
        add_column, [own, *arrived], [shape((width, local), F32)], cost=SMALL
    )
    grad_weight, activated = call(
        lay_out,
        [half, other_half, activated],
        [shape((wide, wide), F32), shape((wide, side), BF16)],
        cost=SMALL,
    )
    return (activated, grad_weight, gradient)


def solution(mesh):
    placed = (
        P("feat", "node"),
        P("node", None, None),
        P("node", None),
        P("node", None),
        P("node"),
        P(),
        P(None, ("node", "feat")),
    )
    return jax.shard_map(
        per_device,
        mesh=mesh,
        in_specs=placed,
        out_specs=(P(None, ("node", "feat")), P(), P("feat", "node")),
        check_vma=False,
    )
```

time: 50.2 us -> 46.8 us (0.932)
  waiting for transfers between devices: 17.6 us -> 14.9 us
  Pallas kernels: 6.69 us -> 4.6 us
  starting transfers between devices: 22.9 us -> 23.8 us
  local copies, waits for them, and re-layouts: 2.04 us -> 2.58 us
    ppermute x20, waiting for transfers between devices: 17.6 us -> 14.9 us  [swapped(): lax.ppermute(x, axis, [(i, i ^ mask) for i in range(lax.axis_size(axis))])]
    pallas_call x11, Pallas kernels: 6.69 us -> 4.6 us  [call(): pl.pallas_call(body, in_specs=[SMEM] * scalars + [spec] * (len(inputs) -...]
    ppermute x20, starting transfers between devices: 22.9 us -> 23.8 us  [swapped(): lax.ppermute(x, axis, [(i, i ^ mask) for i in range(lax.axis_size(axis))])]
    unnamed x18 -> x14, local copies, waits for them, and re-layouts: 2.04 us -> 2.58 us
  transfers between devices with their start and end apart: 20 -> 20, of which waited for: 11 -> 10; matrix products, arithmetic and copies ran while one was open for 0% -> 0% of each run, Pallas kernels for 10% -> 6%
where the time goes in v4:
time: 46.8 us; the launch traced here: 46.7 us
  starting transfers between devices  23.8 us (51%)
  waiting for transfers between devices  14.9 us (32%)
  Pallas kernels  4.6 us (10%)
  local copies, waits for them, and re-layouts  2.58 us (6%)
  between operations  0.77 us (2%)
    ppermute x20, starting transfers between devices, swapped(): lax.ppermute(x, axis, [(i, i ^ mask) for i in range(lax.axis_size(axis))])  23.8 us
    ppermute x20, waiting for transfers between devices, swapped(): lax.ppermute(x, axis, [(i, i ^ mask) for i in range(lax.axis_size(axis))])  14.9 us
    pallas_call x11, Pallas kernels, call(): pl.pallas_call(body, in_specs=[SMEM] * scalars + [spec] * (len(inputs) -...  4.6 us
    unnamed x14, local copies, waits for them, and re-layouts  2.58 us
  transfers between devices with their start and end apart: 20, of which 10 were waited for; matrix products, arithmetic and copies ran while one was open for 0% of the time, Pallas kernels for 6%

profile of v4, /device:TPU:0, one launch (start us, length us, event | category | flops | bytes accessed | tf_op | source)
XLA Modules:
  0.0 46.7 jit_solution(100216380161562096)
XLA Ops:
  0.6 0.0 copy-start.4
  0.6 5.1 %collective-permute-start.2 = (bf16[64,512]{1,0:T(8,128)(2,1)}, bf16[64,512]{1,0:T(8,128)(2,1)S(1)}, u32[]{:S(2)}, u32[]{:S(2)}) collective-permute-start(bf16[64,512]{1,0:T(8,128)(2,1)} %first.1), channel_id=1, source_target_pairs={{0,24},{4,28},{8,16},{12,20},{16,8},{20,12},{24,0},{28,4},{1,25},{... | collective-permute-start | bytes 196616 | tf_op jit(solution)/shard_map/ppermute | solution.py:19
  5.8 0.0 collective-permute-start.1
  5.8 0.6 %collective-permute-start = (bf16[64,512]{1,0:T(8,128)(2,1)}, bf16[64,512]{1,0:T(8,128)(2,1)S(1)}, u32[]{:S(2)}, u32[]{:S(2)}) collective-permute-start(bf16[64,512]{1,0:T(8,128)(2,1)} %first.1), channel_id=1, source_target_pairs={{0,8},{4,12},{8,0},{12,4},{16,24},{20,28},{24,16},{28,20},{1,9},{5... | collective-permute-start | bytes 196616 | tf_op jit(solution)/shard_map/ppermute | solution.py:19
  6.4 1.6 %collective-permute-start.3 = (bf16[64,512]{1,0:T(8,128)(2,1)}, bf16[64,512]{1,0:T(8,128)(2,1)S(1)}, u32[]{:S(2)}, u32[]{:S(2)}) collective-permute-start(bf16[64,512]{1,0:T(8,128)(2,1)} %first.1), channel_id=1, source_target_pairs={{0,4},{4,0},{8,12},{12,8},{16,20},{20,16},{24,28},{28,24},{1,5},{5... | collective-permute-start | bytes 196616 | tf_op jit(solution)/shard_map/ppermute | solution.py:19
  8.0 0.0 copy-start.6
  8.0 0.0 copy-done.4
  8.0 0.7 %copy-done.6 = s32[8]{0:T(128)S(1)} copy-done((s32[8]{0:T(128)S(1)}, s32[8]{0:T(128)}, u32[]{:S(2)}) %copy-start.6) | copy-done | bytes 56
  8.7 0.0 copy-start
  8.7 1.2 %copy-done = bf16[32,128,128]{2,1,0:T(8,128)(2,1)S(1)} copy-done((bf16[32,128,128]{2,1,0:T(8,128)(2,1)S(1)}, bf16[32,128,128]{2,1,0:T(8,128)(2,1)}, u32[]{:S(2)}) %copy-start) | copy-done | bytes 1048600
  9.9 0.0 copy-start.5
  9.9 0.7 %copy-done.5 = s32[8,4]{0,1:T(4,128)S(1)} copy-done((s32[8,4]{0,1:T(4,128)S(1)}, s32[8,4]{0,1:T(4,128)}, u32[]{:S(2)}) %copy-start.5) | copy-done | bytes 152
  10.6 0.8 %shard_map.94 = (bf16[32,128,128]{2,1,0:T(8,128)(2,1)S(1)}, bf16[32,4,16,128]{3,2,1,0:T(8,128)(2,1)S(1)}, bf16[32,4,16,128]{3,2,1,0:T(8,128)(2,1)S(1)}) custom-call(s32[4,8]{1,0:T(4,128)S(1)} %bitcast.2, s32[4,8]{1,0:T(4,128)S(1)} %bitcast.3, s32[8]{0:T(128)S(1)} %copy-done.6, bf16[32,128,128]{2,1,0:T(8,128)(2,1)S(1)} %copy-done), custom_call_target="tpu_custom_call" | custom-call | tf_op jit(solution)/shard_map/pallas_call | solution.py:53
  11.4 0.0 collective-permute-done.2.refs_2_
  11.4 0.2 collective-permute-done.1.refs_1_
  11.6 0.0 collective-permute-done.refs_0_
  11.6 0.0 collective-permute-done.3.across
  11.6 0.0 copy-start.3
  11.6 0.0 copy-start.2
  11.6 1.6 %collective-permute-start.4 = (bf16[3,64,512]{2,1,0:T(8,128)(2,1)S(1)}, bf16[3,64,512]{2,1,0:T(8,128)(2,1)S(1)}, u32[]{:S(2)}, u32[]{:S(2)}) collective-permute-start(bf16[3,64,512]{2,1,0:T(8,128)(2,1)S(1)} %shard_map.95.rest), channel_id=1, source_target_pairs={{0,4},{4,0},{8,12},{12,8},{16,20},{20,16},{24,28},{28,24},{1,5},{5... | collective-permute-start | bytes 589832 | tf_op jit(solution)/shard_map/ppermute | solution.py:19
  13.2 0.0 copy-done.3
  13.2 1.5 %collective-permute-start.9 = (bf16[256,128]{1,0:T(8,128)(2,1)S(1)}, bf16[256,128]{1,0:T(8,128)(2,1)S(1)}, u32[]{:S(2)}, u32[]{:S(2)}) collective-permute-start(bf16[256,128]{1,0:T(8,128)(2,1)S(1)} %copy-done.3), channel_id=1, source_target_pairs={{0,2},{1,3},{2,0},{3,1},{4,6},{5,7},{6,4},{7,5},{8,10},{9,11},{10,... | collective-permute-start | bytes 196616 | tf_op jit(solution)/shard_map/ppermute | solution.py:19
  14.7 0.0 copy-done.2
  14.7 0.6 %shard_map.96.near = f32[4,64,128]{2,1,0:T(8,128)S(1)} custom-call(bf16[32,128,128]{2,1,0:T(8,128)(2,1)S(1)} %get-tuple-element.35.values, bf16[32,4,16,128]{3,2,1,0:T(8,128)(2,1)S(1)} %get-tuple-element.36.row_masks, bf16[32,4,16,128]{3,2,1,0:T(8,128)(2,1)S(1)} %get-tuple-element.37.col_masks, bf16[64,512]{1,0:T(8,128)(2,1)S(1)} %copy-done.2, ...), custom_call_target="tpu_custom_call" | custom-call | tf_op jit(solution)/shard_map/pallas_call | solution.py:53
  15.3 0.0 copy-start.1
  15.3 2.8 %collective-permute-done.4.rest = bf16[3,64,512]{2,1,0:T(8,128)(2,1)S(1)} collective-permute-done((bf16[3,64,512]{2,1,0:T(8,128)(2,1)S(1)}, bf16[3,64,512]{2,1,0:T(8,128)(2,1)S(1)}, u32[]{:S(2)}, u32[]{:S(2)}) %collective-permute-start.4) | collective-permute-done | bytes 196640 | tf_op jit(solution)/shard_map/ppermute | solution.py:19
  18.2 0.4 shard_map.97.refs_0_
  18.6 1.8 %collective-permute-start.6 = (bf16[64,512]{1,0:T(8,128)(2,1)S(1)}, bf16[64,512]{1,0:T(8,128)(2,1)S(1)}, u32[]{:S(2)}, u32[]{:S(2)}) collective-permute-start(bf16[64,512]{1,0:T(8,128)(2,1)S(1)} %shard_map.97.refs_0_), channel_id=1, source_target_pairs={{0,2},{1,3},{2,0},{3,1},{4,6},{5,7},{6,4},{7,5},{8,10},{9,11},{10,... | collective-permute-start | bytes 196616 | tf_op jit(solution)/shard_map/ppermute | solution.py:19
  20.3 0.0 collective-permute-start.8
  20.3 0.0 collective-permute-done.9.refs_6_
  20.3 0.5 %collective-permute-start.10 = (bf16[256,128]{1,0:T(8,128)(2,1)S(1)}, bf16[256,128]{1,0:T(8,128)(2,1)S(1)}, u32[]{:S(2)}, u32[]{:S(2)}) collective-permute-start(bf16[256,128]{1,0:T(8,128)(2,1)S(1)} %collective-permute-done.9.refs_6_), channel_id=1, source_target_pairs={{0,1},{1,0},{2,3},{3,2},{4,5},{5,4},{6,7},{7,6},{8,9},{9,8},{10,11... | collective-permute-start | bytes 196616 | tf_op jit(solution)/shard_map/ppermute | solution.py:19
  20.9 0.0 collective-permute-start.5
  20.9 2.0 %collective-permute-done.6.refs_2_ = bf16[64,512]{1,0:T(8,128)(2,1)S(1)} collective-permute-done((bf16[64,512]{1,0:T(8,128)(2,1)S(1)}, bf16[64,512]{1,0:T(8,128)(2,1)S(1)}, u32[]{:S(2)}, u32[]{:S(2)}) %collective-permute-start.6) | collective-permute-done | bytes 65568 | tf_op jit(solution)/shard_map/ppermute | solution.py:19
  22.9 0.0 collective-permute-start.7
  22.9 0.0 collective-permute-done.8.refs_5_
  22.9 0.0 collective-permute-done.10.refs_7_
  22.9 0.0 collective-permute-done.5.refs_1_
  22.9 1.2 %collective-permute-done.7.refs_3_ = bf16[64,512]{1,0:T(8,128)(2,1)S(1)} collective-permute-done((bf16[64,512]{1,0:T(8,128)(2,1)S(1)}, bf16[64,512]{1,0:T(8,128)(2,1)S(1)}, u32[]{:S(2)}, u32[]{:S(2)}) %collective-permute-start.7) | collective-permute-done | bytes 65568 | tf_op jit(solution)/shard_map/ppermute | solution.py:19
  24.1 0.0 copy-done.1
  24.1 1.0 %shard_map.98 = (bf16[256,128]{1,0:T(8,128)(2,1)S(1)}, bf16[64,512]{1,0:T(8,128)(2,1)S(1)}, bf16[128,256]{1,0:T(8,128)(2,1)S(1)}, bf16[256,512]{1,0:T(8,128)(2,1)S(1)}) custom-call(bf16[32,128,128]{2,1,0:T(8,128)(2,1)S(1)} %get-tuple-element.35.values, bf16[32,4,16,128]{3,2,1,0:T(8,128)(2,1)S(1)} %get-tuple-element.36.row_masks, ...), custom_call_target="tpu_custom_call" | custom-call | tf_op jit(solution)/shard_map/pallas_call | solution.py:53
  25.1 1.7 %collective-permute-start.11 = (bf16[128,256]{1,0:T(8,128)(2,1)S(1)}, bf16[128,256]{1,0:T(8,128)(2,1)S(1)}, u32[]{:S(2)}, u32[]{:S(2)}) collective-permute-start(bf16[128,256]{1,0:T(8,128)(2,1)S(1)} %get-tuple-element.42.one), channel_id=1, source_target_pairs={{0,4},{4,0},{8,12},{12,8},{16,20},{20,16},{24,28},{28,24},{1,5},{5... | collective-permute-start | bytes 196616 | tf_op jit(solution)/shard_map/ppermute | solution.py:19
  26.9 0.3 collective-permute-start.12
  27.2 2.4 %collective-permute-done.11.other = bf16[128,256]{1,0:T(8,128)(2,1)S(1)} collective-permute-done((bf16[128,256]{1,0:T(8,128)(2,1)S(1)}, bf16[128,256]{1,0:T(8,128)(2,1)S(1)}, u32[]{:S(2)}, u32[]{:S(2)}) %collective-permute-start.11) | collective-permute-done | bytes 65568 | tf_op jit(solution)/shard_map/ppermute | solution.py:19
  29.7 3.3 %collective-permute-start.18 = (bf16[128,256]{1,0:T(8,128)(2,1)S(1)}, bf16[128,256]{1,0:T(8,128)(2,1)S(1)}, u32[]{:S(2)}, u32[]{:S(2)}) collective-permute-start(bf16[128,256]{1,0:T(8,128)(2,1)S(1)} %shard_map.99.refs_0_), channel_id=1, source_target_pairs={{0,24},{4,28},{8,16},{12,20},{16,8},{20,12},{24,0},{28,4},{1,25},{... | collective-permute-start | bytes 196616 | tf_op jit(solution)/shard_map/ppermute | solution.py:19
  32.9 0.0 collective-permute-start.17
  32.9 1.2 %collective-permute-start.16 = (bf16[128,256]{1,0:T(8,128)(2,1)S(1)}, bf16[128,256]{1,0:T(8,128)(2,1)S(1)}, u32[]{:S(2)}, u32[]{:S(2)}) collective-permute-start(bf16[128,256]{1,0:T(8,128)(2,1)S(1)} %shard_map.99.refs_0_), channel_id=1, source_target_pairs={{0,8},{4,12},{8,0},{12,4},{16,24},{20,28},{24,16},{28,20},{1,9},{5... | collective-permute-start | bytes 196616 | tf_op jit(solution)/shard_map/ppermute | solution.py:19
  34.1 0.3 shard_map.100.near
  34.4 0.7 %collective-permute-done.12.got = bf16[256,512]{1,0:T(8,128)(2,1)S(1)} collective-permute-done((bf16[256,512]{1,0:T(8,128)(2,1)S(1)}, bf16[256,512]{1,0:T(8,128)(2,1)S(1)}, u32[]{:S(2)}, u32[]{:S(2)}) %collective-permute-start.12) | collective-permute-done | bytes 262176 | tf_op jit(solution)/shard_map/ppermute | solution.py:19
  35.1 0.5 %collective-permute-start.13 = (bf16[64,512]{1,0:T(8,128)(2,1)S(1)}, bf16[64,512]{1,0:T(8,128)(2,1)S(1)}, u32[]{:S(2)}, u32[]{:S(2)}) collective-permute-start(bf16[64,512]{1,0:T(8,128)(2,1)S(1)} %get-tuple-element.46), channel_id=1, source_target_pairs={{0,8},{4,12},{8,0},{12,4},{16,24},{20,28},{24,16},{28,20},{1,9},{5... | collective-permute-start | bytes 196616 | tf_op jit(solution)/shard_map/ppermute | solution.py:19
  35.6 2.7 %collective-permute-start.14 = (bf16[64,512]{1,0:T(8,128)(2,1)S(1)}, bf16[64,512]{1,0:T(8,128)(2,1)S(1)}, u32[]{:S(2)}, u32[]{:S(2)}) collective-permute-start(bf16[64,512]{1,0:T(8,128)(2,1)S(1)} %get-tuple-element.47), channel_id=1, source_target_pairs={{0,16},{4,20},{8,24},{12,28},{16,0},{20,4},{24,8},{28,12},{1,17},{... | collective-permute-start | bytes 196616 | tf_op jit(solution)/shard_map/ppermute | solution.py:19
  38.4 0.0 collective-permute-done.18.refs_3_
  38.4 1.2 %collective-permute-start.15 = (bf16[64,512]{1,0:T(8,128)(2,1)S(1)}, bf16[64,512]{1,0:T(8,128)(2,1)S(1)}, u32[]{:S(2)}, u32[]{:S(2)}) collective-permute-start(bf16[64,512]{1,0:T(8,128)(2,1)S(1)} %get-tuple-element.48), channel_id=1, source_target_pairs={{0,24},{4,28},{8,16},{12,20},{16,8},{20,12},{24,0},{28,4},{1,25},{... | collective-permute-start | bytes 196616 | tf_op jit(solution)/shard_map/ppermute | solution.py:19
  39.6 0.0 collective-permute-done.17.refs_2_
  39.6 0.0 collective-permute-done.16.refs_1_
  39.6 0.6 %collective-permute-done.13.refs_1_ = bf16[64,512]{1,0:T(8,128)(2,1)S(1)} collective-permute-done((bf16[64,512]{1,0:T(8,128)(2,1)S(1)}, bf16[64,512]{1,0:T(8,128)(2,1)S(1)}, u32[]{:S(2)}, u32[]{:S(2)}) %collective-permute-start.13) | collective-permute-done | bytes 65568 | tf_op jit(solution)/shard_map/ppermute | solution.py:19
  40.2 2.6 %collective-permute-done.14.refs_2_ = bf16[64,512]{1,0:T(8,128)(2,1)S(1)} collective-permute-done((bf16[64,512]{1,0:T(8,128)(2,1)S(1)}, bf16[64,512]{1,0:T(8,128)(2,1)S(1)}, u32[]{:S(2)}, u32[]{:S(2)}) %collective-permute-start.14) | collective-permute-done | bytes 65568 | tf_op jit(solution)/shard_map/ppermute | solution.py:19
  42.8 1.7 %collective-permute-done.15.refs_3_ = bf16[64,512]{1,0:T(8,128)(2,1)S(1)} collective-permute-done((bf16[64,512]{1,0:T(8,128)(2,1)S(1)}, bf16[64,512]{1,0:T(8,128)(2,1)S(1)}, u32[]{:S(2)}, u32[]{:S(2)}) %collective-permute-start.15) | collective-permute-done | bytes 65568 | tf_op jit(solution)/shard_map/ppermute | solution.py:19
  44.5 0.1 collective-permute-start.19
  44.6 0.7 %shard_map.104 = f32[64,512]{1,0:T(8,128)} custom-call(f32[64,512]{1,0:T(8,128)S(1)} %get-tuple-element.57.refs_0_, bf16[64,512]{1,0:T(8,128)(2,1)S(1)} %collective-permute-done.13.refs_1_, bf16[64,512]{1,0:T(8,128)(2,1)S(1)} %collective-permute-done.14.refs_2_, bf16[64,512]{1,0:T(8,128)(2,1)S(1)} %collective-permute-done.15.refs_3_), custom_call_target="tpu_custom_call" | custom-call | flops 1024 | bytes 1024 | tf_op jit(solution)/shard_map/pallas_call | solution.py:53
  45.3 0.6 %collective-permute-done.19.other = f32[128,256]{1,0:T(8,128)S(1)} collective-permute-done((f32[128,256]{1,0:T(8,128)S(1)}, f32[128,256]{1,0:T(8,128)S(1)}, u32[]{:S(2)}, u32[]{:S(2)}) %collective-permute-start.19) | collective-permute-done | bytes 131104 | tf_op jit(solution)/shard_map/ppermute | solution.py:19
  45.9 0.7 %shard_map.103 = (f32[256,256]{1,0:T(8,128)}, bf16[256,128]{1,0:T(8,128)(2,1)}) custom-call(f32[128,256]{1,0:T(8,128)S(1)} %shard_map.102.mine, f32[128,256]{1,0:T(8,128)S(1)} %collective-permute-done.19.other, bf16[256,128]{1,0:T(8,128)(2,1)S(1)} %get-tuple-element.54.activated), custom_call_target="tpu_custom_call" | custom-call | flops 1024 | bytes 1024 | tf_op jit(solution)/shard_map/pallas_call | solution.py:53
  (4 shorter events, 0.1 us)
Async XLA Ops:
  0.6 7.4 %copy-start.4 = (s32[8,4]{0,1:T(4,128)S(1)}, s32[8,4]{0,1:T(4,128)}, u32[]{:S(2)}) copy-start(s32[8,4]{0,1:T(4,128)} %param.9) | copy-start | bytes 388
  0.6 10.8 %collective-permute-start.2 = (bf16[64,512]{1,0:T(8,128)(2,1)}, bf16[64,512]{1,0:T(8,128)(2,1)S(1)}, u32[]{:S(2)}, u32[]{:S(2)}) collective-permute-start(bf16[64,512]{1,0:T(8,128)(2,1)} %first.1), channel_id=1, source_target_pairs={{0,24},{4,28},{8,16},{12,20},{16,8},{20,12},{24,0},{28,4},{1,25},{... | collective-permute-start | bytes 196616 | tf_op jit(solution)/shard_map/ppermute | solution.py:19
  5.8 5.8 %collective-permute-start.1 = (bf16[64,512]{1,0:T(8,128)(2,1)}, bf16[64,512]{1,0:T(8,128)(2,1)S(1)}, u32[]{:S(2)}, u32[]{:S(2)}) collective-permute-start(bf16[64,512]{1,0:T(8,128)(2,1)} %first.1), channel_id=1, source_target_pairs={{0,16},{4,20},{8,24},{12,28},{16,0},{20,4},{24,8},{28,12},{1,17},{... | collective-permute-start | bytes 196616 | tf_op jit(solution)/shard_map/ppermute | solution.py:19
  5.8 5.8 %collective-permute-start = (bf16[64,512]{1,0:T(8,128)(2,1)}, bf16[64,512]{1,0:T(8,128)(2,1)S(1)}, u32[]{:S(2)}, u32[]{:S(2)}) collective-permute-start(bf16[64,512]{1,0:T(8,128)(2,1)} %first.1), channel_id=1, source_target_pairs={{0,8},{4,12},{8,0},{12,4},{16,24},{20,28},{24,16},{28,20},{1,9},{5... | collective-permute-start | bytes 196616 | tf_op jit(solution)/shard_map/ppermute | solution.py:19
  6.4 5.2 %collective-permute-start.3 = (bf16[64,512]{1,0:T(8,128)(2,1)}, bf16[64,512]{1,0:T(8,128)(2,1)S(1)}, u32[]{:S(2)}, u32[]{:S(2)}) collective-permute-start(bf16[64,512]{1,0:T(8,128)(2,1)} %first.1), channel_id=1, source_target_pairs={{0,4},{4,0},{8,12},{12,8},{16,20},{20,16},{24,28},{28,24},{1,5},{5... | collective-permute-start | bytes 196616 | tf_op jit(solution)/shard_map/ppermute | solution.py:19
  8.0 0.7 %copy-start.6 = (s32[8]{0:T(128)S(1)}, s32[8]{0:T(128)}, u32[]{:S(2)}) copy-start(s32[8]{0:T(128)} %counts.1) | copy-start | bytes 100
  8.7 1.2 %copy-start = (bf16[32,128,128]{2,1,0:T(8,128)(2,1)S(1)}, bf16[32,128,128]{2,1,0:T(8,128)(2,1)}, u32[]{:S(2)}) copy-start(bf16[32,128,128]{2,1,0:T(8,128)(2,1)} %source.1) | copy-start | bytes 3145732
  9.9 0.7 %copy-start.5 = (s32[8,4]{0,1:T(4,128)S(1)}, s32[8,4]{0,1:T(4,128)}, u32[]{:S(2)}) copy-start(s32[8,4]{0,1:T(4,128)} %param.10) | copy-start | bytes 388
  11.6 1.6 %copy-start.3 = (bf16[256,128]{1,0:T(8,128)(2,1)S(1)}, bf16[256,128]{1,0:T(8,128)(2,1)}, u32[]{:S(2)}) copy-start(bf16[256,128]{1,0:T(8,128)(2,1)} %refs_4_.1) | copy-start | bytes 196612
  11.6 3.1 %copy-start.2 = (bf16[64,512]{1,0:T(8,128)(2,1)S(1)}, bf16[64,512]{1,0:T(8,128)(2,1)}, u32[]{:S(2)}) copy-start(bf16[64,512]{1,0:T(8,128)(2,1)} %first.1) | copy-start | bytes 196612
  11.6 6.5 %collective-permute-start.4 = (bf16[3,64,512]{2,1,0:T(8,128)(2,1)S(1)}, bf16[3,64,512]{2,1,0:T(8,128)(2,1)S(1)}, u32[]{:S(2)}, u32[]{:S(2)}) collective-permute-start(bf16[3,64,512]{2,1,0:T(8,128)(2,1)S(1)} %shard_map.95.rest), channel_id=1, source_target_pairs={{0,4},{4,0},{8,12},{12,8},{16,20},{20,16},{24,28},{28,24},{1,5},{5... | collective-permute-start | bytes 589832 | tf_op jit(solution)/shard_map/ppermute | solution.py:19
  13.2 7.2 %collective-permute-start.9 = (bf16[256,128]{1,0:T(8,128)(2,1)S(1)}, bf16[256,128]{1,0:T(8,128)(2,1)S(1)}, u32[]{:S(2)}, u32[]{:S(2)}) collective-permute-start(bf16[256,128]{1,0:T(8,128)(2,1)S(1)} %copy-done.3), channel_id=1, source_target_pairs={{0,2},{1,3},{2,0},{3,1},{4,6},{5,7},{6,4},{7,5},{8,10},{9,11},{10,... | collective-permute-start | bytes 196616 | tf_op jit(solution)/shard_map/ppermute | solution.py:19
  15.3 8.9 %copy-start.1 = (bf16[256,256]{1,0:T(8,128)(2,1)S(1)}, bf16[256,256]{1,0:T(8,128)(2,1)}, u32[]{:S(2)}) copy-start(bf16[256,256]{1,0:T(8,128)(2,1)} %weight.1) | copy-start | bytes 393220
  18.6 4.3 %collective-permute-start.6 = (bf16[64,512]{1,0:T(8,128)(2,1)S(1)}, bf16[64,512]{1,0:T(8,128)(2,1)S(1)}, u32[]{:S(2)}, u32[]{:S(2)}) collective-permute-start(bf16[64,512]{1,0:T(8,128)(2,1)S(1)} %shard_map.97.refs_0_), channel_id=1, source_target_pairs={{0,2},{1,3},{2,0},{3,1},{4,6},{5,7},{6,4},{7,5},{8,10},{9,11},{10,... | collective-permute-start | bytes 196616 | tf_op jit(solution)/shard_map/ppermute | solution.py:19
  20.3 2.6 %collective-permute-start.8 = (bf16[256,128]{1,0:T(8,128)(2,1)S(1)}, bf16[256,128]{1,0:T(8,128)(2,1)S(1)}, u32[]{:S(2)}, u32[]{:S(2)}) collective-permute-start(bf16[256,128]{1,0:T(8,128)(2,1)S(1)} %copy-done.3), channel_id=1, source_target_pairs={{0,1},{1,0},{2,3},{3,2},{4,5},{5,4},{6,7},{7,6},{8,9},{9,8},{10,11... | collective-permute-start | bytes 196616 | tf_op jit(solution)/shard_map/ppermute | solution.py:19
  20.3 2.6 %collective-permute-start.10 = (bf16[256,128]{1,0:T(8,128)(2,1)S(1)}, bf16[256,128]{1,0:T(8,128)(2,1)S(1)}, u32[]{:S(2)}, u32[]{:S(2)}) collective-permute-start(bf16[256,128]{1,0:T(8,128)(2,1)S(1)} %collective-permute-done.9.refs_6_), channel_id=1, source_target_pairs={{0,1},{1,0},{2,3},{3,2},{4,5},{5,4},{6,7},{7,6},{8,9},{9,8},{10,11... | collective-permute-start | bytes 196616 | tf_op jit(solution)/shard_map/ppermute | solution.py:19
  20.9 2.1 %collective-permute-start.5 = (bf16[64,512]{1,0:T(8,128)(2,1)S(1)}, bf16[64,512]{1,0:T(8,128)(2,1)S(1)}, u32[]{:S(2)}, u32[]{:S(2)}) collective-permute-start(bf16[64,512]{1,0:T(8,128)(2,1)S(1)} %shard_map.97.refs_0_), channel_id=1, source_target_pairs={{0,1},{1,0},{2,3},{3,2},{4,5},{5,4},{6,7},{7,6},{8,9},{9,8},{10,11... | collective-permute-start | bytes 196616 | tf_op jit(solution)/shard_map/ppermute | solution.py:19
  22.9 1.3 %collective-permute-start.7 = (bf16[64,512]{1,0:T(8,128)(2,1)S(1)}, bf16[64,512]{1,0:T(8,128)(2,1)S(1)}, u32[]{:S(2)}, u32[]{:S(2)}) collective-permute-start(bf16[64,512]{1,0:T(8,128)(2,1)S(1)} %collective-permute-done.6.refs_2_), channel_id=1, source_target_pairs={{0,1},{1,0},{2,3},{3,2},{4,5},{5,4},{6,7},{7,6},{8,9},{9,8},{10,11... | collective-permute-start | bytes 196616 | tf_op jit(solution)/shard_map/ppermute | solution.py:19
  25.1 4.5 %collective-permute-start.11 = (bf16[128,256]{1,0:T(8,128)(2,1)S(1)}, bf16[128,256]{1,0:T(8,128)(2,1)S(1)}, u32[]{:S(2)}, u32[]{:S(2)}) collective-permute-start(bf16[128,256]{1,0:T(8,128)(2,1)S(1)} %get-tuple-element.42.one), channel_id=1, source_target_pairs={{0,4},{4,0},{8,12},{12,8},{16,20},{20,16},{24,28},{28,24},{1,5},{5... | collective-permute-start | bytes 196616 | tf_op jit(solution)/shard_map/ppermute | solution.py:19
  26.9 8.2 %collective-permute-start.12 = (bf16[256,512]{1,0:T(8,128)(2,1)S(1)}, bf16[256,512]{1,0:T(8,128)(2,1)S(1)}, u32[]{:S(2)}, u32[]{:S(2)}) collective-permute-start(bf16[256,512]{1,0:T(8,128)(2,1)S(1)} %get-tuple-element.45), channel_id=1, source_target_pairs={{0,4},{4,0},{8,12},{12,8},{16,20},{20,16},{24,28},{28,24},{1,5},{5... | collective-permute-start | bytes 786440 | tf_op jit(solution)/shard_map/ppermute | solution.py:19
  29.7 8.7 %collective-permute-start.18 = (bf16[128,256]{1,0:T(8,128)(2,1)S(1)}, bf16[128,256]{1,0:T(8,128)(2,1)S(1)}, u32[]{:S(2)}, u32[]{:S(2)}) collective-permute-start(bf16[128,256]{1,0:T(8,128)(2,1)S(1)} %shard_map.99.refs_0_), channel_id=1, source_target_pairs={{0,24},{4,28},{8,16},{12,20},{16,8},{20,12},{24,0},{28,4},{1,25},{... | collective-permute-start | bytes 196616 | tf_op jit(solution)/shard_map/ppermute | solution.py:19
  32.9 6.7 %collective-permute-start.17 = (bf16[128,256]{1,0:T(8,128)(2,1)S(1)}, bf16[128,256]{1,0:T(8,128)(2,1)S(1)}, u32[]{:S(2)}, u32[]{:S(2)}) collective-permute-start(bf16[128,256]{1,0:T(8,128)(2,1)S(1)} %shard_map.99.refs_0_), channel_id=1, source_target_pairs={{0,16},{4,20},{8,24},{12,28},{16,0},{20,4},{24,8},{28,12},{1,17},{... | collective-permute-start | bytes 196616 | tf_op jit(solution)/shard_map/ppermute | solution.py:19
  32.9 6.7 %collective-permute-start.16 = (bf16[128,256]{1,0:T(8,128)(2,1)S(1)}, bf16[128,256]{1,0:T(8,128)(2,1)S(1)}, u32[]{:S(2)}, u32[]{:S(2)}) collective-permute-start(bf16[128,256]{1,0:T(8,128)(2,1)S(1)} %shard_map.99.refs_0_), channel_id=1, source_target_pairs={{0,8},{4,12},{8,0},{12,4},{16,24},{20,28},{24,16},{28,20},{1,9},{5... | collective-permute-start | bytes 196616 | tf_op jit(solution)/shard_map/ppermute | solution.py:19
  35.1 5.0 %collective-permute-start.13 = (bf16[64,512]{1,0:T(8,128)(2,1)S(1)}, bf16[64,512]{1,0:T(8,128)(2,1)S(1)}, u32[]{:S(2)}, u32[]{:S(2)}) collective-permute-start(bf16[64,512]{1,0:T(8,128)(2,1)S(1)} %get-tuple-element.46), channel_id=1, source_target_pairs={{0,8},{4,12},{8,0},{12,4},{16,24},{20,28},{24,16},{28,20},{1,9},{5... | collective-permute-start | bytes 196616 | tf_op jit(solution)/shard_map/ppermute | solution.py:19
  35.6 7.2 %collective-permute-start.14 = (bf16[64,512]{1,0:T(8,128)(2,1)S(1)}, bf16[64,512]{1,0:T(8,128)(2,1)S(1)}, u32[]{:S(2)}, u32[]{:S(2)}) collective-permute-start(bf16[64,512]{1,0:T(8,128)(2,1)S(1)} %get-tuple-element.47), channel_id=1, source_target_pairs={{0,16},{4,20},{8,24},{12,28},{16,0},{20,4},{24,8},{28,12},{1,17},{... | collective-permute-start | bytes 196616 | tf_op jit(solution)/shard_map/ppermute | solution.py:19
  38.4 6.1 %collective-permute-start.15 = (bf16[64,512]{1,0:T(8,128)(2,1)S(1)}, bf16[64,512]{1,0:T(8,128)(2,1)S(1)}, u32[]{:S(2)}, u32[]{:S(2)}) collective-permute-start(bf16[64,512]{1,0:T(8,128)(2,1)S(1)} %get-tuple-element.48), channel_id=1, source_target_pairs={{0,24},{4,28},{8,16},{12,20},{16,8},{20,12},{24,0},{28,4},{1,25},{... | collective-permute-start | bytes 196616 | tf_op jit(solution)/shard_map/ppermute | solution.py:19
  44.5 1.4 %collective-permute-start.19 = (f32[128,256]{1,0:T(8,128)S(1)}, f32[128,256]{1,0:T(8,128)S(1)}, u32[]{:S(2)}, u32[]{:S(2)}) collective-permute-start(f32[128,256]{1,0:T(8,128)S(1)} %shard_map.102.mine), channel_id=1, source_target_pairs={{0,1},{1,0},{2,3},{3,2},{4,5},{5,4},{6,7},{7,6},{8,9},{9,8},{10,11... | collective-permute-start | bytes 393224 | tf_op jit(solution)/shard_map/ppermute | solution.py:19

commit v5 on v4

--- a/solution.py
+++ b/solution.py
@@ -155,7 +155,7 @@
 
 def middle(values, row_masks, col_masks, weight, *refs, feat):
     aggs, cots = refs[:feat], refs[feat : 2 * feat]
-    activated, grads, weight_part, sent, agg_full, dpre_full = refs[2 * feat :]
+    activated, grads, mine, dpre_full, sent, agg_full = refs[2 * feat :]
     index = lax.axis_index("feat")
     width, local = aggs[0].shape
     side = cots[0].shape[1]
@@ -171,12 +171,12 @@
         dpre_full[:, at] = dpre.astype(BF16)
     dpre_all = dpre_full[...]
     grads[...] = dot(weight[lanes(index, width), :], dpre_all, ((1,), (0,))).astype(BF16)
-    mine = agg_full[lanes(index & 1, weight_part.shape[0]), :]
-    weight_part[...] = dot(mine, dpre_all, ((1,), (1,))).astype(BF16)
+    mine[...] = agg_full[lanes(index & 1, mine.shape[0]), :]
     add_backward(values, row_masks, col_masks, grads, sent, 1)
 
 
-def backward_near(values, row_masks, col_masks, grads, out):
+def backward_near(values, row_masks, col_masks, grads, mine, dpre, out, weight_part):
+    weight_part[...] = dot(mine[...], dpre[...], ((1,), (1,))).astype(BF16)
     add_backward(values, row_masks, col_masks, grads, out, 0)
 
 
@@ -185,14 +185,7 @@
 
 
 def sum_weights(*refs):
-    refs[-1][...] = tree_sum([r[...].astype(F32) for r in refs[:-1]])
-
-
-def lay_out(mine, other, activated, out, activated_out):
-    activated_out[...] = activated[...]
-    core = lax.axis_index("feat") & 1
-    out[lanes(core, mine.shape[0]), :] = mine[...]
-    out[lanes(core ^ 1, mine.shape[0]), :] = other[...]
+    refs[-1][...] = tree_sum([r[...].astype(F32) for r in refs[:-1]]).astype(refs[-1].dtype)
 
 
 def add_pair(near, got, own, *sent):
@@ -203,8 +196,16 @@
         out[...] = (near[rows] + got[rows].astype(F32)).astype(BF16)
 
 
+def finish(activated, mine, other, column_sum, activated_out, weight_out, gradient):
+    activated_out[...] = activated[...]
+    core = lax.axis_index("feat") & 1
+    weight_out[lanes(core, mine.shape[0]), :] = mine[...]
+    weight_out[lanes(core ^ 1, mine.shape[0]), :] = other[...]
+    gradient[...] = column_sum[...]
+
+
 def add_column(*refs):
-    refs[-1][...] = tree_sum([r[...].astype(F32) for r in refs[:-1]])
+    refs[-1][...] = sum(r[...].astype(F32) for r in refs[:-1])
 
 
 def per_device(features, tile_values, tile_rows, tile_cols, tile_counts, weight, cotangent):
@@ -222,7 +223,10 @@
     masks = shape((tile_values.shape[0], local // side, 16, side), BF16)
     tiles = call(
         prepare,
-        [tile_rows.T, tile_cols.T, tile_counts, tile_values],
+        [
+            pltpu.with_memory_space_constraint(x, pltpu.HBM)
+            for x in (tile_rows.T, tile_cols.T, tile_counts, tile_values)
+        ],
         [shape(tile_values.shape, BF16), masks, masks],
         [pltpu.SemaphoreType.DMA],
         spec=pl.BlockSpec(memory_space=pltpu.HBM),
@@ -242,30 +246,26 @@
         [pltpu.VMEM(totals, F32)],
     )
     aggs = gather_feat(aggregated)
-    activated, grads, weight_part, sent = call(
+    activated, grads, mine, dpre, sent = call(
         functools.partial(middle, feat=feat),
         [*tiles, weight, *aggs, *cots],
         [
             shape((wide, side), BF16),
             shape((width, local), BF16),
-            shape((wide // 2, wide), BF16),
+            shape((wide // 2, local), BF16),
+            shape((wide, local), BF16),
             shape((column * width, local), BF16),
         ],
-        [pltpu.VMEM((wide, local), BF16), pltpu.VMEM((wide, local), BF16)],
-    )
-    other_part = swapped(weight_part, "node", 1)
+        [pltpu.VMEM((wide, local), BF16)],
+    )
     got = swapped(sent, "node", 1)
-    (pair,) = call(
-        add_weights, [weight_part, other_part], [shape((wide // 2, wide), BF16)], cost=SMALL
-    )
-    pair, grads = lax.optimization_barrier((pair, grads))
-    (near_grads,) = call(
+    near_grads, weight_part = call(
         backward_near,
-        [*tiles, grads],
-        [shape((column * width, local), F32)],
+        [*tiles, grads, mine, dpre],
+        [shape((column * width, local), F32), shape((wide // 2, wide), BF16)],
         cost=LARGE,
     )
-    pairs = [pair] + [swapped(pair, "node", 2 * k) for k in range(1, column)]
+    parts = [weight_part] + [swapped(weight_part, "node", 2 * k) for k in range(1, column)]
     own, *chunks = call(
         add_pair,
         [near_grads, got],
@@ -273,18 +273,23 @@
         cost=SMALL,
     )
     arrived = [swapped(c, "node", 2 * k) for k, c in enumerate(chunks, 1)]
-    count = len(arrived)
-    held = lax.optimization_barrier((*arrived, *pairs))
-    arrived, pairs = held[:count], held[count:]
-    (half,) = call(sum_weights, pairs, [shape((wide // 2, wide), F32)], cost=SMALL)
+    *parts, _ = lax.optimization_barrier((*parts, chunks[0]))
+    (part,) = call(sum_weights, parts, [shape((wide // 2, wide), BF16)], cost=SMALL)
+    other = swapped(part, "node", 1)
+    (column_sum,) = call(
+        add_column, [own, *arrived], [shape((width, local), F32)], cost=LARGE
+    )
+    other, column_sum = lax.optimization_barrier((other, column_sum))
+    (half,) = call(sum_weights, [part, other], [shape((wide // 2, wide), F32)], cost=SMALL)
     other_half = swapped(half, "feat", 1)
-    (gradient,) = call(
-        add_column, [own, *arrived], [shape((width, local), F32)], cost=SMALL
-    )
-    grad_weight, activated = call(
-        lay_out,
-        [half, other_half, activated],
-        [shape((wide, wide), F32), shape((wide, side), BF16)],
+    activated, grad_weight, gradient = call(
+        finish,
+        [activated, half, other_half, column_sum],
+        [
+            shape((wide, side), BF16),
+            shape((wide, wide), F32),
+            shape((width, local), F32),
+        ],
         cost=SMALL,
     )
     return (activated, grad_weight, gradient)

time: 46.8 us -> 44.2 us (0.944)
  local copies, waits for them, and re-layouts: 2.58 us -> 0.02 us
  waiting for transfers between devices: 14.9 us -> 13.7 us
  Pallas kernels: 4.6 us -> 5.18 us
  starting transfers between devices: 23.8 us -> 24.3 us
    unnamed x14 -> x6, local copies, waits for them, and re-layouts: 2.58 us -> 0.02 us
    ppermute x20, waiting for transfers between devices: 14.9 us -> 13.7 us  [swapped(): lax.ppermute(x, axis, [(i, i ^ mask) for i in range(lax.axis_size(axis))])]
    pallas_call x11, Pallas kernels: 4.6 us -> 5.18 us  [call(): pl.pallas_call(body, in_specs=[SMEM] * scalars + [spec] * (len(inputs) -...]
    ppermute x20, starting transfers between devices: 23.8 us -> 24.3 us  [swapped(): lax.ppermute(x, axis, [(i, i ^ mask) for i in range(lax.axis_size(axis))])]
  transfers between devices with their start and end apart: 20 -> 20, of which waited for: 10 -> 8; matrix products, arithmetic and copies ran while one was open for 0% -> 0% of each run, Pallas kernels for 6% -> 8%
where the time goes in v5:
time: 44.2 us; the launch traced here: 44 us
  starting transfers between devices  24.3 us (55%)
  waiting for transfers between devices  13.7 us (31%)
  Pallas kernels  5.18 us (12%)
  between operations  0.77 us (2%)
    ppermute x20, starting transfers between devices, swapped(): lax.ppermute(x, axis, [(i, i ^ mask) for i in range(lax.axis_size(axis))])  24.3 us
    ppermute x20, waiting for transfers between devices, swapped(): lax.ppermute(x, axis, [(i, i ^ mask) for i in range(lax.axis_size(axis))])  13.7 us
    pallas_call x11, Pallas kernels, call(): pl.pallas_call(body, in_specs=[SMEM] * scalars + [spec] * (len(inputs) -...  5.18 us
  transfers between devices with their start and end apart: 20, of which 8 were waited for; matrix products, arithmetic and copies ran while one was open for 0% of the time, Pallas kernels for 8%

profile of v5, /device:TPU:0, one launch (start us, length us, event | category | flops | bytes accessed | tf_op | source)
XLA Modules:
  0.0 44.0 jit_solution(13509341832532862393)
XLA Ops:
  0.6 5.1 %collective-permute-start.2 = (bf16[64,512]{1,0:T(8,128)(2,1)}, bf16[64,512]{1,0:T(8,128)(2,1)S(1)}, u32[]{:S(2)}, u32[]{:S(2)}) collective-permute-start(bf16[64,512]{1,0:T(8,128)(2,1)} %first.1), channel_id=1, source_target_pairs={{0,24},{4,28},{8,16},{12,20},{16,8},{20,12},{24,0},{28,4},{1,25},{... | collective-permute-start | bytes 196616 | tf_op jit(solution)/shard_map/ppermute | solution.py:19
  5.7 0.0 collective-permute-start.1
  5.7 0.6 %collective-permute-start = (bf16[64,512]{1,0:T(8,128)(2,1)}, bf16[64,512]{1,0:T(8,128)(2,1)S(1)}, u32[]{:S(2)}, u32[]{:S(2)}) collective-permute-start(bf16[64,512]{1,0:T(8,128)(2,1)} %first.1), channel_id=1, source_target_pairs={{0,8},{4,12},{8,0},{12,4},{16,24},{20,28},{24,16},{28,20},{1,9},{5... | collective-permute-start | bytes 196616 | tf_op jit(solution)/shard_map/ppermute | solution.py:19
  6.4 1.6 %collective-permute-start.3 = (bf16[64,512]{1,0:T(8,128)(2,1)}, bf16[64,512]{1,0:T(8,128)(2,1)S(1)}, u32[]{:S(2)}, u32[]{:S(2)}) collective-permute-start(bf16[64,512]{1,0:T(8,128)(2,1)} %first.1), channel_id=1, source_target_pairs={{0,4},{4,0},{8,12},{12,8},{16,20},{20,16},{24,28},{28,24},{1,5},{5... | collective-permute-start | bytes 196616 | tf_op jit(solution)/shard_map/ppermute | solution.py:19
  8.0 2.0 %shard_map.94 = (bf16[32,128,128]{2,1,0:T(8,128)(2,1)S(1)}, bf16[32,4,16,128]{3,2,1,0:T(8,128)(2,1)S(1)}, bf16[32,4,16,128]{3,2,1,0:T(8,128)(2,1)S(1)}) custom-call(s32[4,8]{1,0:T(4,128)} %bitcast.2, s32[4,8]{1,0:T(4,128)} %bitcast.3, s32[8]{0:T(128)} %counts.1, bf16[32,128,128]{2,1,0:T(8,128)(2,1)} %source.1), custom_call_target="tpu_custom_call" | custom-call | tf_op jit(solution)/shard_map/pallas_call | solution.py:53
  10.0 0.0 collective-permute-done.2.refs_2_
  10.0 1.6 %collective-permute-done.1.refs_1_ = bf16[64,512]{1,0:T(8,128)(2,1)S(1)} collective-permute-done((bf16[64,512]{1,0:T(8,128)(2,1)}, bf16[64,512]{1,0:T(8,128)(2,1)S(1)}, u32[]{:S(2)}, u32[]{:S(2)}) %collective-permute-start.1) | collective-permute-done | bytes 65568 | tf_op jit(solution)/shard_map/ppermute | solution.py:19
  11.6 0.0 collective-permute-done.refs_0_
  11.6 0.0 collective-permute-done.3.across
  11.6 0.0 copy-start.2
  11.6 0.0 copy-start.1
  11.6 1.6 %collective-permute-start.4 = (bf16[3,64,512]{2,1,0:T(8,128)(2,1)S(1)}, bf16[3,64,512]{2,1,0:T(8,128)(2,1)S(1)}, u32[]{:S(2)}, u32[]{:S(2)}) collective-permute-start(bf16[3,64,512]{2,1,0:T(8,128)(2,1)S(1)} %shard_map.95.rest), channel_id=1, source_target_pairs={{0,4},{4,0},{8,12},{12,8},{16,20},{20,16},{24,28},{28,24},{1,5},{5... | collective-permute-start | bytes 589832 | tf_op jit(solution)/shard_map/ppermute | solution.py:19
  13.2 0.0 copy-done.2
  13.2 1.5 %collective-permute-start.9 = (bf16[256,128]{1,0:T(8,128)(2,1)S(1)}, bf16[256,128]{1,0:T(8,128)(2,1)S(1)}, u32[]{:S(2)}, u32[]{:S(2)}) collective-permute-start(bf16[256,128]{1,0:T(8,128)(2,1)S(1)} %copy-done.2), channel_id=1, source_target_pairs={{0,2},{1,3},{2,0},{3,1},{4,6},{5,7},{6,4},{7,5},{8,10},{9,11},{10,... | collective-permute-start | bytes 196616 | tf_op jit(solution)/shard_map/ppermute | solution.py:19
  14.7 0.0 copy-done.1
  14.7 0.6 %shard_map.96.near = f32[4,64,128]{2,1,0:T(8,128)S(1)} custom-call(bf16[32,128,128]{2,1,0:T(8,128)(2,1)S(1)} %get-tuple-element.33.values, bf16[32,4,16,128]{3,2,1,0:T(8,128)(2,1)S(1)} %get-tuple-element.34.row_masks, bf16[32,4,16,128]{3,2,1,0:T(8,128)(2,1)S(1)} %get-tuple-element.35.col_masks, bf16[64,512]{1,0:T(8,128)(2,1)S(1)} %copy-done.1, ...), custom_call_target="tpu_custom_call" | custom-call | tf_op jit(solution)/shard_map/pallas_call | solution.py:53
  15.3 0.0 copy-start
  15.3 2.8 %collective-permute-done.4.rest = bf16[3,64,512]{2,1,0:T(8,128)(2,1)S(1)} collective-permute-done((bf16[3,64,512]{2,1,0:T(8,128)(2,1)S(1)}, bf16[3,64,512]{2,1,0:T(8,128)(2,1)S(1)}, u32[]{:S(2)}, u32[]{:S(2)}) %collective-permute-start.4) | collective-permute-done | bytes 196640 | tf_op jit(solution)/shard_map/ppermute | solution.py:19
  18.1 0.4 shard_map.97.refs_0_
  18.6 1.8 %collective-permute-start.6 = (bf16[64,512]{1,0:T(8,128)(2,1)S(1)}, bf16[64,512]{1,0:T(8,128)(2,1)S(1)}, u32[]{:S(2)}, u32[]{:S(2)}) collective-permute-start(bf16[64,512]{1,0:T(8,128)(2,1)S(1)} %shard_map.97.refs_0_), channel_id=1, source_target_pairs={{0,2},{1,3},{2,0},{3,1},{4,6},{5,7},{6,4},{7,5},{8,10},{9,11},{10,... | collective-permute-start | bytes 196616 | tf_op jit(solution)/shard_map/ppermute | solution.py:19
  20.3 0.0 collective-permute-start.8
  20.3 0.0 collective-permute-done.9.refs_6_
  20.3 0.5 %collective-permute-start.10 = (bf16[256,128]{1,0:T(8,128)(2,1)S(1)}, bf16[256,128]{1,0:T(8,128)(2,1)S(1)}, u32[]{:S(2)}, u32[]{:S(2)}) collective-permute-start(bf16[256,128]{1,0:T(8,128)(2,1)S(1)} %collective-permute-done.9.refs_6_), channel_id=1, source_target_pairs={{0,1},{1,0},{2,3},{3,2},{4,5},{5,4},{6,7},{7,6},{8,9},{9,8},{10,11... | collective-permute-start | bytes 196616 | tf_op jit(solution)/shard_map/ppermute | solution.py:19
  20.8 0.0 collective-permute-start.5
  20.8 2.0 %collective-permute-done.6.refs_2_ = bf16[64,512]{1,0:T(8,128)(2,1)S(1)} collective-permute-done((bf16[64,512]{1,0:T(8,128)(2,1)S(1)}, bf16[64,512]{1,0:T(8,128)(2,1)S(1)}, u32[]{:S(2)}, u32[]{:S(2)}) %collective-permute-start.6) | collective-permute-done | bytes 65568 | tf_op jit(solution)/shard_map/ppermute | solution.py:19
  22.9 0.0 collective-permute-start.7
  22.9 0.0 collective-permute-done.8.refs_5_
  22.9 0.0 collective-permute-done.10.refs_7_
  22.9 0.0 collective-permute-done.5.refs_1_
  22.9 1.2 %collective-permute-done.7.refs_3_ = bf16[64,512]{1,0:T(8,128)(2,1)S(1)} collective-permute-done((bf16[64,512]{1,0:T(8,128)(2,1)S(1)}, bf16[64,512]{1,0:T(8,128)(2,1)S(1)}, u32[]{:S(2)}, u32[]{:S(2)}) %collective-permute-start.7) | collective-permute-done | bytes 65568 | tf_op jit(solution)/shard_map/ppermute | solution.py:19
  24.1 0.0 copy-done
  24.1 0.9 %shard_map.98 = (bf16[256,128]{1,0:T(8,128)(2,1)S(1)}, bf16[64,512]{1,0:T(8,128)(2,1)S(1)}, bf16[128,512]{1,0:T(8,128)(2,1)S(1)}, bf16[256,512]{1,0:T(8,128)(2,1)S(1)}, bf16[256,512]{1,0:T(8,128)(2,1)S(1)}) custom-call(bf16[32,128,128]{2,1,0:T(8,128)(2,1)S(1)} %get-tuple-element.33.values, bf16[32,4,16,128]{3,2,1,0:T(8,128)(2,1)S(1)} %get-tuple-element.34.row_masks, ...), custom_call_target="tpu_custom_call" | custom-call | tf_op jit(solution)/shard_map/pallas_call | solution.py:53
  25.1 1.7 %collective-permute-start.14 = (bf16[256,512]{1,0:T(8,128)(2,1)S(1)}, bf16[256,512]{1,0:T(8,128)(2,1)S(1)}, u32[]{:S(2)}, u32[]{:S(2)}) collective-permute-start(bf16[256,512]{1,0:T(8,128)(2,1)S(1)} %get-tuple-element.46), channel_id=1, source_target_pairs={{0,4},{4,0},{8,12},{12,8},{16,20},{20,16},{24,28},{28,24},{1,5},{5... | collective-permute-start | bytes 786440 | tf_op jit(solution)/shard_map/ppermute | solution.py:19
  26.8 0.4 shard_map.99
  27.2 2.1 %collective-permute-start.13 = (bf16[128,256]{1,0:T(8,128)(2,1)S(1)}, bf16[128,256]{1,0:T(8,128)(2,1)S(1)}, u32[]{:S(2)}, u32[]{:S(2)}) collective-permute-start(bf16[128,256]{1,0:T(8,128)(2,1)S(1)} %get-tuple-element.48.refs_0_), channel_id=1, source_target_pairs={{0,24},{4,28},{8,16},{12,20},{16,8},{20,12},{24,0},{28,4},{1,25},{... | collective-permute-start | bytes 196616 | tf_op jit(solution)/shard_map/ppermute | solution.py:19
  29.3 0.0 collective-permute-start.12
  29.3 2.3 %collective-permute-start.11 = (bf16[128,256]{1,0:T(8,128)(2,1)S(1)}, bf16[128,256]{1,0:T(8,128)(2,1)S(1)}, u32[]{:S(2)}, u32[]{:S(2)}) collective-permute-start(bf16[128,256]{1,0:T(8,128)(2,1)S(1)} %get-tuple-element.48.refs_0_), channel_id=1, source_target_pairs={{0,8},{4,12},{8,0},{12,4},{16,24},{20,28},{24,16},{28,20},{1,9},{5... | collective-permute-start | bytes 196616 | tf_op jit(solution)/shard_map/ppermute | solution.py:19
  31.6 1.9 %collective-permute-done.14.got = bf16[256,512]{1,0:T(8,128)(2,1)S(1)} collective-permute-done((bf16[256,512]{1,0:T(8,128)(2,1)S(1)}, bf16[256,512]{1,0:T(8,128)(2,1)S(1)}, u32[]{:S(2)}, u32[]{:S(2)}) %collective-permute-start.14) | collective-permute-done | bytes 262176 | tf_op jit(solution)/shard_map/ppermute | solution.py:19
  33.5 0.8 %collective-permute-start.17 = (bf16[64,512]{1,0:T(8,128)(2,1)S(1)}, bf16[64,512]{1,0:T(8,128)(2,1)S(1)}, u32[]{:S(2)}, u32[]{:S(2)}) collective-permute-start(bf16[64,512]{1,0:T(8,128)(2,1)S(1)} %get-tuple-element.53), channel_id=1, source_target_pairs={{0,16},{4,20},{8,24},{12,28},{16,0},{20,4},{24,8},{28,12},{1,17},{... | collective-permute-start | bytes 196616 | tf_op jit(solution)/shard_map/ppermute | solution.py:19
  34.4 1.9 %collective-permute-start.18 = (bf16[64,512]{1,0:T(8,128)(2,1)S(1)}, bf16[64,512]{1,0:T(8,128)(2,1)S(1)}, u32[]{:S(2)}, u32[]{:S(2)}) collective-permute-start(bf16[64,512]{1,0:T(8,128)(2,1)S(1)} %get-tuple-element.54), channel_id=1, source_target_pairs={{0,24},{4,28},{8,16},{12,20},{16,8},{20,12},{24,0},{28,4},{1,25},{... | collective-permute-start | bytes 196616 | tf_op jit(solution)/shard_map/ppermute | solution.py:19
  36.2 0.0 collective-permute-done.13.refs_3_
  36.2 0.9 %collective-permute-start.16 = (bf16[64,512]{1,0:T(8,128)(2,1)S(1)}, bf16[64,512]{1,0:T(8,128)(2,1)S(1)}, u32[]{:S(2)}, u32[]{:S(2)}) collective-permute-start(bf16[64,512]{1,0:T(8,128)(2,1)S(1)} %get-tuple-element.47), channel_id=1, source_target_pairs={{0,8},{4,12},{8,0},{12,4},{16,24},{20,28},{24,16},{28,20},{1,9},{5... | collective-permute-start | bytes 196616 | tf_op jit(solution)/shard_map/ppermute | solution.py:19
  37.1 0.0 collective-permute-done.12.refs_2_
  37.1 0.0 collective-permute-done.11.refs_1_
  37.2 1.7 %collective-permute-start.15 = (bf16[128,256]{1,0:T(8,128)(2,1)S(1)}, bf16[128,256]{1,0:T(8,128)(2,1)S(1)}, u32[]{:S(2)}, u32[]{:S(2)}) collective-permute-start(bf16[128,256]{1,0:T(8,128)(2,1)S(1)} %shard_map.101.refs_0_), channel_id=1, source_target_pairs={{0,4},{4,0},{8,12},{12,8},{16,20},{20,16},{24,28},{28,24},{1,5},{5... | collective-permute-start | bytes 196616 | tf_op jit(solution)/shard_map/ppermute | solution.py:19
  38.9 2.2 %collective-permute-done.17.refs_2_ = bf16[64,512]{1,0:T(8,128)(2,1)S(1)} collective-permute-done((bf16[64,512]{1,0:T(8,128)(2,1)S(1)}, bf16[64,512]{1,0:T(8,128)(2,1)S(1)}, u32[]{:S(2)}, u32[]{:S(2)}) %collective-permute-start.17) | collective-permute-done | bytes 65568 | tf_op jit(solution)/shard_map/ppermute | solution.py:19
  41.1 0.0 collective-permute-done.18.refs_3_
  41.1 0.6 %collective-permute-done.16.refs_1_ = bf16[64,512]{1,0:T(8,128)(2,1)S(1)} collective-permute-done((bf16[64,512]{1,0:T(8,128)(2,1)S(1)}, bf16[64,512]{1,0:T(8,128)(2,1)S(1)}, u32[]{:S(2)}, u32[]{:S(2)}) %collective-permute-start.16) | collective-permute-done | bytes 65568 | tf_op jit(solution)/shard_map/ppermute | solution.py:19
  41.7 0.0 collective-permute-done.15.refs_1_
  41.8 0.1 collective-permute-start.19
  41.8 1.3 %collective-permute-done.19.other = f32[128,256]{1,0:T(8,128)S(1)} collective-permute-done((f32[128,256]{1,0:T(8,128)S(1)}, f32[128,256]{1,0:T(8,128)S(1)}, u32[]{:S(2)}, u32[]{:S(2)}) %collective-permute-start.19) | collective-permute-done | bytes 131104 | tf_op jit(solution)/shard_map/ppermute | solution.py:19
  43.2 0.8 %shard_map.104 = (bf16[256,128]{1,0:T(8,128)(2,1)}, f32[256,256]{1,0:T(8,128)}, f32[64,512]{1,0:T(8,128)}) custom-call(bf16[256,128]{1,0:T(8,128)(2,1)S(1)} %get-tuple-element.40.activated, f32[128,256]{1,0:T(8,128)S(1)} %shard_map.103.mine, f32[128,256]{1,0:T(8,128)S(1)} %collective-permute-done.19.other, f32[64,512]{1,0:T(8,128)S(1)} %shard_map.102.column_sum), custom_call_target="tpu_custom_call" | custom-call | flops 1024 | bytes 1024 | tf_op jit(solution)/shard_map/pallas_call | solution.py:53
  (5 shorter events, 0.1 us)
Async XLA Ops:
  0.6 9.4 %collective-permute-start.2 = (bf16[64,512]{1,0:T(8,128)(2,1)}, bf16[64,512]{1,0:T(8,128)(2,1)S(1)}, u32[]{:S(2)}, u32[]{:S(2)}) collective-permute-start(bf16[64,512]{1,0:T(8,128)(2,1)} %first.1), channel_id=1, source_target_pairs={{0,24},{4,28},{8,16},{12,20},{16,8},{20,12},{24,0},{28,4},{1,25},{... | collective-permute-start | bytes 196616 | tf_op jit(solution)/shard_map/ppermute | solution.py:19
  5.7 5.8 %collective-permute-start.1 = (bf16[64,512]{1,0:T(8,128)(2,1)}, bf16[64,512]{1,0:T(8,128)(2,1)S(1)}, u32[]{:S(2)}, u32[]{:S(2)}) collective-permute-start(bf16[64,512]{1,0:T(8,128)(2,1)} %first.1), channel_id=1, source_target_pairs={{0,16},{4,20},{8,24},{12,28},{16,0},{20,4},{24,8},{28,12},{1,17},{... | collective-permute-start | bytes 196616 | tf_op jit(solution)/shard_map/ppermute | solution.py:19
  5.7 5.8 %collective-permute-start = (bf16[64,512]{1,0:T(8,128)(2,1)}, bf16[64,512]{1,0:T(8,128)(2,1)S(1)}, u32[]{:S(2)}, u32[]{:S(2)}) collective-permute-start(bf16[64,512]{1,0:T(8,128)(2,1)} %first.1), channel_id=1, source_target_pairs={{0,8},{4,12},{8,0},{12,4},{16,24},{20,28},{24,16},{28,20},{1,9},{5... | collective-permute-start | bytes 196616 | tf_op jit(solution)/shard_map/ppermute | solution.py:19
  6.4 5.2 %collective-permute-start.3 = (bf16[64,512]{1,0:T(8,128)(2,1)}, bf16[64,512]{1,0:T(8,128)(2,1)S(1)}, u32[]{:S(2)}, u32[]{:S(2)}) collective-permute-start(bf16[64,512]{1,0:T(8,128)(2,1)} %first.1), channel_id=1, source_target_pairs={{0,4},{4,0},{8,12},{12,8},{16,20},{20,16},{24,28},{28,24},{1,5},{5... | collective-permute-start | bytes 196616 | tf_op jit(solution)/shard_map/ppermute | solution.py:19
  11.6 1.6 %copy-start.2 = (bf16[256,128]{1,0:T(8,128)(2,1)S(1)}, bf16[256,128]{1,0:T(8,128)(2,1)}, u32[]{:S(2)}) copy-start(bf16[256,128]{1,0:T(8,128)(2,1)} %refs_4_.1) | copy-start | bytes 196612
  11.6 3.1 %copy-start.1 = (bf16[64,512]{1,0:T(8,128)(2,1)S(1)}, bf16[64,512]{1,0:T(8,128)(2,1)}, u32[]{:S(2)}) copy-start(bf16[64,512]{1,0:T(8,128)(2,1)} %first.1) | copy-start | bytes 196612
  11.6 6.5 %collective-permute-start.4 = (bf16[3,64,512]{2,1,0:T(8,128)(2,1)S(1)}, bf16[3,64,512]{2,1,0:T(8,128)(2,1)S(1)}, u32[]{:S(2)}, u32[]{:S(2)}) collective-permute-start(bf16[3,64,512]{2,1,0:T(8,128)(2,1)S(1)} %shard_map.95.rest), channel_id=1, source_target_pairs={{0,4},{4,0},{8,12},{12,8},{16,20},{20,16},{24,28},{28,24},{1,5},{5... | collective-permute-start | bytes 589832 | tf_op jit(solution)/shard_map/ppermute | solution.py:19
  13.2 7.2 %collective-permute-start.9 = (bf16[256,128]{1,0:T(8,128)(2,1)S(1)}, bf16[256,128]{1,0:T(8,128)(2,1)S(1)}, u32[]{:S(2)}, u32[]{:S(2)}) collective-permute-start(bf16[256,128]{1,0:T(8,128)(2,1)S(1)} %copy-done.2), channel_id=1, source_target_pairs={{0,2},{1,3},{2,0},{3,1},{4,6},{5,7},{6,4},{7,5},{8,10},{9,11},{10,... | collective-permute-start | bytes 196616 | tf_op jit(solution)/shard_map/ppermute | solution.py:19
  15.3 8.9 %copy-start = (bf16[256,256]{1,0:T(8,128)(2,1)S(1)}, bf16[256,256]{1,0:T(8,128)(2,1)}, u32[]{:S(2)}) copy-start(bf16[256,256]{1,0:T(8,128)(2,1)} %weight.1) | copy-start | bytes 393220
  18.6 4.3 %collective-permute-start.6 = (bf16[64,512]{1,0:T(8,128)(2,1)S(1)}, bf16[64,512]{1,0:T(8,128)(2,1)S(1)}, u32[]{:S(2)}, u32[]{:S(2)}) collective-permute-start(bf16[64,512]{1,0:T(8,128)(2,1)S(1)} %shard_map.97.refs_0_), channel_id=1, source_target_pairs={{0,2},{1,3},{2,0},{3,1},{4,6},{5,7},{6,4},{7,5},{8,10},{9,11},{10,... | collective-permute-start | bytes 196616 | tf_op jit(solution)/shard_map/ppermute | solution.py:19
  20.3 2.6 %collective-permute-start.8 = (bf16[256,128]{1,0:T(8,128)(2,1)S(1)}, bf16[256,128]{1,0:T(8,128)(2,1)S(1)}, u32[]{:S(2)}, u32[]{:S(2)}) collective-permute-start(bf16[256,128]{1,0:T(8,128)(2,1)S(1)} %copy-done.2), channel_id=1, source_target_pairs={{0,1},{1,0},{2,3},{3,2},{4,5},{5,4},{6,7},{7,6},{8,9},{9,8},{10,11... | collective-permute-start | bytes 196616 | tf_op jit(solution)/shard_map/ppermute | solution.py:19
  20.3 2.6 %collective-permute-start.10 = (bf16[256,128]{1,0:T(8,128)(2,1)S(1)}, bf16[256,128]{1,0:T(8,128)(2,1)S(1)}, u32[]{:S(2)}, u32[]{:S(2)}) collective-permute-start(bf16[256,128]{1,0:T(8,128)(2,1)S(1)} %collective-permute-done.9.refs_6_), channel_id=1, source_target_pairs={{0,1},{1,0},{2,3},{3,2},{4,5},{5,4},{6,7},{7,6},{8,9},{9,8},{10,11... | collective-permute-start | bytes 196616 | tf_op jit(solution)/shard_map/ppermute | solution.py:19
  20.8 2.1 %collective-permute-start.5 = (bf16[64,512]{1,0:T(8,128)(2,1)S(1)}, bf16[64,512]{1,0:T(8,128)(2,1)S(1)}, u32[]{:S(2)}, u32[]{:S(2)}) collective-permute-start(bf16[64,512]{1,0:T(8,128)(2,1)S(1)} %shard_map.97.refs_0_), channel_id=1, source_target_pairs={{0,1},{1,0},{2,3},{3,2},{4,5},{5,4},{6,7},{7,6},{8,9},{9,8},{10,11... | collective-permute-start | bytes 196616 | tf_op jit(solution)/shard_map/ppermute | solution.py:19
  22.9 1.3 %collective-permute-start.7 = (bf16[64,512]{1,0:T(8,128)(2,1)S(1)}, bf16[64,512]{1,0:T(8,128)(2,1)S(1)}, u32[]{:S(2)}, u32[]{:S(2)}) collective-permute-start(bf16[64,512]{1,0:T(8,128)(2,1)S(1)} %collective-permute-done.6.refs_2_), channel_id=1, source_target_pairs={{0,1},{1,0},{2,3},{3,2},{4,5},{5,4},{6,7},{7,6},{8,9},{9,8},{10,11... | collective-permute-start | bytes 196616 | tf_op jit(solution)/shard_map/ppermute | solution.py:19
  25.1 8.4 %collective-permute-start.14 = (bf16[256,512]{1,0:T(8,128)(2,1)S(1)}, bf16[256,512]{1,0:T(8,128)(2,1)S(1)}, u32[]{:S(2)}, u32[]{:S(2)}) collective-permute-start(bf16[256,512]{1,0:T(8,128)(2,1)S(1)} %get-tuple-element.46), channel_id=1, source_target_pairs={{0,4},{4,0},{8,12},{12,8},{16,20},{20,16},{24,28},{28,24},{1,5},{5... | collective-permute-start | bytes 786440 | tf_op jit(solution)/shard_map/ppermute | solution.py:19
  27.2 9.1 %collective-permute-start.13 = (bf16[128,256]{1,0:T(8,128)(2,1)S(1)}, bf16[128,256]{1,0:T(8,128)(2,1)S(1)}, u32[]{:S(2)}, u32[]{:S(2)}) collective-permute-start(bf16[128,256]{1,0:T(8,128)(2,1)S(1)} %get-tuple-element.48.refs_0_), channel_id=1, source_target_pairs={{0,24},{4,28},{8,16},{12,20},{16,8},{20,12},{24,0},{28,4},{1,25},{... | collective-permute-start | bytes 196616 | tf_op jit(solution)/shard_map/ppermute | solution.py:19
  29.3 7.8 %collective-permute-start.12 = (bf16[128,256]{1,0:T(8,128)(2,1)S(1)}, bf16[128,256]{1,0:T(8,128)(2,1)S(1)}, u32[]{:S(2)}, u32[]{:S(2)}) collective-permute-start(bf16[128,256]{1,0:T(8,128)(2,1)S(1)} %get-tuple-element.48.refs_0_), channel_id=1, source_target_pairs={{0,16},{4,20},{8,24},{12,28},{16,0},{20,4},{24,8},{28,12},{1,17},{... | collective-permute-start | bytes 196616 | tf_op jit(solution)/shard_map/ppermute | solution.py:19
  29.3 7.8 %collective-permute-start.11 = (bf16[128,256]{1,0:T(8,128)(2,1)S(1)}, bf16[128,256]{1,0:T(8,128)(2,1)S(1)}, u32[]{:S(2)}, u32[]{:S(2)}) collective-permute-start(bf16[128,256]{1,0:T(8,128)(2,1)S(1)} %get-tuple-element.48.refs_0_), channel_id=1, source_target_pairs={{0,8},{4,12},{8,0},{12,4},{16,24},{20,28},{24,16},{28,20},{1,9},{5... | collective-permute-start | bytes 196616 | tf_op jit(solution)/shard_map/ppermute | solution.py:19
  33.5 7.6 %collective-permute-start.17 = (bf16[64,512]{1,0:T(8,128)(2,1)S(1)}, bf16[64,512]{1,0:T(8,128)(2,1)S(1)}, u32[]{:S(2)}, u32[]{:S(2)}) collective-permute-start(bf16[64,512]{1,0:T(8,128)(2,1)S(1)} %get-tuple-element.53), channel_id=1, source_target_pairs={{0,16},{4,20},{8,24},{12,28},{16,0},{20,4},{24,8},{28,12},{1,17},{... | collective-permute-start | bytes 196616 | tf_op jit(solution)/shard_map/ppermute | solution.py:19
  34.4 6.7 %collective-permute-start.18 = (bf16[64,512]{1,0:T(8,128)(2,1)S(1)}, bf16[64,512]{1,0:T(8,128)(2,1)S(1)}, u32[]{:S(2)}, u32[]{:S(2)}) collective-permute-start(bf16[64,512]{1,0:T(8,128)(2,1)S(1)} %get-tuple-element.54), channel_id=1, source_target_pairs={{0,24},{4,28},{8,16},{12,20},{16,8},{20,12},{24,0},{28,4},{1,25},{... | collective-permute-start | bytes 196616 | tf_op jit(solution)/shard_map/ppermute | solution.py:19
  36.2 5.4 %collective-permute-start.16 = (bf16[64,512]{1,0:T(8,128)(2,1)S(1)}, bf16[64,512]{1,0:T(8,128)(2,1)S(1)}, u32[]{:S(2)}, u32[]{:S(2)}) collective-permute-start(bf16[64,512]{1,0:T(8,128)(2,1)S(1)} %get-tuple-element.47), channel_id=1, source_target_pairs={{0,8},{4,12},{8,0},{12,4},{16,24},{20,28},{24,16},{28,20},{1,9},{5... | collective-permute-start | bytes 196616 | tf_op jit(solution)/shard_map/ppermute | solution.py:19
  37.2 4.6 %collective-permute-start.15 = (bf16[128,256]{1,0:T(8,128)(2,1)S(1)}, bf16[128,256]{1,0:T(8,128)(2,1)S(1)}, u32[]{:S(2)}, u32[]{:S(2)}) collective-permute-start(bf16[128,256]{1,0:T(8,128)(2,1)S(1)} %shard_map.101.refs_0_), channel_id=1, source_target_pairs={{0,4},{4,0},{8,12},{12,8},{16,20},{20,16},{24,28},{28,24},{1,5},{5... | collective-permute-start | bytes 196616 | tf_op jit(solution)/shard_map/ppermute | solution.py:19
  41.8 1.4 %collective-permute-start.19 = (f32[128,256]{1,0:T(8,128)S(1)}, f32[128,256]{1,0:T(8,128)S(1)}, u32[]{:S(2)}, u32[]{:S(2)}) collective-permute-start(f32[128,256]{1,0:T(8,128)S(1)} %shard_map.103.mine), channel_id=1, source_target_pairs={{0,1},{1,0},{2,3},{3,2},{4,5},{5,4},{6,7},{7,6},{8,9},{9,8},{10,11... | collective-permute-start | bytes 393224 | tf_op jit(solution)/shard_map/ppermute | solution.py:19

commit v6 on v5

--- a/solution.py
+++ b/solution.py
@@ -126,13 +126,13 @@
         out[:, r * side : (r + 1) * side] = totals[r].astype(BF16)
 
 
-def add_backward(values, row_masks, col_masks, grads, out, flip):
+def add_backward(values, row_masks, col_masks, grads, out, flip, first):
     own = lax.axis_index("node") ^ flip
     width = grads.shape[0]
     side = values.shape[1]
 
     def one(k):
-        sums = tile_sums(values, row_masks, col_masks, grads, own ^ (2 * k), False)
+        sums = tile_sums(values, row_masks, col_masks, grads, own ^ (2 * (k + first)), False)
         for c, part in enumerate(sums):
             out[lanes(k, width), c * side : (c + 1) * side] = part.astype(out.dtype)
 
@@ -155,7 +155,7 @@
 
 def middle(values, row_masks, col_masks, weight, *refs, feat):
     aggs, cots = refs[:feat], refs[feat : 2 * feat]
-    activated, grads, mine, dpre_full, sent, agg_full = refs[2 * feat :]
+    activated, grads, mine, dpre_full, sent_own, sent, agg_full = refs[2 * feat :]
     index = lax.axis_index("feat")
     width, local = aggs[0].shape
     side = cots[0].shape[1]
@@ -172,12 +172,13 @@
     dpre_all = dpre_full[...]
     grads[...] = dot(weight[lanes(index, width), :], dpre_all, ((1,), (0,))).astype(BF16)
     mine[...] = agg_full[lanes(index & 1, mine.shape[0]), :]
-    add_backward(values, row_masks, col_masks, grads, sent, 1)
+    add_backward(values, row_masks, col_masks, grads, sent, 1, 1)
+    add_backward(values, row_masks, col_masks, grads, sent_own, 1, 0)
 
 
 def backward_near(values, row_masks, col_masks, grads, mine, dpre, out, weight_part):
     weight_part[...] = dot(mine[...], dpre[...], ((1,), (1,))).astype(BF16)
-    add_backward(values, row_masks, col_masks, grads, out, 0)
+    add_backward(values, row_masks, col_masks, grads, out, 0, 0)
 
 
 def add_weights(one, other, out):
@@ -188,24 +189,26 @@
     refs[-1][...] = tree_sum([r[...].astype(F32) for r in refs[:-1]]).astype(refs[-1].dtype)
 
 
-def add_pair(near, got, own, *sent):
-    width = own.shape[0]
-    own[...] = near[:width] + got[:width].astype(F32)
-    for k, out in enumerate(sent, 1):
+def add_pair(near, got, *sent):
+    width = sent[0].shape[0]
+    for k, out in enumerate(sent):
         rows = slice(k * width, (k + 1) * width)
-        out[...] = (near[rows] + got[rows].astype(F32)).astype(BF16)
-
-
-def finish(activated, mine, other, column_sum, activated_out, weight_out, gradient):
+        out[...] = (near[(k + 1) * width : (k + 2) * width] + got[rows].astype(F32)).astype(BF16)
+
+
+def finish(activated, core, part, across, diagonal, column_sum, *outs):
+    activated_out, weight_out, gradient = outs
     activated_out[...] = activated[...]
-    core = lax.axis_index("feat") & 1
-    weight_out[lanes(core, mine.shape[0]), :] = mine[...]
-    weight_out[lanes(core ^ 1, mine.shape[0]), :] = other[...]
+    own = lax.axis_index("feat") & 1
+    rows = part.shape[0]
+    weight_out[lanes(own, rows), :] = part[...].astype(F32) + across[...].astype(F32)
+    weight_out[lanes(own ^ 1, rows), :] = core[...].astype(F32) + diagonal[...].astype(F32)
     gradient[...] = column_sum[...]
 
 
-def add_column(*refs):
-    refs[-1][...] = sum(r[...].astype(F32) for r in refs[:-1])
+def add_column(near, *refs):
+    width = refs[0].shape[0]
+    refs[-1][...] = near[:width] + sum(r[...].astype(F32) for r in refs[:-1])
 
 
 def per_device(features, tile_values, tile_rows, tile_cols, tile_counts, weight, cotangent):
@@ -246,7 +249,7 @@
         [pltpu.VMEM(totals, F32)],
     )
     aggs = gather_feat(aggregated)
-    activated, grads, mine, dpre, sent = call(
+    activated, grads, mine, dpre, sent_own, sent = call(
         functools.partial(middle, feat=feat),
         [*tiles, weight, *aggs, *cots],
         [
@@ -254,7 +257,8 @@
             shape((width, local), BF16),
             shape((wide // 2, local), BF16),
             shape((wide, local), BF16),
-            shape((column * width, local), BF16),
+            shape((width, local), BF16),
+            shape(((column - 1) * width, local), BF16),
         ],
         [pltpu.VMEM((wide, local), BF16)],
     )
@@ -266,25 +270,33 @@
         cost=LARGE,
     )
     parts = [weight_part] + [swapped(weight_part, "node", 2 * k) for k in range(1, column)]
-    own, *chunks = call(
+    chunks = call(
         add_pair,
         [near_grads, got],
-        [shape((width, local), F32)] + [shape((width, local), BF16)] * (column - 1),
+        [shape((width, local), BF16)] * (column - 1),
         cost=SMALL,
     )
     arrived = [swapped(c, "node", 2 * k) for k, c in enumerate(chunks, 1)]
-    *parts, _ = lax.optimization_barrier((*parts, chunks[0]))
+    sent_own, _ = lax.optimization_barrier((sent_own, chunks[0]))
+    across_own = swapped(sent_own, "node", 1)
+    ordered = lax.optimization_barrier(
+        (parts[0], *[parts[k] for k in (1, 3, 2)], chunks[0])
+    )
+    parts = [ordered[0], *[ordered[k] for k in (1, 3, 2)]]
     (part,) = call(sum_weights, parts, [shape((wide // 2, wide), BF16)], cost=SMALL)
-    other = swapped(part, "node", 1)
+    core = swapped(part, "feat", 1)
+    across = swapped(part, "node", 1)
+    every = range(nodes * feat)
+    diagonal = lax.ppermute(part, ("node", "feat"), [(i, i ^ (feat + 1)) for i in every])
     (column_sum,) = call(
-        add_column, [own, *arrived], [shape((width, local), F32)], cost=LARGE
-    )
-    other, column_sum = lax.optimization_barrier((other, column_sum))
-    (half,) = call(sum_weights, [part, other], [shape((wide // 2, wide), F32)], cost=SMALL)
-    other_half = swapped(half, "feat", 1)
+        add_column, [near_grads, arrived[0], across_own, *arrived[1:]], [shape((width, local), F32)], cost=LARGE
+    )
+    core, diagonal, across, column_sum = lax.optimization_barrier(
+        (core, diagonal, across, column_sum)
+    )
     activated, grad_weight, gradient = call(
         finish,
-        [activated, half, other_half, column_sum],
+        [activated, core, part, across, diagonal, column_sum],
         [
             shape((wide, side), BF16),
             shape((wide, wide), F32),

time: 44.2 us -> 43.3 us (0.980)
  starting transfers between devices: 24.3 us -> 23.4 us
    ppermute x20 -> x21, starting transfers between devices: 24.3 us -> 23.4 us  [swapped(): lax.ppermute(x, axis, [(i, i ^ mask) for i in range(lax.axis_size(axis))])]
    pallas_call x11 -> x10, Pallas kernels: 5.18 us -> 5.15 us  [call(): pl.pallas_call(body, in_specs=[SMEM] * scalars + [spec] * (len(inputs) -...]
    ppermute x20 -> x21, waiting for transfers between devices: 13.7 us -> 13.7 us  [swapped(): lax.ppermute(x, axis, [(i, i ^ mask) for i in range(lax.axis_size(axis))])]
  transfers between devices with their start and end apart: 20 -> 22, of which waited for: 8 -> 10; matrix products, arithmetic and copies ran while one was open for 0% -> 0% of each run, Pallas kernels for 8% -> 8%
where the time goes in v6:
time: 43.3 us; the launch traced here: 43 us
  starting transfers between devices  23.4 us (54%)
  waiting for transfers between devices  13.7 us (32%)
  Pallas kernels  5.15 us (12%)
  between operations  0.75 us (2%)
    ppermute x21, starting transfers between devices, swapped(): lax.ppermute(x, axis, [(i, i ^ mask) for i in range(lax.axis_size(axis))])  23.4 us
    ppermute x21, waiting for transfers between devices, swapped(): lax.ppermute(x, axis, [(i, i ^ mask) for i in range(lax.axis_size(axis))])  13.7 us
    pallas_call x10, Pallas kernels, call(): pl.pallas_call(body, in_specs=[SMEM] * scalars + [spec] * (len(inputs) -...  5.15 us
  transfers between devices with their start and end apart: 22, of which 10 were waited for; matrix products, arithmetic and copies ran while one was open for 0% of the time, Pallas kernels for 8%

profile of v6, /device:TPU:0, one launch (start us, length us, event | category | flops | bytes accessed | tf_op | source)
XLA Modules:
  0.0 43.0 jit_solution(9216968672219928505)
XLA Ops:
  0.6 5.1 %collective-permute-start.2 = (bf16[64,512]{1,0:T(8,128)(2,1)}, bf16[64,512]{1,0:T(8,128)(2,1)S(1)}, u32[]{:S(2)}, u32[]{:S(2)}) collective-permute-start(bf16[64,512]{1,0:T(8,128)(2,1)} %first.1), channel_id=1, source_target_pairs={{0,24},{4,28},{8,16},{12,20},{16,8},{20,12},{24,0},{28,4},{1,25},{... | collective-permute-start | bytes 196616 | tf_op jit(solution)/shard_map/ppermute | solution.py:19
  5.7 0.0 collective-permute-start.1
  5.7 0.6 %collective-permute-start = (bf16[64,512]{1,0:T(8,128)(2,1)}, bf16[64,512]{1,0:T(8,128)(2,1)S(1)}, u32[]{:S(2)}, u32[]{:S(2)}) collective-permute-start(bf16[64,512]{1,0:T(8,128)(2,1)} %first.1), channel_id=1, source_target_pairs={{0,8},{4,12},{8,0},{12,4},{16,24},{20,28},{24,16},{28,20},{1,9},{5... | collective-permute-start | bytes 196616 | tf_op jit(solution)/shard_map/ppermute | solution.py:19
  6.4 1.6 %collective-permute-start.3 = (bf16[64,512]{1,0:T(8,128)(2,1)}, bf16[64,512]{1,0:T(8,128)(2,1)S(1)}, u32[]{:S(2)}, u32[]{:S(2)}) collective-permute-start(bf16[64,512]{1,0:T(8,128)(2,1)} %first.1), channel_id=1, source_target_pairs={{0,4},{4,0},{8,12},{12,8},{16,20},{20,16},{24,28},{28,24},{1,5},{5... | collective-permute-start | bytes 196616 | tf_op jit(solution)/shard_map/ppermute | solution.py:19
  8.0 2.0 %shard_map.94 = (bf16[32,128,128]{2,1,0:T(8,128)(2,1)S(1)}, bf16[32,4,16,128]{3,2,1,0:T(8,128)(2,1)S(1)}, bf16[32,4,16,128]{3,2,1,0:T(8,128)(2,1)S(1)}) custom-call(s32[4,8]{1,0:T(4,128)} %bitcast.2, s32[4,8]{1,0:T(4,128)} %bitcast.3, s32[8]{0:T(128)} %counts.1, bf16[32,128,128]{2,1,0:T(8,128)(2,1)} %source.1), custom_call_target="tpu_custom_call" | custom-call | tf_op jit(solution)/shard_map/pallas_call | solution.py:53
  10.0 0.0 collective-permute-done.2.refs_2_
  10.0 1.6 %collective-permute-done.1.refs_1_ = bf16[64,512]{1,0:T(8,128)(2,1)S(1)} collective-permute-done((bf16[64,512]{1,0:T(8,128)(2,1)}, bf16[64,512]{1,0:T(8,128)(2,1)S(1)}, u32[]{:S(2)}, u32[]{:S(2)}) %collective-permute-start.1) | collective-permute-done | bytes 65568 | tf_op jit(solution)/shard_map/ppermute | solution.py:19
  11.6 0.0 collective-permute-done.refs_0_
  11.6 0.0 collective-permute-done.3.across
  11.6 0.0 copy-start.2
  11.6 0.0 copy-start.1
  11.6 1.6 %collective-permute-start.4 = (bf16[3,64,512]{2,1,0:T(8,128)(2,1)S(1)}, bf16[3,64,512]{2,1,0:T(8,128)(2,1)S(1)}, u32[]{:S(2)}, u32[]{:S(2)}) collective-permute-start(bf16[3,64,512]{2,1,0:T(8,128)(2,1)S(1)} %shard_map.95.rest), channel_id=1, source_target_pairs={{0,4},{4,0},{8,12},{12,8},{16,20},{20,16},{24,28},{28,24},{1,5},{5... | collective-permute-start | bytes 589832 | tf_op jit(solution)/shard_map/ppermute | solution.py:19
  13.2 0.0 copy-done.2
  13.2 1.5 %collective-permute-start.9 = (bf16[256,128]{1,0:T(8,128)(2,1)S(1)}, bf16[256,128]{1,0:T(8,128)(2,1)S(1)}, u32[]{:S(2)}, u32[]{:S(2)}) collective-permute-start(bf16[256,128]{1,0:T(8,128)(2,1)S(1)} %copy-done.2), channel_id=1, source_target_pairs={{0,2},{1,3},{2,0},{3,1},{4,6},{5,7},{6,4},{7,5},{8,10},{9,11},{10,... | collective-permute-start | bytes 196616 | tf_op jit(solution)/shard_map/ppermute | solution.py:19
  14.7 0.0 copy-done.1
  14.7 0.6 %shard_map.96.near = f32[4,64,128]{2,1,0:T(8,128)S(1)} custom-call(bf16[32,128,128]{2,1,0:T(8,128)(2,1)S(1)} %get-tuple-element.36.values, bf16[32,4,16,128]{3,2,1,0:T(8,128)(2,1)S(1)} %get-tuple-element.37.row_masks, bf16[32,4,16,128]{3,2,1,0:T(8,128)(2,1)S(1)} %get-tuple-element.38.col_masks, bf16[64,512]{1,0:T(8,128)(2,1)S(1)} %copy-done.1, ...), custom_call_target="tpu_custom_call" | custom-call | tf_op jit(solution)/shard_map/pallas_call | solution.py:53
  15.3 0.0 copy-start
  15.3 2.8 %collective-permute-done.4.rest = bf16[3,64,512]{2,1,0:T(8,128)(2,1)S(1)} collective-permute-done((bf16[3,64,512]{2,1,0:T(8,128)(2,1)S(1)}, bf16[3,64,512]{2,1,0:T(8,128)(2,1)S(1)}, u32[]{:S(2)}, u32[]{:S(2)}) %collective-permute-start.4) | collective-permute-done | bytes 196640 | tf_op jit(solution)/shard_map/ppermute | solution.py:19
  18.1 0.4 shard_map.97.refs_0_
  18.6 1.8 %collective-permute-start.6 = (bf16[64,512]{1,0:T(8,128)(2,1)S(1)}, bf16[64,512]{1,0:T(8,128)(2,1)S(1)}, u32[]{:S(2)}, u32[]{:S(2)}) collective-permute-start(bf16[64,512]{1,0:T(8,128)(2,1)S(1)} %shard_map.97.refs_0_), channel_id=1, source_target_pairs={{0,2},{1,3},{2,0},{3,1},{4,6},{5,7},{6,4},{7,5},{8,10},{9,11},{10,... | collective-permute-start | bytes 196616 | tf_op jit(solution)/shard_map/ppermute | solution.py:19
  20.3 0.0 collective-permute-start.8
  20.3 0.0 collective-permute-done.9.refs_6_
  20.3 0.5 %collective-permute-start.10 = (bf16[256,128]{1,0:T(8,128)(2,1)S(1)}, bf16[256,128]{1,0:T(8,128)(2,1)S(1)}, u32[]{:S(2)}, u32[]{:S(2)}) collective-permute-start(bf16[256,128]{1,0:T(8,128)(2,1)S(1)} %collective-permute-done.9.refs_6_), channel_id=1, source_target_pairs={{0,1},{1,0},{2,3},{3,2},{4,5},{5,4},{6,7},{7,6},{8,9},{9,8},{10,11... | collective-permute-start | bytes 196616 | tf_op jit(solution)/shard_map/ppermute | solution.py:19
  20.8 0.0 collective-permute-start.5
  20.8 2.0 %collective-permute-done.6.refs_2_ = bf16[64,512]{1,0:T(8,128)(2,1)S(1)} collective-permute-done((bf16[64,512]{1,0:T(8,128)(2,1)S(1)}, bf16[64,512]{1,0:T(8,128)(2,1)S(1)}, u32[]{:S(2)}, u32[]{:S(2)}) %collective-permute-start.6) | collective-permute-done | bytes 65568 | tf_op jit(solution)/shard_map/ppermute | solution.py:19
  22.9 0.0 collective-permute-start.7
  22.9 0.0 collective-permute-done.8.refs_5_
  22.9 0.0 collective-permute-done.10.refs_7_
  22.9 0.0 collective-permute-done.5.refs_1_
  22.9 1.2 %collective-permute-done.7.refs_3_ = bf16[64,512]{1,0:T(8,128)(2,1)S(1)} collective-permute-done((bf16[64,512]{1,0:T(8,128)(2,1)S(1)}, bf16[64,512]{1,0:T(8,128)(2,1)S(1)}, u32[]{:S(2)}, u32[]{:S(2)}) %collective-permute-start.7) | collective-permute-done | bytes 65568 | tf_op jit(solution)/shard_map/ppermute | solution.py:19
  24.1 0.0 copy-done
  24.1 0.9 %shard_map.98 = (bf16[256,128]{1,0:T(8,128)(2,1)S(1)}, bf16[64,512]{1,0:T(8,128)(2,1)S(1)}, bf16[128,512]{1,0:T(8,128)(2,1)S(1)}, bf16[256,512]{1,0:T(8,128)(2,1...) custom-call(bf16[32,128,128]{2,1,0:T(8,128)(2,1)S(1)} %get-tuple-element.36.values, ...), custom_call_target="tpu_custom_call" | custom-call | tf_op jit(solution)/shard_map/pallas_call | solution.py:53
  25.1 1.7 %collective-permute-start.14 = (bf16[192,512]{1,0:T(8,128)(2,1)S(1)}, bf16[192,512]{1,0:T(8,128)(2,1)S(1)}, u32[]{:S(2)}, u32[]{:S(2)}) collective-permute-start(bf16[192,512]{1,0:T(8,128)(2,1)S(1)} %get-tuple-element.49), channel_id=1, source_target_pairs={{0,4},{4,0},{8,12},{12,8},{16,20},{20,16},{24,28},{28,24},{1,5},{5... | collective-permute-start | bytes 589832 | tf_op jit(solution)/shard_map/ppermute | solution.py:19
  26.8 0.4 shard_map.99
  27.2 0.6 %collective-permute-start.13 = (bf16[128,256]{1,0:T(8,128)(2,1)S(1)}, bf16[128,256]{1,0:T(8,128)(2,1)S(1)}, u32[]{:S(2)}, u32[]{:S(2)}) collective-permute-start(bf16[128,256]{1,0:T(8,128)(2,1)S(1)} %get-tuple-element.51.refs_0_), channel_id=1, source_target_pairs={{0,16},{4,20},{8,24},{12,28},{16,0},{20,4},{24,8},{28,12},{1,17},{... | collective-permute-start | bytes 196616 | tf_op jit(solution)/shard_map/ppermute | solution.py:19
  27.8 1.9 %collective-permute-start.12 = (bf16[128,256]{1,0:T(8,128)(2,1)S(1)}, bf16[128,256]{1,0:T(8,128)(2,1)S(1)}, u32[]{:S(2)}, u32[]{:S(2)}) collective-permute-start(bf16[128,256]{1,0:T(8,128)(2,1)S(1)} %get-tuple-element.51.refs_0_), channel_id=1, source_target_pairs={{0,24},{4,28},{8,16},{12,20},{16,8},{20,12},{24,0},{28,4},{1,25},{... | collective-permute-start | bytes 196616 | tf_op jit(solution)/shard_map/ppermute | solution.py:19
  29.7 1.1 %collective-permute-start.11 = (bf16[128,256]{1,0:T(8,128)(2,1)S(1)}, bf16[128,256]{1,0:T(8,128)(2,1)S(1)}, u32[]{:S(2)}, u32[]{:S(2)}) collective-permute-start(bf16[128,256]{1,0:T(8,128)(2,1)S(1)} %get-tuple-element.51.refs_0_), channel_id=1, source_target_pairs={{0,8},{4,12},{8,0},{12,4},{16,24},{20,28},{24,16},{28,20},{1,9},{5... | collective-permute-start | bytes 196616 | tf_op jit(solution)/shard_map/ppermute | solution.py:19
  30.7 1.4 %collective-permute-done.14.got = bf16[192,512]{1,0:T(8,128)(2,1)S(1)} collective-permute-done((bf16[192,512]{1,0:T(8,128)(2,1)S(1)}, bf16[192,512]{1,0:T(8,128)(2,1)S(1)}, u32[]{:S(2)}, u32[]{:S(2)}) %collective-permute-start.14) | collective-permute-done | bytes 196640 | tf_op jit(solution)/shard_map/ppermute | solution.py:19
  32.1 1.7 %collective-permute-start.19 = (bf16[64,512]{1,0:T(8,128)(2,1)S(1)}, bf16[64,512]{1,0:T(8,128)(2,1)S(1)}, u32[]{:S(2)}, u32[]{:S(2)}) collective-permute-start(bf16[64,512]{1,0:T(8,128)(2,1)S(1)} %get-tuple-element.56), channel_id=1, source_target_pairs={{0,4},{4,0},{8,12},{12,8},{16,20},{20,16},{24,28},{28,24},{1,5},{5... | collective-permute-start | bytes 196616 | tf_op jit(solution)/shard_map/ppermute | solution.py:19
  33.9 0.6 %collective-permute-start.20 = (bf16[64,512]{1,0:T(8,128)(2,1)S(1)}, bf16[64,512]{1,0:T(8,128)(2,1)S(1)}, u32[]{:S(2)}, u32[]{:S(2)}) collective-permute-start(bf16[64,512]{1,0:T(8,128)(2,1)S(1)} %get-tuple-element.57), channel_id=1, source_target_pairs={{0,16},{4,20},{8,24},{12,28},{16,0},{20,4},{24,8},{28,12},{1,17},{... | collective-permute-start | bytes 196616 | tf_op jit(solution)/shard_map/ppermute | solution.py:19
  34.5 0.3 collective-permute-done.13.refs_2_
  34.7 2.0 %collective-permute-start.21 = (bf16[64,512]{1,0:T(8,128)(2,1)S(1)}, bf16[64,512]{1,0:T(8,128)(2,1)S(1)}, u32[]{:S(2)}, u32[]{:S(2)}) collective-permute-start(bf16[64,512]{1,0:T(8,128)(2,1)S(1)} %get-tuple-element.58), channel_id=1, source_target_pairs={{0,24},{4,28},{8,16},{12,20},{16,8},{20,12},{24,0},{28,4},{1,25},{... | collective-permute-start | bytes 196616 | tf_op jit(solution)/shard_map/ppermute | solution.py:19
  36.7 0.0 collective-permute-done.12.refs_3_
  36.7 0.7 %collective-permute-start.18 = (bf16[64,512]{1,0:T(8,128)(2,1)S(1)}, bf16[64,512]{1,0:T(8,128)(2,1)S(1)}, u32[]{:S(2)}, u32[]{:S(2)}) collective-permute-start(bf16[64,512]{1,0:T(8,128)(2,1)S(1)} %get-tuple-element.50), channel_id=1, source_target_pairs={{0,8},{4,12},{8,0},{12,4},{16,24},{20,28},{24,16},{28,20},{1,9},{5... | collective-permute-start | bytes 196616 | tf_op jit(solution)/shard_map/ppermute | solution.py:19
  37.4 0.0 collective-permute-done.11.refs_1_
  37.4 0.4 collective-permute-start.17
  37.8 0.0 collective-permute-done.19.refs_1_
  37.8 0.0 collective-permute-start.16
  37.8 2.3 %collective-permute-done.20.refs_2_ = bf16[64,512]{1,0:T(8,128)(2,1)S(1)} collective-permute-done((bf16[64,512]{1,0:T(8,128)(2,1)S(1)}, bf16[64,512]{1,0:T(8,128)(2,1)S(1)}, u32[]{:S(2)}, u32[]{:S(2)}) %collective-permute-start.20) | collective-permute-done | bytes 65568 | tf_op jit(solution)/shard_map/ppermute | solution.py:19
  40.2 0.0 collective-permute-start.15
  40.2 0.8 %collective-permute-done.21.refs_3_ = bf16[64,512]{1,0:T(8,128)(2,1)S(1)} collective-permute-done((bf16[64,512]{1,0:T(8,128)(2,1)S(1)}, bf16[64,512]{1,0:T(8,128)(2,1)S(1)}, u32[]{:S(2)}, u32[]{:S(2)}) %collective-permute-start.21) | collective-permute-done | bytes 65568 | tf_op jit(solution)/shard_map/ppermute | solution.py:19
  41.0 0.6 %collective-permute-done.18.refs_0_ = bf16[64,512]{1,0:T(8,128)(2,1)S(1)} collective-permute-done((bf16[64,512]{1,0:T(8,128)(2,1)S(1)}, bf16[64,512]{1,0:T(8,128)(2,1)S(1)}, u32[]{:S(2)}, u32[]{:S(2)}) %collective-permute-start.18) | collective-permute-done | bytes 65568 | tf_op jit(solution)/shard_map/ppermute | solution.py:19
  41.6 0.6 %collective-permute-done.17.across = bf16[128,256]{1,0:T(8,128)(2,1)S(1)} collective-permute-done((bf16[128,256]{1,0:T(8,128)(2,1)S(1)}, bf16[128,256]{1,0:T(8,128)(2,1)S(1)}, u32[]{:S(2)}, u32[]{:S(2)}) %collective-permute-start.17) | collective-permute-done | bytes 65568 | tf_op jit(solution)/shard_map/ppermute | solution.py:19
  42.2 0.0 collective-permute-done.16.diagonal
  42.2 0.0 collective-permute-done.15.core
  42.2 0.8 %shard_map.103 = (bf16[256,128]{1,0:T(8,128)(2,1)}, f32[256,256]{1,0:T(8,128)}, f32[64,512]{1,0:T(8,128)}) custom-call(bf16[256,128]{1,0:T(8,128)(2,1)S(1)} %get-tuple-element.43.activated, bf16[128,256]{1,0:T(8,128)(2,1)S(1)} %collective-permute-done.15.core, bf16[128,256]{1,0:T(8,128)(2,1)S(1)} %shard_map.101.part, ...), custom_call_target="tpu_custom_call" | custom-call | flops 1024 | bytes 1024 | tf_op jit(solution)/shard_map/pallas_call | solution.py:53
  (4 shorter events, 0.1 us)
Async XLA Ops:
  0.6 9.4 %collective-permute-start.2 = (bf16[64,512]{1,0:T(8,128)(2,1)}, bf16[64,512]{1,0:T(8,128)(2,1)S(1)}, u32[]{:S(2)}, u32[]{:S(2)}) collective-permute-start(bf16[64,512]{1,0:T(8,128)(2,1)} %first.1), channel_id=1, source_target_pairs={{0,24},{4,28},{8,16},{12,20},{16,8},{20,12},{24,0},{28,4},{1,25},{... | collective-permute-start | bytes 196616 | tf_op jit(solution)/shard_map/ppermute | solution.py:19
  5.7 5.8 %collective-permute-start.1 = (bf16[64,512]{1,0:T(8,128)(2,1)}, bf16[64,512]{1,0:T(8,128)(2,1)S(1)}, u32[]{:S(2)}, u32[]{:S(2)}) collective-permute-start(bf16[64,512]{1,0:T(8,128)(2,1)} %first.1), channel_id=1, source_target_pairs={{0,16},{4,20},{8,24},{12,28},{16,0},{20,4},{24,8},{28,12},{1,17},{... | collective-permute-start | bytes 196616 | tf_op jit(solution)/shard_map/ppermute | solution.py:19
  5.7 5.8 %collective-permute-start = (bf16[64,512]{1,0:T(8,128)(2,1)}, bf16[64,512]{1,0:T(8,128)(2,1)S(1)}, u32[]{:S(2)}, u32[]{:S(2)}) collective-permute-start(bf16[64,512]{1,0:T(8,128)(2,1)} %first.1), channel_id=1, source_target_pairs={{0,8},{4,12},{8,0},{12,4},{16,24},{20,28},{24,16},{28,20},{1,9},{5... | collective-permute-start | bytes 196616 | tf_op jit(solution)/shard_map/ppermute | solution.py:19
  6.4 5.2 %collective-permute-start.3 = (bf16[64,512]{1,0:T(8,128)(2,1)}, bf16[64,512]{1,0:T(8,128)(2,1)S(1)}, u32[]{:S(2)}, u32[]{:S(2)}) collective-permute-start(bf16[64,512]{1,0:T(8,128)(2,1)} %first.1), channel_id=1, source_target_pairs={{0,4},{4,0},{8,12},{12,8},{16,20},{20,16},{24,28},{28,24},{1,5},{5... | collective-permute-start | bytes 196616 | tf_op jit(solution)/shard_map/ppermute | solution.py:19
  11.6 1.6 %copy-start.2 = (bf16[256,128]{1,0:T(8,128)(2,1)S(1)}, bf16[256,128]{1,0:T(8,128)(2,1)}, u32[]{:S(2)}) copy-start(bf16[256,128]{1,0:T(8,128)(2,1)} %refs_4_.1) | copy-start | bytes 196612
  11.6 3.1 %copy-start.1 = (bf16[64,512]{1,0:T(8,128)(2,1)S(1)}, bf16[64,512]{1,0:T(8,128)(2,1)}, u32[]{:S(2)}) copy-start(bf16[64,512]{1,0:T(8,128)(2,1)} %first.1) | copy-start | bytes 196612
  11.6 6.5 %collective-permute-start.4 = (bf16[3,64,512]{2,1,0:T(8,128)(2,1)S(1)}, bf16[3,64,512]{2,1,0:T(8,128)(2,1)S(1)}, u32[]{:S(2)}, u32[]{:S(2)}) collective-permute-start(bf16[3,64,512]{2,1,0:T(8,128)(2,1)S(1)} %shard_map.95.rest), channel_id=1, source_target_pairs={{0,4},{4,0},{8,12},{12,8},{16,20},{20,16},{24,28},{28,24},{1,5},{5... | collective-permute-start | bytes 589832 | tf_op jit(solution)/shard_map/ppermute | solution.py:19
  13.2 7.2 %collective-permute-start.9 = (bf16[256,128]{1,0:T(8,128)(2,1)S(1)}, bf16[256,128]{1,0:T(8,128)(2,1)S(1)}, u32[]{:S(2)}, u32[]{:S(2)}) collective-permute-start(bf16[256,128]{1,0:T(8,128)(2,1)S(1)} %copy-done.2), channel_id=1, source_target_pairs={{0,2},{1,3},{2,0},{3,1},{4,6},{5,7},{6,4},{7,5},{8,10},{9,11},{10,... | collective-permute-start | bytes 196616 | tf_op jit(solution)/shard_map/ppermute | solution.py:19
  15.3 8.9 %copy-start = (bf16[256,256]{1,0:T(8,128)(2,1)S(1)}, bf16[256,256]{1,0:T(8,128)(2,1)}, u32[]{:S(2)}) copy-start(bf16[256,256]{1,0:T(8,128)(2,1)} %weight.1) | copy-start | bytes 393220
  18.6 4.3 %collective-permute-start.6 = (bf16[64,512]{1,0:T(8,128)(2,1)S(1)}, bf16[64,512]{1,0:T(8,128)(2,1)S(1)}, u32[]{:S(2)}, u32[]{:S(2)}) collective-permute-start(bf16[64,512]{1,0:T(8,128)(2,1)S(1)} %shard_map.97.refs_0_), channel_id=1, source_target_pairs={{0,2},{1,3},{2,0},{3,1},{4,6},{5,7},{6,4},{7,5},{8,10},{9,11},{10,... | collective-permute-start | bytes 196616 | tf_op jit(solution)/shard_map/ppermute | solution.py:19
  20.3 2.6 %collective-permute-start.8 = (bf16[256,128]{1,0:T(8,128)(2,1)S(1)}, bf16[256,128]{1,0:T(8,128)(2,1)S(1)}, u32[]{:S(2)}, u32[]{:S(2)}) collective-permute-start(bf16[256,128]{1,0:T(8,128)(2,1)S(1)} %copy-done.2), channel_id=1, source_target_pairs={{0,1},{1,0},{2,3},{3,2},{4,5},{5,4},{6,7},{7,6},{8,9},{9,8},{10,11... | collective-permute-start | bytes 196616 | tf_op jit(solution)/shard_map/ppermute | solution.py:19
  20.3 2.6 %collective-permute-start.10 = (bf16[256,128]{1,0:T(8,128)(2,1)S(1)}, bf16[256,128]{1,0:T(8,128)(2,1)S(1)}, u32[]{:S(2)}, u32[]{:S(2)}) collective-permute-start(bf16[256,128]{1,0:T(8,128)(2,1)S(1)} %collective-permute-done.9.refs_6_), channel_id=1, source_target_pairs={{0,1},{1,0},{2,3},{3,2},{4,5},{5,4},{6,7},{7,6},{8,9},{9,8},{10,11... | collective-permute-start | bytes 196616 | tf_op jit(solution)/shard_map/ppermute | solution.py:19
  20.8 2.1 %collective-permute-start.5 = (bf16[64,512]{1,0:T(8,128)(2,1)S(1)}, bf16[64,512]{1,0:T(8,128)(2,1)S(1)}, u32[]{:S(2)}, u32[]{:S(2)}) collective-permute-start(bf16[64,512]{1,0:T(8,128)(2,1)S(1)} %shard_map.97.refs_0_), channel_id=1, source_target_pairs={{0,1},{1,0},{2,3},{3,2},{4,5},{5,4},{6,7},{7,6},{8,9},{9,8},{10,11... | collective-permute-start | bytes 196616 | tf_op jit(solution)/shard_map/ppermute | solution.py:19
  22.9 1.3 %collective-permute-start.7 = (bf16[64,512]{1,0:T(8,128)(2,1)S(1)}, bf16[64,512]{1,0:T(8,128)(2,1)S(1)}, u32[]{:S(2)}, u32[]{:S(2)}) collective-permute-start(bf16[64,512]{1,0:T(8,128)(2,1)S(1)} %collective-permute-done.6.refs_2_), channel_id=1, source_target_pairs={{0,1},{1,0},{2,3},{3,2},{4,5},{5,4},{6,7},{7,6},{8,9},{9,8},{10,11... | collective-permute-start | bytes 196616 | tf_op jit(solution)/shard_map/ppermute | solution.py:19
  25.1 7.0 %collective-permute-start.14 = (bf16[192,512]{1,0:T(8,128)(2,1)S(1)}, bf16[192,512]{1,0:T(8,128)(2,1)S(1)}, u32[]{:S(2)}, u32[]{:S(2)}) collective-permute-start(bf16[192,512]{1,0:T(8,128)(2,1)S(1)} %get-tuple-element.49), channel_id=1, source_target_pairs={{0,4},{4,0},{8,12},{12,8},{16,20},{20,16},{24,28},{28,24},{1,5},{5... | collective-permute-start | bytes 589832 | tf_op jit(solution)/shard_map/ppermute | solution.py:19
  27.2 7.6 %collective-permute-start.13 = (bf16[128,256]{1,0:T(8,128)(2,1)S(1)}, bf16[128,256]{1,0:T(8,128)(2,1)S(1)}, u32[]{:S(2)}, u32[]{:S(2)}) collective-permute-start(bf16[128,256]{1,0:T(8,128)(2,1)S(1)} %get-tuple-element.51.refs_0_), channel_id=1, source_target_pairs={{0,16},{4,20},{8,24},{12,28},{16,0},{20,4},{24,8},{28,12},{1,17},{... | collective-permute-start | bytes 196616 | tf_op jit(solution)/shard_map/ppermute | solution.py:19
  27.8 8.9 %collective-permute-start.12 = (bf16[128,256]{1,0:T(8,128)(2,1)S(1)}, bf16[128,256]{1,0:T(8,128)(2,1)S(1)}, u32[]{:S(2)}, u32[]{:S(2)}) collective-permute-start(bf16[128,256]{1,0:T(8,128)(2,1)S(1)} %get-tuple-element.51.refs_0_), channel_id=1, source_target_pairs={{0,24},{4,28},{8,16},{12,20},{16,8},{20,12},{24,0},{28,4},{1,25},{... | collective-permute-start | bytes 196616 | tf_op jit(solution)/shard_map/ppermute | solution.py:19
  29.7 7.7 %collective-permute-start.11 = (bf16[128,256]{1,0:T(8,128)(2,1)S(1)}, bf16[128,256]{1,0:T(8,128)(2,1)S(1)}, u32[]{:S(2)}, u32[]{:S(2)}) collective-permute-start(bf16[128,256]{1,0:T(8,128)(2,1)S(1)} %get-tuple-element.51.refs_0_), channel_id=1, source_target_pairs={{0,8},{4,12},{8,0},{12,4},{16,24},{20,28},{24,16},{28,20},{1,9},{5... | collective-permute-start | bytes 196616 | tf_op jit(solution)/shard_map/ppermute | solution.py:19
  32.1 5.7 %collective-permute-start.19 = (bf16[64,512]{1,0:T(8,128)(2,1)S(1)}, bf16[64,512]{1,0:T(8,128)(2,1)S(1)}, u32[]{:S(2)}, u32[]{:S(2)}) collective-permute-start(bf16[64,512]{1,0:T(8,128)(2,1)S(1)} %get-tuple-element.56), channel_id=1, source_target_pairs={{0,4},{4,0},{8,12},{12,8},{16,20},{20,16},{24,28},{28,24},{1,5},{5... | collective-permute-start | bytes 196616 | tf_op jit(solution)/shard_map/ppermute | solution.py:19
  33.9 6.3 %collective-permute-start.20 = (bf16[64,512]{1,0:T(8,128)(2,1)S(1)}, bf16[64,512]{1,0:T(8,128)(2,1)S(1)}, u32[]{:S(2)}, u32[]{:S(2)}) collective-permute-start(bf16[64,512]{1,0:T(8,128)(2,1)S(1)} %get-tuple-element.57), channel_id=1, source_target_pairs={{0,16},{4,20},{8,24},{12,28},{16,0},{20,4},{24,8},{28,12},{1,17},{... | collective-permute-start | bytes 196616 | tf_op jit(solution)/shard_map/ppermute | solution.py:19
  34.7 6.2 %collective-permute-start.21 = (bf16[64,512]{1,0:T(8,128)(2,1)S(1)}, bf16[64,512]{1,0:T(8,128)(2,1)S(1)}, u32[]{:S(2)}, u32[]{:S(2)}) collective-permute-start(bf16[64,512]{1,0:T(8,128)(2,1)S(1)} %get-tuple-element.58), channel_id=1, source_target_pairs={{0,24},{4,28},{8,16},{12,20},{16,8},{20,12},{24,0},{28,4},{1,25},{... | collective-permute-start | bytes 196616 | tf_op jit(solution)/shard_map/ppermute | solution.py:19
  36.7 4.9 %collective-permute-start.18 = (bf16[64,512]{1,0:T(8,128)(2,1)S(1)}, bf16[64,512]{1,0:T(8,128)(2,1)S(1)}, u32[]{:S(2)}, u32[]{:S(2)}) collective-permute-start(bf16[64,512]{1,0:T(8,128)(2,1)S(1)} %get-tuple-element.50), channel_id=1, source_target_pairs={{0,8},{4,12},{8,0},{12,4},{16,24},{20,28},{24,16},{28,20},{1,9},{5... | collective-permute-start | bytes 196616 | tf_op jit(solution)/shard_map/ppermute | solution.py:19
  37.4 4.8 %collective-permute-start.17 = (bf16[128,256]{1,0:T(8,128)(2,1)S(1)}, bf16[128,256]{1,0:T(8,128)(2,1)S(1)}, u32[]{:S(2)}, u32[]{:S(2)}) collective-permute-start(bf16[128,256]{1,0:T(8,128)(2,1)S(1)} %shard_map.101.part), channel_id=1, source_target_pairs={{0,4},{4,0},{8,12},{12,8},{16,20},{20,16},{24,28},{28,24},{1,5},{5... | collective-permute-start | bytes 196616 | tf_op jit(solution)/shard_map/ppermute | solution.py:19
  37.8 4.4 %collective-permute-start.16 = (bf16[128,256]{1,0:T(8,128)(2,1)S(1)}, bf16[128,256]{1,0:T(8,128)(2,1)S(1)}, u32[]{:S(2)}, u32[]{:S(2)}) collective-permute-start(bf16[128,256]{1,0:T(8,128)(2,1)S(1)} %shard_map.101.part), channel_id=1, source_target_pairs={{0,5},{1,4},{2,7},{3,6},{4,1},{5,0},{6,3},{7,2},{8,13},{9,12},{10,... | collective-permute-start | bytes 196616 | tf_op jit(solution)/shard_map/ppermute | solution.py:290
  40.2 2.1 %collective-permute-start.15 = (bf16[128,256]{1,0:T(8,128)(2,1)S(1)}, bf16[128,256]{1,0:T(8,128)(2,1)S(1)}, u32[]{:S(2)}, u32[]{:S(2)}) collective-permute-start(bf16[128,256]{1,0:T(8,128)(2,1)S(1)} %shard_map.101.part), channel_id=1, source_target_pairs={{0,1},{1,0},{2,3},{3,2},{4,5},{5,4},{6,7},{7,6},{8,9},{9,8},{10,11... | collective-permute-start | bytes 196616 | tf_op jit(solution)/shard_map/ppermute | solution.py:19

commit v7 on v6

--- a/solution.py
+++ b/solution.py
@@ -155,7 +155,7 @@
 
 def middle(values, row_masks, col_masks, weight, *refs, feat):
     aggs, cots = refs[:feat], refs[feat : 2 * feat]
-    activated, grads, mine, dpre_full, sent_own, sent, agg_full = refs[2 * feat :]
+    activated, grads, mine, dpre_full, sent, agg_full = refs[2 * feat :]
     index = lax.axis_index("feat")
     width, local = aggs[0].shape
     side = cots[0].shape[1]
@@ -173,12 +173,14 @@
     grads[...] = dot(weight[lanes(index, width), :], dpre_all, ((1,), (0,))).astype(BF16)
     mine[...] = agg_full[lanes(index & 1, mine.shape[0]), :]
     add_backward(values, row_masks, col_masks, grads, sent, 1, 1)
-    add_backward(values, row_masks, col_masks, grads, sent_own, 1, 0)
-
-
-def backward_near(values, row_masks, col_masks, grads, mine, dpre, out, weight_part):
+
+
+def backward_near(
+    values, row_masks, col_masks, grads, mine, dpre, out, weight_part, sent_own
+):
     weight_part[...] = dot(mine[...], dpre[...], ((1,), (1,))).astype(BF16)
     add_backward(values, row_masks, col_masks, grads, out, 0, 0)
+    add_backward(values, row_masks, col_masks, grads, sent_own, 1, 0)
 
 
 def add_weights(one, other, out):
@@ -249,7 +251,7 @@
         [pltpu.VMEM(totals, F32)],
     )
     aggs = gather_feat(aggregated)
-    activated, grads, mine, dpre, sent_own, sent = call(
+    activated, grads, mine, dpre, sent = call(
         functools.partial(middle, feat=feat),
         [*tiles, weight, *aggs, *cots],
         [
@@ -257,16 +259,19 @@
             shape((width, local), BF16),
             shape((wide // 2, local), BF16),
             shape((wide, local), BF16),
-            shape((width, local), BF16),
             shape(((column - 1) * width, local), BF16),
         ],
         [pltpu.VMEM((wide, local), BF16)],
     )
     got = swapped(sent, "node", 1)
-    near_grads, weight_part = call(
+    near_grads, weight_part, sent_own = call(
         backward_near,
         [*tiles, grads, mine, dpre],
-        [shape((column * width, local), F32), shape((wide // 2, wide), BF16)],
+        [
+            shape((column * width, local), F32),
+            shape((wide // 2, wide), BF16),
+            shape((width, local), BF16),
+        ],
         cost=LARGE,
     )
     parts = [weight_part] + [swapped(weight_part, "node", 2 * k) for k in range(1, column)]
@@ -280,9 +285,9 @@
     sent_own, _ = lax.optimization_barrier((sent_own, chunks[0]))
     across_own = swapped(sent_own, "node", 1)
     ordered = lax.optimization_barrier(
-        (parts[0], *[parts[k] for k in (1, 3, 2)], chunks[0])
-    )
-    parts = [ordered[0], *[ordered[k] for k in (1, 3, 2)]]
+        (parts[0], *[parts[k] for k in (3, 1, 2)], chunks[0])
+    )
+    parts = [ordered[0], *[ordered[k] for k in (2, 3, 1)]]
     (part,) = call(sum_weights, parts, [shape((wide // 2, wide), BF16)], cost=SMALL)
     core = swapped(part, "feat", 1)
     across = swapped(part, "node", 1)

time: 43.3 us -> 43.2 us (level)
  waiting for transfers between devices: 13.7 us -> 12.4 us
  starting transfers between devices: 23.4 us -> 24.6 us
    ppermute x21, waiting for transfers between devices: 13.7 us -> 12.4 us  [swapped(): lax.ppermute(x, axis, [(i, i ^ mask) for i in range(lax.axis_size(axis))])]
    ppermute x21, starting transfers between devices: 23.4 us -> 24.6 us  [swapped(): lax.ppermute(x, axis, [(i, i ^ mask) for i in range(lax.axis_size(axis))])]
  transfers between devices with their start and end apart: 22 -> 22, of which waited for: 10 -> 8; matrix products, arithmetic and copies ran while one was open for 0% -> 0% of each run, Pallas kernels for 8% -> 8%
where the time goes in v7:
time: 43.2 us; the launch traced here: 43 us
  starting transfers between devices  24.6 us (57%)
  waiting for transfers between devices  12.4 us (29%)
  Pallas kernels  5.15 us (12%)
  between operations  0.75 us (2%)
    ppermute x21, starting transfers between devices, swapped(): lax.ppermute(x, axis, [(i, i ^ mask) for i in range(lax.axis_size(axis))])  24.6 us
    ppermute x21, waiting for transfers between devices, swapped(): lax.ppermute(x, axis, [(i, i ^ mask) for i in range(lax.axis_size(axis))])  12.4 us
    pallas_call x10, Pallas kernels, call(): pl.pallas_call(body, in_specs=[SMEM] * scalars + [spec] * (len(inputs) -...  5.15 us
  transfers between devices with their start and end apart: 22, of which 8 were waited for; matrix products, arithmetic and copies ran while one was open for 0% of the time, Pallas kernels for 8%

profile of v7, /device:TPU:0, one launch (start us, length us, event | category | flops | bytes accessed | tf_op | source)
XLA Modules:
  0.0 43.0 jit_solution(8749013556284475092)
XLA Ops:
  0.6 5.1 %collective-permute-start.2 = (bf16[64,512]{1,0:T(8,128)(2,1)}, bf16[64,512]{1,0:T(8,128)(2,1)S(1)}, u32[]{:S(2)}, u32[]{:S(2)}) collective-permute-start(bf16[64,512]{1,0:T(8,128)(2,1)} %first.1), channel_id=1, source_target_pairs={{0,24},{4,28},{8,16},{12,20},{16,8},{20,12},{24,0},{28,4},{1,25},{... | collective-permute-start | bytes 196616 | tf_op jit(solution)/shard_map/ppermute | solution.py:19
  5.7 0.0 collective-permute-start.1
  5.7 0.6 %collective-permute-start = (bf16[64,512]{1,0:T(8,128)(2,1)}, bf16[64,512]{1,0:T(8,128)(2,1)S(1)}, u32[]{:S(2)}, u32[]{:S(2)}) collective-permute-start(bf16[64,512]{1,0:T(8,128)(2,1)} %first.1), channel_id=1, source_target_pairs={{0,8},{4,12},{8,0},{12,4},{16,24},{20,28},{24,16},{28,20},{1,9},{5... | collective-permute-start | bytes 196616 | tf_op jit(solution)/shard_map/ppermute | solution.py:19
  6.4 1.6 %collective-permute-start.3 = (bf16[64,512]{1,0:T(8,128)(2,1)}, bf16[64,512]{1,0:T(8,128)(2,1)S(1)}, u32[]{:S(2)}, u32[]{:S(2)}) collective-permute-start(bf16[64,512]{1,0:T(8,128)(2,1)} %first.1), channel_id=1, source_target_pairs={{0,4},{4,0},{8,12},{12,8},{16,20},{20,16},{24,28},{28,24},{1,5},{5... | collective-permute-start | bytes 196616 | tf_op jit(solution)/shard_map/ppermute | solution.py:19
  8.0 2.0 %shard_map.94 = (bf16[32,128,128]{2,1,0:T(8,128)(2,1)S(1)}, bf16[32,4,16,128]{3,2,1,0:T(8,128)(2,1)S(1)}, bf16[32,4,16,128]{3,2,1,0:T(8,128)(2,1)S(1)}) custom-call(s32[4,8]{1,0:T(4,128)} %bitcast.2, s32[4,8]{1,0:T(4,128)} %bitcast.3, s32[8]{0:T(128)} %counts.1, bf16[32,128,128]{2,1,0:T(8,128)(2,1)} %source.1), custom_call_target="tpu_custom_call" | custom-call | tf_op jit(solution)/shard_map/pallas_call | solution.py:53
  10.0 0.0 collective-permute-done.2.refs_2_
  10.0 1.6 %collective-permute-done.1.refs_1_ = bf16[64,512]{1,0:T(8,128)(2,1)S(1)} collective-permute-done((bf16[64,512]{1,0:T(8,128)(2,1)}, bf16[64,512]{1,0:T(8,128)(2,1)S(1)}, u32[]{:S(2)}, u32[]{:S(2)}) %collective-permute-start.1) | collective-permute-done | bytes 65568 | tf_op jit(solution)/shard_map/ppermute | solution.py:19
  11.6 0.0 collective-permute-done.refs_0_
  11.6 0.0 collective-permute-done.3.across
  11.6 0.0 copy-start.2
  11.6 0.0 copy-start.1
  11.6 1.6 %collective-permute-start.4 = (bf16[3,64,512]{2,1,0:T(8,128)(2,1)S(1)}, bf16[3,64,512]{2,1,0:T(8,128)(2,1)S(1)}, u32[]{:S(2)}, u32[]{:S(2)}) collective-permute-start(bf16[3,64,512]{2,1,0:T(8,128)(2,1)S(1)} %shard_map.95.rest), channel_id=1, source_target_pairs={{0,4},{4,0},{8,12},{12,8},{16,20},{20,16},{24,28},{28,24},{1,5},{5... | collective-permute-start | bytes 589832 | tf_op jit(solution)/shard_map/ppermute | solution.py:19
  13.2 0.0 copy-done.2
  13.2 1.5 %collective-permute-start.9 = (bf16[256,128]{1,0:T(8,128)(2,1)S(1)}, bf16[256,128]{1,0:T(8,128)(2,1)S(1)}, u32[]{:S(2)}, u32[]{:S(2)}) collective-permute-start(bf16[256,128]{1,0:T(8,128)(2,1)S(1)} %copy-done.2), channel_id=1, source_target_pairs={{0,2},{1,3},{2,0},{3,1},{4,6},{5,7},{6,4},{7,5},{8,10},{9,11},{10,... | collective-permute-start | bytes 196616 | tf_op jit(solution)/shard_map/ppermute | solution.py:19
  14.7 0.0 copy-done.1
  14.7 0.6 %shard_map.96.near = f32[4,64,128]{2,1,0:T(8,128)S(1)} custom-call(bf16[32,128,128]{2,1,0:T(8,128)(2,1)S(1)} %get-tuple-element.36.values, bf16[32,4,16,128]{3,2,1,0:T(8,128)(2,1)S(1)} %get-tuple-element.37.row_masks, bf16[32,4,16,128]{3,2,1,0:T(8,128)(2,1)S(1)} %get-tuple-element.38.col_masks, bf16[64,512]{1,0:T(8,128)(2,1)S(1)} %copy-done.1, ...), custom_call_target="tpu_custom_call" | custom-call | tf_op jit(solution)/shard_map/pallas_call | solution.py:53
  15.3 0.0 copy-start
  15.3 2.8 %collective-permute-done.4.rest = bf16[3,64,512]{2,1,0:T(8,128)(2,1)S(1)} collective-permute-done((bf16[3,64,512]{2,1,0:T(8,128)(2,1)S(1)}, bf16[3,64,512]{2,1,0:T(8,128)(2,1)S(1)}, u32[]{:S(2)}, u32[]{:S(2)}) %collective-permute-start.4) | collective-permute-done | bytes 196640 | tf_op jit(solution)/shard_map/ppermute | solution.py:19
  18.1 0.4 shard_map.97.refs_0_
  18.6 1.8 %collective-permute-start.6 = (bf16[64,512]{1,0:T(8,128)(2,1)S(1)}, bf16[64,512]{1,0:T(8,128)(2,1)S(1)}, u32[]{:S(2)}, u32[]{:S(2)}) collective-permute-start(bf16[64,512]{1,0:T(8,128)(2,1)S(1)} %shard_map.97.refs_0_), channel_id=1, source_target_pairs={{0,2},{1,3},{2,0},{3,1},{4,6},{5,7},{6,4},{7,5},{8,10},{9,11},{10,... | collective-permute-start | bytes 196616 | tf_op jit(solution)/shard_map/ppermute | solution.py:19
  20.3 0.0 collective-permute-start.8
  20.3 0.0 collective-permute-done.9.refs_6_
  20.3 0.5 %collective-permute-start.10 = (bf16[256,128]{1,0:T(8,128)(2,1)S(1)}, bf16[256,128]{1,0:T(8,128)(2,1)S(1)}, u32[]{:S(2)}, u32[]{:S(2)}) collective-permute-start(bf16[256,128]{1,0:T(8,128)(2,1)S(1)} %collective-permute-done.9.refs_6_), channel_id=1, source_target_pairs={{0,1},{1,0},{2,3},{3,2},{4,5},{5,4},{6,7},{7,6},{8,9},{9,8},{10,11... | collective-permute-start | bytes 196616 | tf_op jit(solution)/shard_map/ppermute | solution.py:19
  20.8 0.0 collective-permute-start.5
  20.8 2.0 %collective-permute-done.6.refs_2_ = bf16[64,512]{1,0:T(8,128)(2,1)S(1)} collective-permute-done((bf16[64,512]{1,0:T(8,128)(2,1)S(1)}, bf16[64,512]{1,0:T(8,128)(2,1)S(1)}, u32[]{:S(2)}, u32[]{:S(2)}) %collective-permute-start.6) | collective-permute-done | bytes 65568 | tf_op jit(solution)/shard_map/ppermute | solution.py:19
  22.9 0.0 collective-permute-start.7
  22.9 0.0 collective-permute-done.8.refs_5_
  22.9 0.0 collective-permute-done.10.refs_7_
  22.9 0.0 collective-permute-done.5.refs_1_
  22.9 1.2 %collective-permute-done.7.refs_3_ = bf16[64,512]{1,0:T(8,128)(2,1)S(1)} collective-permute-done((bf16[64,512]{1,0:T(8,128)(2,1)S(1)}, bf16[64,512]{1,0:T(8,128)(2,1)S(1)}, u32[]{:S(2)}, u32[]{:S(2)}) %collective-permute-start.7) | collective-permute-done | bytes 65568 | tf_op jit(solution)/shard_map/ppermute | solution.py:19
  24.1 0.0 copy-done
  24.1 0.9 %shard_map.98 = (bf16[256,128]{1,0:T(8,128)(2,1)S(1)}, bf16[64,512]{1,0:T(8,128)(2,1)S(1)}, bf16[128,512]{1,0:T(8,128)(2,1)S(1)}, bf16[256,512]{1,0:T(8,128)(2,1)S(1)}, bf16[192,512]{1,0:T(8,128)(2,1)S(1)}) custom-call(bf16[32,128,128]{2,1,0:T(8,128)(2,1)S(1)} %get-tuple-element.36.values, bf16[32,4,16,128]{3,2,1,0:T(8,128)(2,1)S(1)} %get-tuple-element.37.row_masks, ...), custom_call_target="tpu_custom_call" | custom-call | tf_op jit(solution)/shard_map/pallas_call | solution.py:53
  25.0 1.7 %collective-permute-start.14 = (bf16[192,512]{1,0:T(8,128)(2,1)S(1)}, bf16[192,512]{1,0:T(8,128)(2,1)S(1)}, u32[]{:S(2)}, u32[]{:S(2)}) collective-permute-start(bf16[192,512]{1,0:T(8,128)(2,1)S(1)} %get-tuple-element.49), channel_id=1, source_target_pairs={{0,4},{4,0},{8,12},{12,8},{16,20},{20,16},{24,28},{28,24},{1,5},{5... | collective-permute-start | bytes 589832 | tf_op jit(solution)/shard_map/ppermute | solution.py:19
  26.8 0.4 shard_map.99
  27.2 0.6 %collective-permute-start.13 = (bf16[128,256]{1,0:T(8,128)(2,1)S(1)}, bf16[128,256]{1,0:T(8,128)(2,1)S(1)}, u32[]{:S(2)}, u32[]{:S(2)}) collective-permute-start(bf16[128,256]{1,0:T(8,128)(2,1)S(1)} %get-tuple-element.51.refs_0_), channel_id=1, source_target_pairs={{0,16},{4,20},{8,24},{12,28},{16,0},{20,4},{24,8},{28,12},{1,17},{... | collective-permute-start | bytes 196616 | tf_op jit(solution)/shard_map/ppermute | solution.py:19
  27.8 2.0 %collective-permute-start.12 = (bf16[128,256]{1,0:T(8,128)(2,1)S(1)}, bf16[128,256]{1,0:T(8,128)(2,1)S(1)}, u32[]{:S(2)}, u32[]{:S(2)}) collective-permute-start(bf16[128,256]{1,0:T(8,128)(2,1)S(1)} %get-tuple-element.51.refs_0_), channel_id=1, source_target_pairs={{0,8},{4,12},{8,0},{12,4},{16,24},{20,28},{24,16},{28,20},{1,9},{5... | collective-permute-start | bytes 196616 | tf_op jit(solution)/shard_map/ppermute | solution.py:19
  29.9 1.8 %collective-permute-start.11 = (bf16[128,256]{1,0:T(8,128)(2,1)S(1)}, bf16[128,256]{1,0:T(8,128)(2,1)S(1)}, u32[]{:S(2)}, u32[]{:S(2)}) collective-permute-start(bf16[128,256]{1,0:T(8,128)(2,1)S(1)} %get-tuple-element.51.refs_0_), channel_id=1, source_target_pairs={{0,24},{4,28},{8,16},{12,20},{16,8},{20,12},{24,0},{28,4},{1,25},{... | collective-permute-start | bytes 196616 | tf_op jit(solution)/shard_map/ppermute | solution.py:19
  31.6 0.4 collective-permute-done.14.got
  32.1 1.7 %collective-permute-start.19 = (bf16[64,512]{1,0:T(8,128)(2,1)S(1)}, bf16[64,512]{1,0:T(8,128)(2,1)S(1)}, u32[]{:S(2)}, u32[]{:S(2)}) collective-permute-start(bf16[64,512]{1,0:T(8,128)(2,1)S(1)} %get-tuple-element.56), channel_id=1, source_target_pairs={{0,4},{4,0},{8,12},{12,8},{16,20},{20,16},{24,28},{28,24},{1,5},{5... | collective-permute-start | bytes 196616 | tf_op jit(solution)/shard_map/ppermute | solution.py:19
  33.8 0.6 %collective-permute-start.20 = (bf16[64,512]{1,0:T(8,128)(2,1)S(1)}, bf16[64,512]{1,0:T(8,128)(2,1)S(1)}, u32[]{:S(2)}, u32[]{:S(2)}) collective-permute-start(bf16[64,512]{1,0:T(8,128)(2,1)S(1)} %get-tuple-element.57), channel_id=1, source_target_pairs={{0,16},{4,20},{8,24},{12,28},{16,0},{20,4},{24,8},{28,12},{1,17},{... | collective-permute-start | bytes 196616 | tf_op jit(solution)/shard_map/ppermute | solution.py:19
  34.4 0.0 collective-permute-done.13.refs_2_
  34.4 1.9 %collective-permute-start.21 = (bf16[64,512]{1,0:T(8,128)(2,1)S(1)}, bf16[64,512]{1,0:T(8,128)(2,1)S(1)}, u32[]{:S(2)}, u32[]{:S(2)}) collective-permute-start(bf16[64,512]{1,0:T(8,128)(2,1)S(1)} %get-tuple-element.58), channel_id=1, source_target_pairs={{0,24},{4,28},{8,16},{12,20},{16,8},{20,12},{24,0},{28,4},{1,25},{... | collective-permute-start | bytes 196616 | tf_op jit(solution)/shard_map/ppermute | solution.py:19
  36.3 0.0 collective-permute-done.12.refs_1_
  36.3 1.1 %collective-permute-start.18 = (bf16[64,512]{1,0:T(8,128)(2,1)S(1)}, bf16[64,512]{1,0:T(8,128)(2,1)S(1)}, u32[]{:S(2)}, u32[]{:S(2)}) collective-permute-start(bf16[64,512]{1,0:T(8,128)(2,1)S(1)} %get-tuple-element.50), channel_id=1, source_target_pairs={{0,8},{4,12},{8,0},{12,4},{16,24},{20,28},{24,16},{28,20},{1,9},{5... | collective-permute-start | bytes 196616 | tf_op jit(solution)/shard_map/ppermute | solution.py:19
  37.3 0.0 collective-permute-done.11.refs_3_
  37.4 0.4 collective-permute-start.17
  37.8 0.0 collective-permute-done.19.refs_1_
  37.8 0.0 collective-permute-start.16
  37.8 3.1 %collective-permute-done.20.refs_2_ = bf16[64,512]{1,0:T(8,128)(2,1)S(1)} collective-permute-done((bf16[64,512]{1,0:T(8,128)(2,1)S(1)}, bf16[64,512]{1,0:T(8,128)(2,1)S(1)}, u32[]{:S(2)}, u32[]{:S(2)}) %collective-permute-start.20) | collective-permute-done | bytes 65568 | tf_op jit(solution)/shard_map/ppermute | solution.py:19
  40.9 0.0 collective-permute-start.15
  40.9 0.0 collective-permute-done.21.refs_3_
  40.9 0.6 %collective-permute-done.18.refs_0_ = bf16[64,512]{1,0:T(8,128)(2,1)S(1)} collective-permute-done((bf16[64,512]{1,0:T(8,128)(2,1)S(1)}, bf16[64,512]{1,0:T(8,128)(2,1)S(1)}, u32[]{:S(2)}, u32[]{:S(2)}) %collective-permute-start.18) | collective-permute-done | bytes 65568 | tf_op jit(solution)/shard_map/ppermute | solution.py:19
  41.6 0.6 %collective-permute-done.17.across = bf16[128,256]{1,0:T(8,128)(2,1)S(1)} collective-permute-done((bf16[128,256]{1,0:T(8,128)(2,1)S(1)}, bf16[128,256]{1,0:T(8,128)(2,1)S(1)}, u32[]{:S(2)}, u32[]{:S(2)}) %collective-permute-start.17) | collective-permute-done | bytes 65568 | tf_op jit(solution)/shard_map/ppermute | solution.py:19
  42.2 0.0 collective-permute-done.16.diagonal
  42.2 0.0 collective-permute-done.15.core
  42.2 0.8 %shard_map.103 = (bf16[256,128]{1,0:T(8,128)(2,1)}, f32[256,256]{1,0:T(8,128)}, f32[64,512]{1,0:T(8,128)}) custom-call(bf16[256,128]{1,0:T(8,128)(2,1)S(1)} %get-tuple-element.43.activated, bf16[128,256]{1,0:T(8,128)(2,1)S(1)} %collective-permute-done.15.core, bf16[128,256]{1,0:T(8,128)(2,1)S(1)} %shard_map.101.part, ...), custom_call_target="tpu_custom_call" | custom-call | flops 1024 | bytes 1024 | tf_op jit(solution)/shard_map/pallas_call | solution.py:53
  (4 shorter events, 0.1 us)
Async XLA Ops:
  0.6 9.4 %collective-permute-start.2 = (bf16[64,512]{1,0:T(8,128)(2,1)}, bf16[64,512]{1,0:T(8,128)(2,1)S(1)}, u32[]{:S(2)}, u32[]{:S(2)}) collective-permute-start(bf16[64,512]{1,0:T(8,128)(2,1)} %first.1), channel_id=1, source_target_pairs={{0,24},{4,28},{8,16},{12,20},{16,8},{20,12},{24,0},{28,4},{1,25},{... | collective-permute-start | bytes 196616 | tf_op jit(solution)/shard_map/ppermute | solution.py:19
  5.7 5.8 %collective-permute-start.1 = (bf16[64,512]{1,0:T(8,128)(2,1)}, bf16[64,512]{1,0:T(8,128)(2,1)S(1)}, u32[]{:S(2)}, u32[]{:S(2)}) collective-permute-start(bf16[64,512]{1,0:T(8,128)(2,1)} %first.1), channel_id=1, source_target_pairs={{0,16},{4,20},{8,24},{12,28},{16,0},{20,4},{24,8},{28,12},{1,17},{... | collective-permute-start | bytes 196616 | tf_op jit(solution)/shard_map/ppermute | solution.py:19
  5.7 5.8 %collective-permute-start = (bf16[64,512]{1,0:T(8,128)(2,1)}, bf16[64,512]{1,0:T(8,128)(2,1)S(1)}, u32[]{:S(2)}, u32[]{:S(2)}) collective-permute-start(bf16[64,512]{1,0:T(8,128)(2,1)} %first.1), channel_id=1, source_target_pairs={{0,8},{4,12},{8,0},{12,4},{16,24},{20,28},{24,16},{28,20},{1,9},{5... | collective-permute-start | bytes 196616 | tf_op jit(solution)/shard_map/ppermute | solution.py:19
  6.4 5.2 %collective-permute-start.3 = (bf16[64,512]{1,0:T(8,128)(2,1)}, bf16[64,512]{1,0:T(8,128)(2,1)S(1)}, u32[]{:S(2)}, u32[]{:S(2)}) collective-permute-start(bf16[64,512]{1,0:T(8,128)(2,1)} %first.1), channel_id=1, source_target_pairs={{0,4},{4,0},{8,12},{12,8},{16,20},{20,16},{24,28},{28,24},{1,5},{5... | collective-permute-start | bytes 196616 | tf_op jit(solution)/shard_map/ppermute | solution.py:19
  11.6 1.6 %copy-start.2 = (bf16[256,128]{1,0:T(8,128)(2,1)S(1)}, bf16[256,128]{1,0:T(8,128)(2,1)}, u32[]{:S(2)}) copy-start(bf16[256,128]{1,0:T(8,128)(2,1)} %refs_4_.1) | copy-start | bytes 196612
  11.6 3.1 %copy-start.1 = (bf16[64,512]{1,0:T(8,128)(2,1)S(1)}, bf16[64,512]{1,0:T(8,128)(2,1)}, u32[]{:S(2)}) copy-start(bf16[64,512]{1,0:T(8,128)(2,1)} %first.1) | copy-start | bytes 196612
  11.6 6.5 %collective-permute-start.4 = (bf16[3,64,512]{2,1,0:T(8,128)(2,1)S(1)}, bf16[3,64,512]{2,1,0:T(8,128)(2,1)S(1)}, u32[]{:S(2)}, u32[]{:S(2)}) collective-permute-start(bf16[3,64,512]{2,1,0:T(8,128)(2,1)S(1)} %shard_map.95.rest), channel_id=1, source_target_pairs={{0,4},{4,0},{8,12},{12,8},{16,20},{20,16},{24,28},{28,24},{1,5},{5... | collective-permute-start | bytes 589832 | tf_op jit(solution)/shard_map/ppermute | solution.py:19
  13.2 7.2 %collective-permute-start.9 = (bf16[256,128]{1,0:T(8,128)(2,1)S(1)}, bf16[256,128]{1,0:T(8,128)(2,1)S(1)}, u32[]{:S(2)}, u32[]{:S(2)}) collective-permute-start(bf16[256,128]{1,0:T(8,128)(2,1)S(1)} %copy-done.2), channel_id=1, source_target_pairs={{0,2},{1,3},{2,0},{3,1},{4,6},{5,7},{6,4},{7,5},{8,10},{9,11},{10,... | collective-permute-start | bytes 196616 | tf_op jit(solution)/shard_map/ppermute | solution.py:19
  15.3 8.9 %copy-start = (bf16[256,256]{1,0:T(8,128)(2,1)S(1)}, bf16[256,256]{1,0:T(8,128)(2,1)}, u32[]{:S(2)}) copy-start(bf16[256,256]{1,0:T(8,128)(2,1)} %weight.1) | copy-start | bytes 393220
  18.6 4.3 %collective-permute-start.6 = (bf16[64,512]{1,0:T(8,128)(2,1)S(1)}, bf16[64,512]{1,0:T(8,128)(2,1)S(1)}, u32[]{:S(2)}, u32[]{:S(2)}) collective-permute-start(bf16[64,512]{1,0:T(8,128)(2,1)S(1)} %shard_map.97.refs_0_), channel_id=1, source_target_pairs={{0,2},{1,3},{2,0},{3,1},{4,6},{5,7},{6,4},{7,5},{8,10},{9,11},{10,... | collective-permute-start | bytes 196616 | tf_op jit(solution)/shard_map/ppermute | solution.py:19
  20.3 2.6 %collective-permute-start.8 = (bf16[256,128]{1,0:T(8,128)(2,1)S(1)}, bf16[256,128]{1,0:T(8,128)(2,1)S(1)}, u32[]{:S(2)}, u32[]{:S(2)}) collective-permute-start(bf16[256,128]{1,0:T(8,128)(2,1)S(1)} %copy-done.2), channel_id=1, source_target_pairs={{0,1},{1,0},{2,3},{3,2},{4,5},{5,4},{6,7},{7,6},{8,9},{9,8},{10,11... | collective-permute-start | bytes 196616 | tf_op jit(solution)/shard_map/ppermute | solution.py:19
  20.3 2.6 %collective-permute-start.10 = (bf16[256,128]{1,0:T(8,128)(2,1)S(1)}, bf16[256,128]{1,0:T(8,128)(2,1)S(1)}, u32[]{:S(2)}, u32[]{:S(2)}) collective-permute-start(bf16[256,128]{1,0:T(8,128)(2,1)S(1)} %collective-permute-done.9.refs_6_), channel_id=1, source_target_pairs={{0,1},{1,0},{2,3},{3,2},{4,5},{5,4},{6,7},{7,6},{8,9},{9,8},{10,11... | collective-permute-start | bytes 196616 | tf_op jit(solution)/shard_map/ppermute | solution.py:19
  20.8 2.1 %collective-permute-start.5 = (bf16[64,512]{1,0:T(8,128)(2,1)S(1)}, bf16[64,512]{1,0:T(8,128)(2,1)S(1)}, u32[]{:S(2)}, u32[]{:S(2)}) collective-permute-start(bf16[64,512]{1,0:T(8,128)(2,1)S(1)} %shard_map.97.refs_0_), channel_id=1, source_target_pairs={{0,1},{1,0},{2,3},{3,2},{4,5},{5,4},{6,7},{7,6},{8,9},{9,8},{10,11... | collective-permute-start | bytes 196616 | tf_op jit(solution)/shard_map/ppermute | solution.py:19
  22.9 1.3 %collective-permute-start.7 = (bf16[64,512]{1,0:T(8,128)(2,1)S(1)}, bf16[64,512]{1,0:T(8,128)(2,1)S(1)}, u32[]{:S(2)}, u32[]{:S(2)}) collective-permute-start(bf16[64,512]{1,0:T(8,128)(2,1)S(1)} %collective-permute-done.6.refs_2_), channel_id=1, source_target_pairs={{0,1},{1,0},{2,3},{3,2},{4,5},{5,4},{6,7},{7,6},{8,9},{9,8},{10,11... | collective-permute-start | bytes 196616 | tf_op jit(solution)/shard_map/ppermute | solution.py:19
  25.0 7.0 %collective-permute-start.14 = (bf16[192,512]{1,0:T(8,128)(2,1)S(1)}, bf16[192,512]{1,0:T(8,128)(2,1)S(1)}, u32[]{:S(2)}, u32[]{:S(2)}) collective-permute-start(bf16[192,512]{1,0:T(8,128)(2,1)S(1)} %get-tuple-element.49), channel_id=1, source_target_pairs={{0,4},{4,0},{8,12},{12,8},{16,20},{20,16},{24,28},{28,24},{1,5},{5... | collective-permute-start | bytes 589832 | tf_op jit(solution)/shard_map/ppermute | solution.py:19
  27.2 7.2 %collective-permute-start.13 = (bf16[128,256]{1,0:T(8,128)(2,1)S(1)}, bf16[128,256]{1,0:T(8,128)(2,1)S(1)}, u32[]{:S(2)}, u32[]{:S(2)}) collective-permute-start(bf16[128,256]{1,0:T(8,128)(2,1)S(1)} %get-tuple-element.51.refs_0_), channel_id=1, source_target_pairs={{0,16},{4,20},{8,24},{12,28},{16,0},{20,4},{24,8},{28,12},{1,17},{... | collective-permute-start | bytes 196616 | tf_op jit(solution)/shard_map/ppermute | solution.py:19
  27.8 8.4 %collective-permute-start.12 = (bf16[128,256]{1,0:T(8,128)(2,1)S(1)}, bf16[128,256]{1,0:T(8,128)(2,1)S(1)}, u32[]{:S(2)}, u32[]{:S(2)}) collective-permute-start(bf16[128,256]{1,0:T(8,128)(2,1)S(1)} %get-tuple-element.51.refs_0_), channel_id=1, source_target_pairs={{0,8},{4,12},{8,0},{12,4},{16,24},{20,28},{24,16},{28,20},{1,9},{5... | collective-permute-start | bytes 196616 | tf_op jit(solution)/shard_map/ppermute | solution.py:19
  29.9 7.5 %collective-permute-start.11 = (bf16[128,256]{1,0:T(8,128)(2,1)S(1)}, bf16[128,256]{1,0:T(8,128)(2,1)S(1)}, u32[]{:S(2)}, u32[]{:S(2)}) collective-permute-start(bf16[128,256]{1,0:T(8,128)(2,1)S(1)} %get-tuple-element.51.refs_0_), channel_id=1, source_target_pairs={{0,24},{4,28},{8,16},{12,20},{16,8},{20,12},{24,0},{28,4},{1,25},{... | collective-permute-start | bytes 196616 | tf_op jit(solution)/shard_map/ppermute | solution.py:19
  32.1 5.7 %collective-permute-start.19 = (bf16[64,512]{1,0:T(8,128)(2,1)S(1)}, bf16[64,512]{1,0:T(8,128)(2,1)S(1)}, u32[]{:S(2)}, u32[]{:S(2)}) collective-permute-start(bf16[64,512]{1,0:T(8,128)(2,1)S(1)} %get-tuple-element.56), channel_id=1, source_target_pairs={{0,4},{4,0},{8,12},{12,8},{16,20},{20,16},{24,28},{28,24},{1,5},{5... | collective-permute-start | bytes 196616 | tf_op jit(solution)/shard_map/ppermute | solution.py:19
  33.8 7.1 %collective-permute-start.20 = (bf16[64,512]{1,0:T(8,128)(2,1)S(1)}, bf16[64,512]{1,0:T(8,128)(2,1)S(1)}, u32[]{:S(2)}, u32[]{:S(2)}) collective-permute-start(bf16[64,512]{1,0:T(8,128)(2,1)S(1)} %get-tuple-element.57), channel_id=1, source_target_pairs={{0,16},{4,20},{8,24},{12,28},{16,0},{20,4},{24,8},{28,12},{1,17},{... | collective-permute-start | bytes 196616 | tf_op jit(solution)/shard_map/ppermute | solution.py:19
  34.4 6.5 %collective-permute-start.21 = (bf16[64,512]{1,0:T(8,128)(2,1)S(1)}, bf16[64,512]{1,0:T(8,128)(2,1)S(1)}, u32[]{:S(2)}, u32[]{:S(2)}) collective-permute-start(bf16[64,512]{1,0:T(8,128)(2,1)S(1)} %get-tuple-element.58), channel_id=1, source_target_pairs={{0,24},{4,28},{8,16},{12,20},{16,8},{20,12},{24,0},{28,4},{1,25},{... | collective-permute-start | bytes 196616 | tf_op jit(solution)/shard_map/ppermute | solution.py:19
  36.3 5.3 %collective-permute-start.18 = (bf16[64,512]{1,0:T(8,128)(2,1)S(1)}, bf16[64,512]{1,0:T(8,128)(2,1)S(1)}, u32[]{:S(2)}, u32[]{:S(2)}) collective-permute-start(bf16[64,512]{1,0:T(8,128)(2,1)S(1)} %get-tuple-element.50), channel_id=1, source_target_pairs={{0,8},{4,12},{8,0},{12,4},{16,24},{20,28},{24,16},{28,20},{1,9},{5... | collective-permute-start | bytes 196616 | tf_op jit(solution)/shard_map/ppermute | solution.py:19
  37.4 4.8 %collective-permute-start.17 = (bf16[128,256]{1,0:T(8,128)(2,1)S(1)}, bf16[128,256]{1,0:T(8,128)(2,1)S(1)}, u32[]{:S(2)}, u32[]{:S(2)}) collective-permute-start(bf16[128,256]{1,0:T(8,128)(2,1)S(1)} %shard_map.101.part), channel_id=1, source_target_pairs={{0,4},{4,0},{8,12},{12,8},{16,20},{20,16},{24,28},{28,24},{1,5},{5... | collective-permute-start | bytes 196616 | tf_op jit(solution)/shard_map/ppermute | solution.py:19
  37.8 4.4 %collective-permute-start.16 = (bf16[128,256]{1,0:T(8,128)(2,1)S(1)}, bf16[128,256]{1,0:T(8,128)(2,1)S(1)}, u32[]{:S(2)}, u32[]{:S(2)}) collective-permute-start(bf16[128,256]{1,0:T(8,128)(2,1)S(1)} %shard_map.101.part), channel_id=1, source_target_pairs={{0,5},{1,4},{2,7},{3,6},{4,1},{5,0},{6,3},{7,2},{8,13},{9,12},{10,... | collective-permute-start | bytes 196616 | tf_op jit(solution)/shard_map/ppermute | solution.py:295
  40.9 1.3 %collective-permute-start.15 = (bf16[128,256]{1,0:T(8,128)(2,1)S(1)}, bf16[128,256]{1,0:T(8,128)(2,1)S(1)}, u32[]{:S(2)}, u32[]{:S(2)}) collective-permute-start(bf16[128,256]{1,0:T(8,128)(2,1)S(1)} %shard_map.101.part), channel_id=1, source_target_pairs={{0,1},{1,0},{2,3},{3,2},{4,5},{5,4},{6,7},{7,6},{8,9},{9,8},{10,11... | collective-permute-start | bytes 196616 | tf_op jit(solution)/shard_map/ppermute | solution.py:19

commit v8 on v6

--- a/solution.py
+++ b/solution.py
@@ -234,7 +234,10 @@
         [pltpu.SemaphoreType.DMA],
         spec=pl.BlockSpec(memory_space=pltpu.HBM),
     )
-    *pieces, own_across, t0, t1, t2 = lax.optimization_barrier((*pieces, own_across, *tiles))
+    *ordered, own_across, t0, t1, t2 = lax.optimization_barrier(
+        (*[pieces[k] for k in (1, 0, 2)], own_across, *tiles)
+    )
+    pieces = [ordered[k] for k in (1, 0, 2)]
     tiles = (t0, t1, t2)
     (pieces,) = call(stack, pieces, [shape((column - 1, width, local), BF16)])
     far_pieces = swapped(pieces, "node", 1)

time: 43.3 us -> 43.2 us (level)
  starting transfers between devices: 23.4 us -> 24.5 us
  waiting for transfers between devices: 13.7 us -> 12.6 us
    ppermute x21, waiting for transfers between devices: 13.7 us -> 12.6 us  [swapped(): lax.ppermute(x, axis, [(i, i ^ mask) for i in range(lax.axis_size(axis))])]
    ppermute x21, starting transfers between devices: 23.4 us -> 24.5 us  [swapped(): lax.ppermute(x, axis, [(i, i ^ mask) for i in range(lax.axis_size(axis))])]
where the time goes in v8:
time: 43.2 us; the launch traced here: 43 us
  starting transfers between devices  24.5 us (57%)
  waiting for transfers between devices  12.6 us (29%)
  Pallas kernels  5.15 us (12%)
  between operations  0.74 us (2%)
    ppermute x21, starting transfers between devices, swapped(): lax.ppermute(x, axis, [(i, i ^ mask) for i in range(lax.axis_size(axis))])  24.5 us
    ppermute x21, waiting for transfers between devices, swapped(): lax.ppermute(x, axis, [(i, i ^ mask) for i in range(lax.axis_size(axis))])  12.6 us
    pallas_call x10, Pallas kernels, call(): pl.pallas_call(body, in_specs=[SMEM] * scalars + [spec] * (len(inputs) -...  5.15 us
  transfers between devices with their start and end apart: 22, of which 10 were waited for; matrix products, arithmetic and copies ran while one was open for 0% of the time, Pallas kernels for 8%

profile of v8, /device:TPU:0, one launch (start us, length us, event | category | flops | bytes accessed | tf_op | source)
XLA Modules:
  0.0 43.0 jit_solution(5131975273993485406)
XLA Ops:
  0.6 5.1 %collective-permute-start.2 = (bf16[64,512]{1,0:T(8,128)(2,1)}, bf16[64,512]{1,0:T(8,128)(2,1)S(1)}, u32[]{:S(2)}, u32[]{:S(2)}) collective-permute-start(bf16[64,512]{1,0:T(8,128)(2,1)} %first.1), channel_id=1, source_target_pairs={{0,24},{4,28},{8,16},{12,20},{16,8},{20,12},{24,0},{28,4},{1,25},{... | collective-permute-start | bytes 196616 | tf_op jit(solution)/shard_map/ppermute | solution.py:19
  5.7 0.0 collective-permute-start.1
  5.7 0.6 %collective-permute-start = (bf16[64,512]{1,0:T(8,128)(2,1)}, bf16[64,512]{1,0:T(8,128)(2,1)S(1)}, u32[]{:S(2)}, u32[]{:S(2)}) collective-permute-start(bf16[64,512]{1,0:T(8,128)(2,1)} %first.1), channel_id=1, source_target_pairs={{0,16},{4,20},{8,24},{12,28},{16,0},{20,4},{24,8},{28,12},{1,17},{... | collective-permute-start | bytes 196616 | tf_op jit(solution)/shard_map/ppermute | solution.py:19
  6.4 1.6 %collective-permute-start.3 = (bf16[64,512]{1,0:T(8,128)(2,1)}, bf16[64,512]{1,0:T(8,128)(2,1)S(1)}, u32[]{:S(2)}, u32[]{:S(2)}) collective-permute-start(bf16[64,512]{1,0:T(8,128)(2,1)} %first.1), channel_id=1, source_target_pairs={{0,4},{4,0},{8,12},{12,8},{16,20},{20,16},{24,28},{28,24},{1,5},{5... | collective-permute-start | bytes 196616 | tf_op jit(solution)/shard_map/ppermute | solution.py:19
  8.0 2.0 %shard_map.94 = (bf16[32,128,128]{2,1,0:T(8,128)(2,1)S(1)}, bf16[32,4,16,128]{3,2,1,0:T(8,128)(2,1)S(1)}, bf16[32,4,16,128]{3,2,1,0:T(8,128)(2,1)S(1)}) custom-call(s32[4,8]{1,0:T(4,128)} %bitcast.2, s32[4,8]{1,0:T(4,128)} %bitcast.3, s32[8]{0:T(128)} %counts.1, bf16[32,128,128]{2,1,0:T(8,128)(2,1)} %source.1), custom_call_target="tpu_custom_call" | custom-call | tf_op jit(solution)/shard_map/pallas_call | solution.py:53
  10.0 0.0 collective-permute-done.2.refs_2_
  10.0 0.6 %collective-permute-done.1.refs_0_ = bf16[64,512]{1,0:T(8,128)(2,1)S(1)} collective-permute-done((bf16[64,512]{1,0:T(8,128)(2,1)}, bf16[64,512]{1,0:T(8,128)(2,1)S(1)}, u32[]{:S(2)}, u32[]{:S(2)}) %collective-permute-start.1) | collective-permute-done | bytes 65568 | tf_op jit(solution)/shard_map/ppermute | solution.py:19
  10.6 1.0 %collective-permute-done.refs_1_ = bf16[64,512]{1,0:T(8,128)(2,1)S(1)} collective-permute-done((bf16[64,512]{1,0:T(8,128)(2,1)}, bf16[64,512]{1,0:T(8,128)(2,1)S(1)}, u32[]{:S(2)}, u32[]{:S(2)}) %collective-permute-start) | collective-permute-done | bytes 65568 | tf_op jit(solution)/shard_map/ppermute | solution.py:19
  11.6 0.0 collective-permute-done.3.across
  11.6 0.0 copy-start.2
  11.6 0.0 copy-start.1
  11.6 1.6 %collective-permute-start.4 = (bf16[3,64,512]{2,1,0:T(8,128)(2,1)S(1)}, bf16[3,64,512]{2,1,0:T(8,128)(2,1)S(1)}, u32[]{:S(2)}, u32[]{:S(2)}) collective-permute-start(bf16[3,64,512]{2,1,0:T(8,128)(2,1)S(1)} %shard_map.95.rest), channel_id=1, source_target_pairs={{0,4},{4,0},{8,12},{12,8},{16,20},{20,16},{24,28},{28,24},{1,5},{5... | collective-permute-start | bytes 589832 | tf_op jit(solution)/shard_map/ppermute | solution.py:19
  13.2 0.0 copy-done.2
  13.2 1.5 %collective-permute-start.9 = (bf16[256,128]{1,0:T(8,128)(2,1)S(1)}, bf16[256,128]{1,0:T(8,128)(2,1)S(1)}, u32[]{:S(2)}, u32[]{:S(2)}) collective-permute-start(bf16[256,128]{1,0:T(8,128)(2,1)S(1)} %copy-done.2), channel_id=1, source_target_pairs={{0,2},{1,3},{2,0},{3,1},{4,6},{5,7},{6,4},{7,5},{8,10},{9,11},{10,... | collective-permute-start | bytes 196616 | tf_op jit(solution)/shard_map/ppermute | solution.py:19
  14.7 0.0 copy-done.1
  14.7 0.6 %shard_map.96.near = f32[4,64,128]{2,1,0:T(8,128)S(1)} custom-call(bf16[32,128,128]{2,1,0:T(8,128)(2,1)S(1)} %get-tuple-element.36.values, bf16[32,4,16,128]{3,2,1,0:T(8,128)(2,1)S(1)} %get-tuple-element.37.row_masks, bf16[32,4,16,128]{3,2,1,0:T(8,128)(2,1)S(1)} %get-tuple-element.38.col_masks, bf16[64,512]{1,0:T(8,128)(2,1)S(1)} %copy-done.1, ...), custom_call_target="tpu_custom_call" | custom-call | tf_op jit(solution)/shard_map/pallas_call | solution.py:53
  15.3 0.0 copy-start
  15.3 2.1 %collective-permute-done.4.rest = bf16[3,64,512]{2,1,0:T(8,128)(2,1)S(1)} collective-permute-done((bf16[3,64,512]{2,1,0:T(8,128)(2,1)S(1)}, bf16[3,64,512]{2,1,0:T(8,128)(2,1)S(1)}, u32[]{:S(2)}, u32[]{:S(2)}) %collective-permute-start.4) | collective-permute-done | bytes 196640 | tf_op jit(solution)/shard_map/ppermute | solution.py:19
  17.4 0.4 shard_map.97.refs_0_
  17.8 1.6 %collective-permute-start.6 = (bf16[64,512]{1,0:T(8,128)(2,1)S(1)}, bf16[64,512]{1,0:T(8,128)(2,1)S(1)}, u32[]{:S(2)}, u32[]{:S(2)}) collective-permute-start(bf16[64,512]{1,0:T(8,128)(2,1)S(1)} %shard_map.97.refs_0_), channel_id=1, source_target_pairs={{0,2},{1,3},{2,0},{3,1},{4,6},{5,7},{6,4},{7,5},{8,10},{9,11},{10,... | collective-permute-start | bytes 196616 | tf_op jit(solution)/shard_map/ppermute | solution.py:19
  19.3 0.0 collective-permute-start.8
  19.4 0.0 collective-permute-done.9.refs_6_
  19.4 0.5 %collective-permute-start.10 = (bf16[256,128]{1,0:T(8,128)(2,1)S(1)}, bf16[256,128]{1,0:T(8,128)(2,1)S(1)}, u32[]{:S(2)}, u32[]{:S(2)}) collective-permute-start(bf16[256,128]{1,0:T(8,128)(2,1)S(1)} %collective-permute-done.9.refs_6_), channel_id=1, source_target_pairs={{0,1},{1,0},{2,3},{3,2},{4,5},{5,4},{6,7},{7,6},{8,9},{9,8},{10,11... | collective-permute-start | bytes 196616 | tf_op jit(solution)/shard_map/ppermute | solution.py:19
  19.9 0.0 collective-permute-start.5
  19.9 2.2 %collective-permute-done.6.refs_2_ = bf16[64,512]{1,0:T(8,128)(2,1)S(1)} collective-permute-done((bf16[64,512]{1,0:T(8,128)(2,1)S(1)}, bf16[64,512]{1,0:T(8,128)(2,1)S(1)}, u32[]{:S(2)}, u32[]{:S(2)}) %collective-permute-start.6) | collective-permute-done | bytes 65568 | tf_op jit(solution)/shard_map/ppermute | solution.py:19
  22.1 0.0 collective-permute-start.7
  22.1 0.0 collective-permute-done.8.refs_5_
  22.1 0.0 collective-permute-done.10.refs_7_
  22.1 0.0 collective-permute-done.5.refs_1_
  22.1 1.2 %collective-permute-done.7.refs_3_ = bf16[64,512]{1,0:T(8,128)(2,1)S(1)} collective-permute-done((bf16[64,512]{1,0:T(8,128)(2,1)S(1)}, bf16[64,512]{1,0:T(8,128)(2,1)S(1)}, u32[]{:S(2)}, u32[]{:S(2)}) %collective-permute-start.7) | collective-permute-done | bytes 65568 | tf_op jit(solution)/shard_map/ppermute | solution.py:19
  23.4 0.0 copy-done
  23.4 0.9 %shard_map.98 = (bf16[256,128]{1,0:T(8,128)(2,1)S(1)}, bf16[64,512]{1,0:T(8,128)(2,1)S(1)}, bf16[128,512]{1,0:T(8,128)(2,1)S(1)}, bf16[256,512]{1,0:T(8,128)(2,1...) custom-call(bf16[32,128,128]{2,1,0:T(8,128)(2,1)S(1)} %get-tuple-element.36.values, ...), custom_call_target="tpu_custom_call" | custom-call | tf_op jit(solution)/shard_map/pallas_call | solution.py:53
  24.3 1.6 %collective-permute-start.14 = (bf16[192,512]{1,0:T(8,128)(2,1)S(1)}, bf16[192,512]{1,0:T(8,128)(2,1)S(1)}, u32[]{:S(2)}, u32[]{:S(2)}) collective-permute-start(bf16[192,512]{1,0:T(8,128)(2,1)S(1)} %get-tuple-element.49), channel_id=1, source_target_pairs={{0,4},{4,0},{8,12},{12,8},{16,20},{20,16},{24,28},{28,24},{1,5},{5... | collective-permute-start | bytes 589832 | tf_op jit(solution)/shard_map/ppermute | solution.py:19
  25.8 0.4 shard_map.99
  26.2 2.0 %collective-permute-start.13 = (bf16[128,256]{1,0:T(8,128)(2,1)S(1)}, bf16[128,256]{1,0:T(8,128)(2,1)S(1)}, u32[]{:S(2)}, u32[]{:S(2)}) collective-permute-start(bf16[128,256]{1,0:T(8,128)(2,1)S(1)} %get-tuple-element.51.refs_0_), channel_id=1, source_target_pairs={{0,16},{4,20},{8,24},{12,28},{16,0},{20,4},{24,8},{28,12},{1,17},{... | collective-permute-start | bytes 196616 | tf_op jit(solution)/shard_map/ppermute | solution.py:19
  28.2 2.0 %collective-permute-start.12 = (bf16[128,256]{1,0:T(8,128)(2,1)S(1)}, bf16[128,256]{1,0:T(8,128)(2,1)S(1)}, u32[]{:S(2)}, u32[]{:S(2)}) collective-permute-start(bf16[128,256]{1,0:T(8,128)(2,1)S(1)} %get-tuple-element.51.refs_0_), channel_id=1, source_target_pairs={{0,24},{4,28},{8,16},{12,20},{16,8},{20,12},{24,0},{28,4},{1,25},{... | collective-permute-start | bytes 196616 | tf_op jit(solution)/shard_map/ppermute | solution.py:19
  30.2 0.0 collective-permute-start.11
  30.2 1.1 %collective-permute-done.14.got = bf16[192,512]{1,0:T(8,128)(2,1)S(1)} collective-permute-done((bf16[192,512]{1,0:T(8,128)(2,1)S(1)}, bf16[192,512]{1,0:T(8,128)(2,1)S(1)}, u32[]{:S(2)}, u32[]{:S(2)}) %collective-permute-start.14) | collective-permute-done | bytes 196640 | tf_op jit(solution)/shard_map/ppermute | solution.py:19
  31.3 1.6 %collective-permute-start.19 = (bf16[64,512]{1,0:T(8,128)(2,1)S(1)}, bf16[64,512]{1,0:T(8,128)(2,1)S(1)}, u32[]{:S(2)}, u32[]{:S(2)}) collective-permute-start(bf16[64,512]{1,0:T(8,128)(2,1)S(1)} %get-tuple-element.56), channel_id=1, source_target_pairs={{0,4},{4,0},{8,12},{12,8},{16,20},{20,16},{24,28},{28,24},{1,5},{5... | collective-permute-start | bytes 196616 | tf_op jit(solution)/shard_map/ppermute | solution.py:19
  32.9 2.0 %collective-permute-start.20 = (bf16[64,512]{1,0:T(8,128)(2,1)S(1)}, bf16[64,512]{1,0:T(8,128)(2,1)S(1)}, u32[]{:S(2)}, u32[]{:S(2)}) collective-permute-start(bf16[64,512]{1,0:T(8,128)(2,1)S(1)} %get-tuple-element.57), channel_id=1, source_target_pairs={{0,16},{4,20},{8,24},{12,28},{16,0},{20,4},{24,8},{28,12},{1,17},{... | collective-permute-start | bytes 196616 | tf_op jit(solution)/shard_map/ppermute | solution.py:19
  34.8 0.0 collective-permute-done.13.refs_2_
  34.9 2.3 %collective-permute-start.21 = (bf16[64,512]{1,0:T(8,128)(2,1)S(1)}, bf16[64,512]{1,0:T(8,128)(2,1)S(1)}, u32[]{:S(2)}, u32[]{:S(2)}) collective-permute-start(bf16[64,512]{1,0:T(8,128)(2,1)S(1)} %get-tuple-element.58), channel_id=1, source_target_pairs={{0,24},{4,28},{8,16},{12,20},{16,8},{20,12},{24,0},{28,4},{1,25},{... | collective-permute-start | bytes 196616 | tf_op jit(solution)/shard_map/ppermute | solution.py:19
  37.1 0.0 collective-permute-done.12.refs_3_
  37.1 0.0 collective-permute-start.18
  37.1 0.0 collective-permute-done.11.refs_1_
  37.2 0.6 %collective-permute-start.17 = (bf16[128,256]{1,0:T(8,128)(2,1)S(1)}, bf16[128,256]{1,0:T(8,128)(2,1)S(1)}, u32[]{:S(2)}, u32[]{:S(2)}) collective-permute-start(bf16[128,256]{1,0:T(8,128)(2,1)S(1)} %shard_map.101.part), channel_id=1, source_target_pairs={{0,4},{4,0},{8,12},{12,8},{16,20},{20,16},{24,28},{28,24},{1,5},{5... | collective-permute-start | bytes 196616 | tf_op jit(solution)/shard_map/ppermute | solution.py:19
  37.8 0.0 collective-permute-done.19.refs_1_
  37.8 0.0 collective-permute-start.16
  37.8 2.3 %collective-permute-done.20.refs_2_ = bf16[64,512]{1,0:T(8,128)(2,1)S(1)} collective-permute-done((bf16[64,512]{1,0:T(8,128)(2,1)S(1)}, bf16[64,512]{1,0:T(8,128)(2,1)S(1)}, u32[]{:S(2)}, u32[]{:S(2)}) %collective-permute-start.20) | collective-permute-done | bytes 65568 | tf_op jit(solution)/shard_map/ppermute | solution.py:19
  40.1 0.0 collective-permute-start.15
  40.1 0.9 %collective-permute-done.21.refs_3_ = bf16[64,512]{1,0:T(8,128)(2,1)S(1)} collective-permute-done((bf16[64,512]{1,0:T(8,128)(2,1)S(1)}, bf16[64,512]{1,0:T(8,128)(2,1)S(1)}, u32[]{:S(2)}, u32[]{:S(2)}) %collective-permute-start.21) | collective-permute-done | bytes 65568 | tf_op jit(solution)/shard_map/ppermute | solution.py:19
  41.0 0.7 %collective-permute-done.18.refs_0_ = bf16[64,512]{1,0:T(8,128)(2,1)S(1)} collective-permute-done((bf16[64,512]{1,0:T(8,128)(2,1)S(1)}, bf16[64,512]{1,0:T(8,128)(2,1)S(1)}, u32[]{:S(2)}, u32[]{:S(2)}) %collective-permute-start.18) | collective-permute-done | bytes 65568 | tf_op jit(solution)/shard_map/ppermute | solution.py:19
  41.7 0.4 %collective-permute-done.17.across = bf16[128,256]{1,0:T(8,128)(2,1)S(1)} collective-permute-done((bf16[128,256]{1,0:T(8,128)(2,1)S(1)}, bf16[128,256]{1,0:T(8,128)(2,1)S(1)}, u32[]{:S(2)}, u32[]{:S(2)}) %collective-permute-start.17) | collective-permute-done | bytes 65568 | tf_op jit(solution)/shard_map/ppermute | solution.py:19
  42.2 0.0 collective-permute-done.16.diagonal
  42.2 0.0 collective-permute-done.15.core
  42.2 0.8 %shard_map.103 = (bf16[256,128]{1,0:T(8,128)(2,1)}, f32[256,256]{1,0:T(8,128)}, f32[64,512]{1,0:T(8,128)}) custom-call(bf16[256,128]{1,0:T(8,128)(2,1)S(1)} %get-tuple-element.43.activated, bf16[128,256]{1,0:T(8,128)(2,1)S(1)} %collective-permute-done.15.core, bf16[128,256]{1,0:T(8,128)(2,1)S(1)} %shard_map.101.part, ...), custom_call_target="tpu_custom_call" | custom-call | flops 1024 | bytes 1024 | tf_op jit(solution)/shard_map/pallas_call | solution.py:53
  (4 shorter events, 0.1 us)
Async XLA Ops:
  0.6 9.4 %collective-permute-start.2 = (bf16[64,512]{1,0:T(8,128)(2,1)}, bf16[64,512]{1,0:T(8,128)(2,1)S(1)}, u32[]{:S(2)}, u32[]{:S(2)}) collective-permute-start(bf16[64,512]{1,0:T(8,128)(2,1)} %first.1), channel_id=1, source_target_pairs={{0,24},{4,28},{8,16},{12,20},{16,8},{20,12},{24,0},{28,4},{1,25},{... | collective-permute-start | bytes 196616 | tf_op jit(solution)/shard_map/ppermute | solution.py:19
  5.7 4.9 %collective-permute-start.1 = (bf16[64,512]{1,0:T(8,128)(2,1)}, bf16[64,512]{1,0:T(8,128)(2,1)S(1)}, u32[]{:S(2)}, u32[]{:S(2)}) collective-permute-start(bf16[64,512]{1,0:T(8,128)(2,1)} %first.1), channel_id=1, source_target_pairs={{0,8},{4,12},{8,0},{12,4},{16,24},{20,28},{24,16},{28,20},{1,9},{5... | collective-permute-start | bytes 196616 | tf_op jit(solution)/shard_map/ppermute | solution.py:19
  5.7 5.8 %collective-permute-start = (bf16[64,512]{1,0:T(8,128)(2,1)}, bf16[64,512]{1,0:T(8,128)(2,1)S(1)}, u32[]{:S(2)}, u32[]{:S(2)}) collective-permute-start(bf16[64,512]{1,0:T(8,128)(2,1)} %first.1), channel_id=1, source_target_pairs={{0,16},{4,20},{8,24},{12,28},{16,0},{20,4},{24,8},{28,12},{1,17},{... | collective-permute-start | bytes 196616 | tf_op jit(solution)/shard_map/ppermute | solution.py:19
  6.4 5.2 %collective-permute-start.3 = (bf16[64,512]{1,0:T(8,128)(2,1)}, bf16[64,512]{1,0:T(8,128)(2,1)S(1)}, u32[]{:S(2)}, u32[]{:S(2)}) collective-permute-start(bf16[64,512]{1,0:T(8,128)(2,1)} %first.1), channel_id=1, source_target_pairs={{0,4},{4,0},{8,12},{12,8},{16,20},{20,16},{24,28},{28,24},{1,5},{5... | collective-permute-start | bytes 196616 | tf_op jit(solution)/shard_map/ppermute | solution.py:19
  11.6 1.6 %copy-start.2 = (bf16[256,128]{1,0:T(8,128)(2,1)S(1)}, bf16[256,128]{1,0:T(8,128)(2,1)}, u32[]{:S(2)}) copy-start(bf16[256,128]{1,0:T(8,128)(2,1)} %refs_4_.1) | copy-start | bytes 196612
  11.6 3.1 %copy-start.1 = (bf16[64,512]{1,0:T(8,128)(2,1)S(1)}, bf16[64,512]{1,0:T(8,128)(2,1)}, u32[]{:S(2)}) copy-start(bf16[64,512]{1,0:T(8,128)(2,1)} %first.1) | copy-start | bytes 196612
  11.6 5.7 %collective-permute-start.4 = (bf16[3,64,512]{2,1,0:T(8,128)(2,1)S(1)}, bf16[3,64,512]{2,1,0:T(8,128)(2,1)S(1)}, u32[]{:S(2)}, u32[]{:S(2)}) collective-permute-start(bf16[3,64,512]{2,1,0:T(8,128)(2,1)S(1)} %shard_map.95.rest), channel_id=1, source_target_pairs={{0,4},{4,0},{8,12},{12,8},{16,20},{20,16},{24,28},{28,24},{1,5},{5... | collective-permute-start | bytes 589832 | tf_op jit(solution)/shard_map/ppermute | solution.py:19
  13.2 6.2 %collective-permute-start.9 = (bf16[256,128]{1,0:T(8,128)(2,1)S(1)}, bf16[256,128]{1,0:T(8,128)(2,1)S(1)}, u32[]{:S(2)}, u32[]{:S(2)}) collective-permute-start(bf16[256,128]{1,0:T(8,128)(2,1)S(1)} %copy-done.2), channel_id=1, source_target_pairs={{0,2},{1,3},{2,0},{3,1},{4,6},{5,7},{6,4},{7,5},{8,10},{9,11},{10,... | collective-permute-start | bytes 196616 | tf_op jit(solution)/shard_map/ppermute | solution.py:19
  15.3 8.1 %copy-start = (bf16[256,256]{1,0:T(8,128)(2,1)S(1)}, bf16[256,256]{1,0:T(8,128)(2,1)}, u32[]{:S(2)}) copy-start(bf16[256,256]{1,0:T(8,128)(2,1)} %weight.1) | copy-start | bytes 393220
  17.8 4.3 %collective-permute-start.6 = (bf16[64,512]{1,0:T(8,128)(2,1)S(1)}, bf16[64,512]{1,0:T(8,128)(2,1)S(1)}, u32[]{:S(2)}, u32[]{:S(2)}) collective-permute-start(bf16[64,512]{1,0:T(8,128)(2,1)S(1)} %shard_map.97.refs_0_), channel_id=1, source_target_pairs={{0,2},{1,3},{2,0},{3,1},{4,6},{5,7},{6,4},{7,5},{8,10},{9,11},{10,... | collective-permute-start | bytes 196616 | tf_op jit(solution)/shard_map/ppermute | solution.py:19
  19.3 2.8 %collective-permute-start.8 = (bf16[256,128]{1,0:T(8,128)(2,1)S(1)}, bf16[256,128]{1,0:T(8,128)(2,1)S(1)}, u32[]{:S(2)}, u32[]{:S(2)}) collective-permute-start(bf16[256,128]{1,0:T(8,128)(2,1)S(1)} %copy-done.2), channel_id=1, source_target_pairs={{0,1},{1,0},{2,3},{3,2},{4,5},{5,4},{6,7},{7,6},{8,9},{9,8},{10,11... | collective-permute-start | bytes 196616 | tf_op jit(solution)/shard_map/ppermute | solution.py:19
  19.4 2.7 %collective-permute-start.10 = (bf16[256,128]{1,0:T(8,128)(2,1)S(1)}, bf16[256,128]{1,0:T(8,128)(2,1)S(1)}, u32[]{:S(2)}, u32[]{:S(2)}) collective-permute-start(bf16[256,128]{1,0:T(8,128)(2,1)S(1)} %collective-permute-done.9.refs_6_), channel_id=1, source_target_pairs={{0,1},{1,0},{2,3},{3,2},{4,5},{5,4},{6,7},{7,6},{8,9},{9,8},{10,11... | collective-permute-start | bytes 196616 | tf_op jit(solution)/shard_map/ppermute | solution.py:19
  19.9 2.2 %collective-permute-start.5 = (bf16[64,512]{1,0:T(8,128)(2,1)S(1)}, bf16[64,512]{1,0:T(8,128)(2,1)S(1)}, u32[]{:S(2)}, u32[]{:S(2)}) collective-permute-start(bf16[64,512]{1,0:T(8,128)(2,1)S(1)} %shard_map.97.refs_0_), channel_id=1, source_target_pairs={{0,1},{1,0},{2,3},{3,2},{4,5},{5,4},{6,7},{7,6},{8,9},{9,8},{10,11... | collective-permute-start | bytes 196616 | tf_op jit(solution)/shard_map/ppermute | solution.py:19
  22.1 1.3 %collective-permute-start.7 = (bf16[64,512]{1,0:T(8,128)(2,1)S(1)}, bf16[64,512]{1,0:T(8,128)(2,1)S(1)}, u32[]{:S(2)}, u32[]{:S(2)}) collective-permute-start(bf16[64,512]{1,0:T(8,128)(2,1)S(1)} %collective-permute-done.6.refs_2_), channel_id=1, source_target_pairs={{0,1},{1,0},{2,3},{3,2},{4,5},{5,4},{6,7},{7,6},{8,9},{9,8},{10,11... | collective-permute-start | bytes 196616 | tf_op jit(solution)/shard_map/ppermute | solution.py:19
  24.3 7.0 %collective-permute-start.14 = (bf16[192,512]{1,0:T(8,128)(2,1)S(1)}, bf16[192,512]{1,0:T(8,128)(2,1)S(1)}, u32[]{:S(2)}, u32[]{:S(2)}) collective-permute-start(bf16[192,512]{1,0:T(8,128)(2,1)S(1)} %get-tuple-element.49), channel_id=1, source_target_pairs={{0,4},{4,0},{8,12},{12,8},{16,20},{20,16},{24,28},{28,24},{1,5},{5... | collective-permute-start | bytes 589832 | tf_op jit(solution)/shard_map/ppermute | solution.py:19
  26.2 8.7 %collective-permute-start.13 = (bf16[128,256]{1,0:T(8,128)(2,1)S(1)}, bf16[128,256]{1,0:T(8,128)(2,1)S(1)}, u32[]{:S(2)}, u32[]{:S(2)}) collective-permute-start(bf16[128,256]{1,0:T(8,128)(2,1)S(1)} %get-tuple-element.51.refs_0_), channel_id=1, source_target_pairs={{0,16},{4,20},{8,24},{12,28},{16,0},{20,4},{24,8},{28,12},{1,17},{... | collective-permute-start | bytes 196616 | tf_op jit(solution)/shard_map/ppermute | solution.py:19
  28.2 8.9 %collective-permute-start.12 = (bf16[128,256]{1,0:T(8,128)(2,1)S(1)}, bf16[128,256]{1,0:T(8,128)(2,1)S(1)}, u32[]{:S(2)}, u32[]{:S(2)}) collective-permute-start(bf16[128,256]{1,0:T(8,128)(2,1)S(1)} %get-tuple-element.51.refs_0_), channel_id=1, source_target_pairs={{0,24},{4,28},{8,16},{12,20},{16,8},{20,12},{24,0},{28,4},{1,25},{... | collective-permute-start | bytes 196616 | tf_op jit(solution)/shard_map/ppermute | solution.py:19
  30.2 6.9 %collective-permute-start.11 = (bf16[128,256]{1,0:T(8,128)(2,1)S(1)}, bf16[128,256]{1,0:T(8,128)(2,1)S(1)}, u32[]{:S(2)}, u32[]{:S(2)}) collective-permute-start(bf16[128,256]{1,0:T(8,128)(2,1)S(1)} %get-tuple-element.51.refs_0_), channel_id=1, source_target_pairs={{0,8},{4,12},{8,0},{12,4},{16,24},{20,28},{24,16},{28,20},{1,9},{5... | collective-permute-start | bytes 196616 | tf_op jit(solution)/shard_map/ppermute | solution.py:19
  31.3 6.4 %collective-permute-start.19 = (bf16[64,512]{1,0:T(8,128)(2,1)S(1)}, bf16[64,512]{1,0:T(8,128)(2,1)S(1)}, u32[]{:S(2)}, u32[]{:S(2)}) collective-permute-start(bf16[64,512]{1,0:T(8,128)(2,1)S(1)} %get-tuple-element.56), channel_id=1, source_target_pairs={{0,4},{4,0},{8,12},{12,8},{16,20},{20,16},{24,28},{28,24},{1,5},{5... | collective-permute-start | bytes 196616 | tf_op jit(solution)/shard_map/ppermute | solution.py:19
  32.9 7.2 %collective-permute-start.20 = (bf16[64,512]{1,0:T(8,128)(2,1)S(1)}, bf16[64,512]{1,0:T(8,128)(2,1)S(1)}, u32[]{:S(2)}, u32[]{:S(2)}) collective-permute-start(bf16[64,512]{1,0:T(8,128)(2,1)S(1)} %get-tuple-element.57), channel_id=1, source_target_pairs={{0,16},{4,20},{8,24},{12,28},{16,0},{20,4},{24,8},{28,12},{1,17},{... | collective-permute-start | bytes 196616 | tf_op jit(solution)/shard_map/ppermute | solution.py:19
  34.9 6.1 %collective-permute-start.21 = (bf16[64,512]{1,0:T(8,128)(2,1)S(1)}, bf16[64,512]{1,0:T(8,128)(2,1)S(1)}, u32[]{:S(2)}, u32[]{:S(2)}) collective-permute-start(bf16[64,512]{1,0:T(8,128)(2,1)S(1)} %get-tuple-element.58), channel_id=1, source_target_pairs={{0,24},{4,28},{8,16},{12,20},{16,8},{20,12},{24,0},{28,4},{1,25},{... | collective-permute-start | bytes 196616 | tf_op jit(solution)/shard_map/ppermute | solution.py:19
  37.1 4.6 %collective-permute-start.18 = (bf16[64,512]{1,0:T(8,128)(2,1)S(1)}, bf16[64,512]{1,0:T(8,128)(2,1)S(1)}, u32[]{:S(2)}, u32[]{:S(2)}) collective-permute-start(bf16[64,512]{1,0:T(8,128)(2,1)S(1)} %get-tuple-element.50), channel_id=1, source_target_pairs={{0,8},{4,12},{8,0},{12,4},{16,24},{20,28},{24,16},{28,20},{1,9},{5... | collective-permute-start | bytes 196616 | tf_op jit(solution)/shard_map/ppermute | solution.py:19
  37.2 5.0 %collective-permute-start.17 = (bf16[128,256]{1,0:T(8,128)(2,1)S(1)}, bf16[128,256]{1,0:T(8,128)(2,1)S(1)}, u32[]{:S(2)}, u32[]{:S(2)}) collective-permute-start(bf16[128,256]{1,0:T(8,128)(2,1)S(1)} %shard_map.101.part), channel_id=1, source_target_pairs={{0,4},{4,0},{8,12},{12,8},{16,20},{20,16},{24,28},{28,24},{1,5},{5... | collective-permute-start | bytes 196616 | tf_op jit(solution)/shard_map/ppermute | solution.py:19
  37.8 4.4 %collective-permute-start.16 = (bf16[128,256]{1,0:T(8,128)(2,1)S(1)}, bf16[128,256]{1,0:T(8,128)(2,1)S(1)}, u32[]{:S(2)}, u32[]{:S(2)}) collective-permute-start(bf16[128,256]{1,0:T(8,128)(2,1)S(1)} %shard_map.101.part), channel_id=1, source_target_pairs={{0,5},{1,4},{2,7},{3,6},{4,1},{5,0},{6,3},{7,2},{8,13},{9,12},{10,... | collective-permute-start | bytes 196616 | tf_op jit(solution)/shard_map/ppermute | solution.py:293
  40.1 2.1 %collective-permute-start.15 = (bf16[128,256]{1,0:T(8,128)(2,1)S(1)}, bf16[128,256]{1,0:T(8,128)(2,1)S(1)}, u32[]{:S(2)}, u32[]{:S(2)}) collective-permute-start(bf16[128,256]{1,0:T(8,128)(2,1)S(1)} %shard_map.101.part), channel_id=1, source_target_pairs={{0,1},{1,0},{2,3},{3,2},{4,5},{5,4},{6,7},{7,6},{8,9},{9,8},{10,11... | collective-permute-start | bytes 196616 | tf_op jit(solution)/shard_map/ppermute | solution.py:19
